TPU v7x, 32 devices: a whole 2x2x4 slice. The times are simulated.
32 devices in a mesh: row: 4 (over z), col: 8 (over y, x, core).
Axes of the slice: x: 2, y: 2, z: 4, core: 2. Of those that a mesh axis runs over, the one named last changes fastest.
Arguments:
- activations: bfloat16 [256, 256, 384], P('row', 'col'), may hold values from -6 to 6
- cotangent: bfloat16 [256, 256, 384], P('row', 'col'), may hold values from -6 to 6
- first_gain: float32 [384], replicated, may hold values from 0.1 to 1.9
- joint_weight: bfloat16 [384, 1152], replicated, may hold values from -4 to 4, as said below
- output_weight: bfloat16 [384, 384], replicated, may hold values from -0.3125 to 0.3125
- second_gain: float32 [384], replicated, may hold values from 0.1 to 1.9
- expand_weight: bfloat16 [384, 1536], replicated, may hold values from -0.3125 to 0.3125
- reduce_weight: bfloat16 [1536, 384], replicated, may hold values from -0.15625 to 0.15625
Outputs:
- block_out: bfloat16 [256, 256, 384], P('row', 'col')
- grad_input: bfloat16 [256, 256, 384], P('row', 'col')
- grad_joint: float32 [384, 1152], replicated
- grad_project: float32 [384, 384], replicated
- grad_expand: float32 [384, 1536], replicated
- grad_reduce: float32 [1536, 384], replicated
- grad_first_gain: float32 [384], replicated
- grad_second_gain: float32 [384], replicated
Inputs may be any that keep to these rules, and one draw needn't show every extreme that they name: `joint_weight`: Queries, keys and values side by side along the columns, each 384 wide, heads of 32 consecutive columns.
All inputs are finite; a program needn't handle non-finite values.
Results may differ from a plain program's by a relative error of at most 0.014.
The roundings to bfloat16 on the way count: a program that leaves them out, or rounds other values in their place, can miss the bound.
Values may be sent and summed in bfloat16 or wider, within the bound.
No kernel may reach another device: no remote copies, remote signals or barrier semaphores. Data moves between devices by JAX's collectives and lax.ppermute only.
A program may use at most 192 MiB of HBM per device.

v0:
```python
import jax
import jax.numpy as jnp
from jax import lax
from jax.experimental import pallas as pl
from jax.experimental.pallas import tpu as pltpu
from jax.sharding import PartitionSpec as P


HEADS = 12
GRID = 16
SUB = 8
EPSILON = 1e-05
INV_ROOT_TAU = 0.3989422804014327
SQRT_HALF = 0.7071067811865476
LOG2E = 1.4426950408889634
BF = jnp.bfloat16
F32 = jnp.float32

ERFC_P = 0.4
ERFC_C = (
    0.2256758624069583,
    0.22566957331484927,
    0.20784305752189558,
    0.16853970978283367,
    0.1414388899580775,
    -0.005621196233437842,
    0.16909944767289115,
    -0.18290897174728507,
    0.05026375199644912,
)


def nn(a, b):
    return lax.dot_general(a, b, (((1,), (0,)), ((), ())), preferred_element_type=F32)


def nt(a, b):
    return lax.dot_general(a, b, (((1,), (1,)), ((), ())), preferred_element_type=F32)


def tn(a, b):
    return lax.dot_general(a, b, (((0,), (0,)), ((), ())), preferred_element_type=F32)


def gelu_parts(pre):
    gauss = jnp.exp2(pre * pre * (-0.5 * LOG2E))
    t = 1.0 / (1.0 + (ERFC_P * SQRT_HALF) * jnp.abs(pre))
    poly = jnp.full_like(t, 0.5 * ERFC_C[-1])
    for coef in ERFC_C[-2::-1]:
        poly = poly * t + 0.5 * coef
    half_erfc = gauss * (t * poly)
    phi = jnp.where(pre < 0.0, half_erfc, 1.0 - half_erfc)
    return phi, gauss


def normalize(values):
    center = values - jnp.mean(values, axis=0, keepdims=True)
    inv_std = lax.rsqrt(jnp.mean(center * center, axis=0, keepdims=True) + EPSILON)
    return center * inv_std, inv_std


def norm_back(scaled, normed, inv_std):
    return inv_std * (
        scaled
        - jnp.mean(scaled, axis=0, keepdims=True)
        - normed * jnp.mean(scaled * normed, axis=0, keepdims=True)
    )


def load_rows(ref):
    pieces, _, sub, width = ref.shape
    return ref[...].reshape(pieces, sub, width).astype(F32).reshape(pieces * sub, width)


def store_rows(ref, rows):
    pieces, _, sub, width = ref.shape
    ref[...] = rows.reshape(pieces, 1, sub, width).astype(ref.dtype)


def fold_lanes(values):
    total = values[:, :128]
    for start in range(128, values.shape[1], 128):
        total = total + values[:, start : start + 128]
    return total


def begin(carried, acc_ref, grad_gain_ref):
    if carried:
        acc_ref[...] = carried[0][...]
        grad_gain_ref[...] = carried[1][...]
    else:
        acc_ref[...] = jnp.zeros_like(acc_ref)
        grad_gain_ref[...] = jnp.zeros_like(grad_gain_ref)


def finish(acc_ref, grads_ref, grad_gain_ref):
    rows = acc_ref.shape[0]
    grads_ref[:rows] = acc_ref[...].astype(grads_ref.dtype)
    if grads_ref.shape[0] > rows:
        gains = jnp.sum(grad_gain_ref[...].T, axis=0, keepdims=True)
        spare = grads_ref.shape[0] - rows
        first = lax.broadcasted_iota(jnp.int32, (spare, gains.shape[1]), 0) == 0
        grads_ref[rows:] = jnp.where(first, gains, 0.0).astype(grads_ref.dtype)


def attend_kernel(act_ref, gain_ref, joint_ref, flat_ref, triple_ref, mixed_ref):
    width = gain_ref.shape[0]
    head = width // HEADS
    factor = head ** (-0.5) * LOG2E
    flat = load_rows(act_ref).T
    flat_ref[0] = flat.astype(BF)
    normed, _ = normalize(flat)
    scaled = (normed * gain_ref[...]).astype(BF)
    triple_ref[0] = nn(joint_ref[...], scaled).astype(BF)
    for h in range(HEADS):
        rows = slice(h * head, (h + 1) * head)
        queries = triple_ref[0, h * head : (h + 1) * head]
        keys = triple_ref[0, width + h * head : width + (h + 1) * head]
        values = triple_ref[0, 2 * width + h * head : 2 * width + (h + 1) * head]
        scores = tn(keys, queries)
        weights = jnp.exp2((scores - jnp.max(scores, axis=0, keepdims=True)) * factor)
        weights = weights * (1.0 / jnp.sum(weights, axis=0, keepdims=True))
        mixed_ref[0, rows] = nn(values, weights.astype(BF)).astype(BF)


def mlp_kernel(
    flat_ref, mixed_ref, cot_ref, gain_ref, out_t_ref, up_t_ref, down_t_ref, down_ref, up_ref, out_w_ref,
    *rest,
):
    carried = rest[:-6]
    result_ref, grad_att_ref, grad_mixed_ref, grads_ref, grad_gain_ref, acc_ref = rest[-6:]
    step = pl.program_id(0)
    width = gain_ref.shape[0]
    hidden_dim = up_ref.shape[1]

    @pl.when(step == 0)
    def _():
        begin(carried, acc_ref, grad_gain_ref)

    cot_rows = load_rows(cot_ref)
    cot_b = cot_rows.astype(BF)
    cot_t = cot_rows.T
    cot_tb = cot_t.astype(BF)
    mixed = mixed_ref[0]
    attended = flat_ref[0].astype(F32) + nn(out_t_ref[...], mixed)
    normed, inv_std = normalize(attended)
    gain = gain_ref[...]
    scaled = (normed * gain).astype(BF)
    result = attended
    grad_scaled = jnp.zeros_like(attended)
    piece = width
    for start in range(0, hidden_dim, piece):
        part = slice(start, start + piece)
        pre = nn(up_t_ref[part], scaled)
        phi, gauss = gelu_parts(pre)
        hidden = (pre * phi).astype(BF)
        result = result + nn(down_t_ref[:, part], hidden)
        acc_ref[part] += nn(hidden, cot_b)
        grad_hidden = nn(down_ref[part], cot_tb).astype(BF).astype(F32)
        grad_pre = (grad_hidden * (phi + pre * gauss * INV_ROOT_TAU)).astype(BF)
        grad_scaled = grad_scaled + nn(up_ref[:, part], grad_pre)
        acc_ref[hidden_dim + start : hidden_dim + start + piece] += nt(grad_pre, scaled)
    store_rows(result_ref, result.T)
    grad_gain_ref[...] += fold_lanes(grad_scaled * normed)
    grad_att = cot_t + norm_back(grad_scaled * gain, normed, inv_std)
    grad_att_ref[0] = grad_att
    grad_att_b = grad_att.astype(BF)
    acc_ref[2 * hidden_dim :] += nt(mixed, grad_att_b)
    grad_mixed_ref[0] = nn(out_w_ref[...], grad_att_b).astype(BF)

    @pl.when(step == pl.num_programs(0) - 1)
    def _():
        finish(acc_ref, grads_ref, grad_gain_ref)


def back_kernel(
    flat_ref, triple_ref, grad_mixed_ref, grad_att_ref, gain_ref, joint_ref,
    *rest,
):
    carried = rest[:-5]
    grad_in_ref, grads_ref, grad_gain_ref, acc_ref, grad_triple_ref = rest[-5:]
    step = pl.program_id(0)
    width = gain_ref.shape[0]
    head = width // HEADS
    scale = head ** (-0.5)

    @pl.when(step == 0)
    def _():
        begin(carried, acc_ref, grad_gain_ref)

    for h in range(HEADS):
        queries = triple_ref[0, h * head : (h + 1) * head]
        keys = triple_ref[0, width + h * head : width + (h + 1) * head]
        values = triple_ref[0, 2 * width + h * head : 2 * width + (h + 1) * head]
        grad_heads = grad_mixed_ref[0, h * head : (h + 1) * head]
        scores = tn(keys, queries)
        weights = jnp.exp2((scores - jnp.max(scores, axis=0, keepdims=True)) * (scale * LOG2E))
        weights = weights * (1.0 / jnp.sum(weights, axis=0, keepdims=True))
        grad_weights = tn(values, grad_heads)
        inner = jnp.sum(weights * grad_weights, axis=0, keepdims=True)
        grad_scores = (weights * (grad_weights - inner) * scale).astype(BF)
        grad_triple_ref[h * head : (h + 1) * head] = nn(keys, grad_scores).astype(BF)
        grad_triple_ref[width + h * head : width + (h + 1) * head] = nt(queries, grad_scores).astype(BF)
        grad_triple_ref[2 * width + h * head : 2 * width + (h + 1) * head] = nt(
            grad_heads, weights.astype(BF)
        ).astype(BF)
    normed, inv_std = normalize(flat_ref[0].astype(F32))
    gain = gain_ref[...]
    scaled = (normed * gain).astype(BF)
    acc_ref[...] += nt(grad_triple_ref[...], scaled)
    grad_scaled = nn(joint_ref[...], grad_triple_ref[...])
    grad_gain_ref[...] += fold_lanes(grad_scaled * normed)
    grad_in = grad_att_ref[0] + norm_back(grad_scaled * gain, normed, inv_std)
    store_rows(grad_in_ref, grad_in.T)

    @pl.when(step == pl.num_programs(0) - 1)
    def _():
        finish(acc_ref, grads_ref, grad_gain_ref)


def pack_kernel(tile_ref, sends_ref, rows_ref):
    lines, _, chunk_rows, columns, width = tile_ref.shape
    cols, groups, share, _ = sends_ref.shape
    for line in range(lines):
        for row in range(chunk_rows):
            for block in range(columns // cols):
                near, part = block // (columns // cols // (share // lines)), block % (groups // chunk_rows)
                start = (row * (groups // chunk_rows) + part) * share + line * (share // lines) + near
                values = tile_ref[line, 0, row, block * cols : (block + 1) * cols].astype(F32)
                for lane in range(width // 128):
                    rows_ref[lane, pl.ds(start, cols, stride=groups * share)] = values[
                        :, lane * 128 : (lane + 1) * 128
                    ]
    for lane in range(width // 128):
        sends_ref[:, :, :, lane * 128 : (lane + 1) * 128] = (
            rows_ref[lane].reshape(cols, groups, share, 128).astype(BF)
        )


def unpack_kernel(*refs):
    *arrived, tile_ref, rows_ref = refs
    lines, _, all_rows, columns, width = tile_ref.shape
    cols, groups, share, _ = arrived[0].shape
    chunk_rows = all_rows // len(arrived)
    parts = groups // chunk_rows
    for chunk, part_ref in enumerate(arrived):
        for lane in range(width // 128):
            piece = part_ref[:, :, :, lane * 128 : (lane + 1) * 128].astype(F32)
            rows_ref[lane] = piece.reshape(cols * groups * share, 128)
        for line in range(lines):
            for row in range(chunk_rows):
                for block in range(columns // cols):
                    near, part = block // parts, block % parts
                    start = (row * parts + part) * share + line * (share // lines) + near
                    values = jnp.concatenate(
                        [
                            rows_ref[lane, pl.ds(start, cols, stride=groups * share)]
                            for lane in range(width // 128)
                        ],
                        axis=1,
                    )
                    tile_ref[line, 0, chunk * chunk_rows + row, block * cols : (block + 1) * cols] = (
                        values.astype(BF)
                    )


def pack_call(tile, chunk, chunk_rows, row_devs, cols, parts):
    lines, _, _, columns, width = tile.shape
    groups, share = chunk_rows * parts, lines * columns // (cols * parts)
    return pl.pallas_call(
        pack_kernel,
        grid=(row_devs,),
        in_specs=[
            pl.BlockSpec((lines, 1, chunk_rows, columns, width), lambda r: (0, r, chunk, 0, 0))
        ],
        out_specs=pl.BlockSpec((cols, groups, share, width), lambda r: (r, 0, 0, 0)),
        out_shape=jax.ShapeDtypeStruct((row_devs * cols, groups, share, width), BF),
        scratch_shapes=[pltpu.VMEM((width // 128, cols * groups * share, 128), F32)],
        compiler_params=params(),
        cost_estimate=cost(1e6, 4 * row_devs * cols * groups * share * width, 0),
    )(tile)


def unpack_call(arrived, lines, all_rows, columns, row_devs):
    devices, groups, share, width = arrived[0].shape
    cols = devices // row_devs
    piece = pl.BlockSpec((cols, groups, share, width), lambda r: (r, 0, 0, 0))
    return pl.pallas_call(
        unpack_kernel,
        grid=(row_devs,),
        in_specs=[piece] * len(arrived),
        out_specs=pl.BlockSpec((lines, 1, all_rows, columns, width), lambda r: (0, r, 0, 0, 0)),
        out_shape=jax.ShapeDtypeStruct((lines, row_devs, all_rows, columns, width), BF),
        scratch_shapes=[pltpu.VMEM((width // 128, cols * groups * share, 128), F32)],
        compiler_params=params(),
        cost_estimate=cost(1e6, 4 * lines * row_devs * all_rows * columns * width, 0),
    )(*arrived)


def whole(array):
    return pl.BlockSpec(array.shape, lambda g: (0,) * array.ndim)


def per_group(shape):
    return pl.BlockSpec((1,) + shape, lambda g: (g, 0, 0))


def pieces_spec(array):
    pieces, _, sub, width = array.shape
    return pl.BlockSpec((pieces, 1, sub, width), lambda g: (0, g, 0, 0))


def params():
    return pltpu.CompilerParams(dimension_semantics=("arbitrary",), vmem_limit_bytes=60 << 20)


def cost(flops, bytes_moved, exps):
    return pl.CostEstimate(flops=int(flops), bytes_accessed=int(bytes_moved), transcendentals=int(exps))


def attend_call(act, gain, joint_t):
    pieces, groups, sub, width = act.shape
    tokens = pieces * sub
    return pl.pallas_call(
        attend_kernel,
        grid=(groups,),
        in_specs=[pieces_spec(act), whole(gain), whole(joint_t)],
        out_specs=[per_group((width, tokens)), per_group((3 * width, tokens)), per_group((width, tokens))],
        out_shape=[
            jax.ShapeDtypeStruct((groups, width, tokens), BF),
            jax.ShapeDtypeStruct((groups, 3 * width, tokens), BF),
            jax.ShapeDtypeStruct((groups, width, tokens), BF),
        ],
        compiler_params=params(),
        cost_estimate=cost(3e9 * groups, 12 * groups * tokens * width, 0),
    )(act, gain, joint_t)


def mlp_call(flat, mixed, cot, gain, weights, carried, spare):
    pieces, groups, sub, width = cot.shape
    tokens = pieces * sub
    hidden_dim = weights[1].shape[0]
    rows = 2 * hidden_dim + width
    return pl.pallas_call(
        mlp_kernel,
        grid=(groups,),
        in_specs=[per_group((width, tokens)), per_group((width, tokens)), pieces_spec(cot), whole(gain)]
        + [whole(w) for w in weights + carried],
        out_specs=[
            pieces_spec(cot),
            per_group((width, tokens)),
            per_group((width, tokens)),
            pl.BlockSpec((rows + spare, width), lambda g: (0, 0)),
            pl.BlockSpec((width, 128), lambda g: (0, 0)),
        ],
        out_shape=[
            jax.ShapeDtypeStruct(cot.shape, BF),
            jax.ShapeDtypeStruct((groups, width, tokens), F32),
            jax.ShapeDtypeStruct((groups, width, tokens), BF),
            jax.ShapeDtypeStruct((rows + spare, width), BF if spare else F32),
            jax.ShapeDtypeStruct((width, 128), F32),
        ],
        scratch_shapes=[pltpu.VMEM((rows, width), F32)],
        compiler_params=params(),
        cost_estimate=cost(4e9 * groups, 14 * groups * tokens * width, 0),
    )(flat, mixed, cot, gain, *weights, *carried)


def back_call(flat, triple, grad_mixed, grad_att, gain, joint, like, carried, spare):
    rows = joint.shape[1]
    pieces, groups, sub, width = like.shape
    tokens = pieces * sub
    return pl.pallas_call(
        back_kernel,
        grid=(groups,),
        in_specs=[
            per_group((width, tokens)),
            per_group((3 * width, tokens)),
            per_group((width, tokens)),
            per_group((width, tokens)),
            whole(gain),
            whole(joint),
        ]
        + [whole(w) for w in carried],
        out_specs=[
            pieces_spec(like),
            pl.BlockSpec((rows + spare, width), lambda g: (0, 0)),
            pl.BlockSpec((width, 128), lambda g: (0, 0)),
        ],
        out_shape=[
            jax.ShapeDtypeStruct(like.shape, BF),
            jax.ShapeDtypeStruct((rows + spare, width), BF if spare else F32),
            jax.ShapeDtypeStruct((width, 128), F32),
        ],
        scratch_shapes=[pltpu.VMEM((3 * width, width), F32), pltpu.VMEM((3 * width, tokens), BF)],
        compiler_params=params(),
        cost_estimate=cost(6e9 * groups, 18 * groups * tokens * width, 0),
    )(flat, triple, grad_mixed, grad_att, gain, joint, *carried)


def tie(value, *after):
    return lax.optimization_barrier((value,) + after)[0]


def peers(axis, low, high):
    return lax.axis_index(axis) // (1 << low) % (1 << (high - low)), 1 << (high - low)


def swap(values, axis, offset):
    return lax.ppermute(values, axis, [(i, i ^ offset) for i in range(lax.axis_size(axis))])


def scatter_sum(values, axis, low, high):
    mine, count = peers(axis, low, high)
    parts = values.reshape((count, values.shape[0] // count) + values.shape[1:])
    total = lax.dynamic_index_in_dim(parts, mine, 0, keepdims=False).astype(F32)
    for other in range(1, count):
        part = lax.dynamic_index_in_dim(parts, mine ^ other, 0, keepdims=False)
        total = total + swap(part, axis, other << low).astype(F32)
    return total.astype(BF)


def collect(values, axis, low, high):
    mine, count = peers(axis, low, high)
    got = jnp.stack([values] + [swap(values, axis, other << low) for other in range(1, count)])
    return jnp.concatenate(
        [lax.dynamic_index_in_dim(got, slot ^ mine, 0, keepdims=False) for slot in range(count)]
    )


def stages():
    row_bits = lax.axis_size("row").bit_length() - 1
    col_bits = lax.axis_size("col").bit_length() - 1
    return (("col", 0, 1), ("col", 1, col_bits), ("row", 0, row_bits))


def shards(
    activations,
    cotangent,
    first_gain,
    joint_weight,
    output_weight,
    second_gain,
    expand_weight,
    reduce_weight,
):
    row_devs = lax.axis_size("row")
    col_devs = lax.axis_size("col")
    devices = row_devs * col_devs
    both = ("row", "col")
    tile_rows, tile_cols, channels = activations.shape
    local_rows = GRID // row_devs
    local_cols = GRID // col_devs
    stride_rows = tile_rows // local_rows
    stride_cols = tile_cols // local_cols
    part_rows = stride_rows // row_devs
    part_cols = stride_cols // col_devs
    share = local_rows * local_cols
    tokens = GRID * GRID
    factor = float(tile_rows * tile_cols * devices) ** (-0.5)

    chunks = 2
    chunk_rows = part_rows // chunks
    chunk_groups = chunk_rows * part_cols

    kernels_pack = share % SUB == 0 and col_devs == SUB

    def pack(tile, chunk):
        if kernels_pack:
            tile = tile.reshape(local_rows, row_devs, part_rows, tile_cols, channels)
            return pack_call(tile, chunk, chunk_rows, row_devs, col_devs, part_cols)
        sends = tile.reshape(
            local_rows, row_devs, part_rows, local_cols, part_cols, col_devs, channels
        )[:, :, chunk * chunk_rows : (chunk + 1) * chunk_rows]
        return sends.transpose(1, 5, 2, 4, 0, 3, 6).reshape(devices, chunk_groups, share, channels)

    def send(sends, *after):
        got = lax.all_to_all(tie(sends, *after), both, split_axis=0, concat_axis=0, tiled=True)
        if share % SUB:
            got = got.transpose(0, 2, 1, 3).reshape(tokens // SUB, SUB, chunk_groups, channels)
            got = got.transpose(0, 2, 1, 3)
        return got.reshape(tokens // SUB, chunk_groups, SUB, channels)

    def give_back(pieces, *after):
        if share % SUB:
            pieces = pieces.transpose(0, 2, 1, 3).reshape(devices, share, chunk_groups, channels)
            pieces = pieces.transpose(0, 2, 1, 3)
        pieces = tie(pieces.reshape(devices, chunk_groups, share, channels), *after)
        return lax.all_to_all(pieces, both, split_axis=0, concat_axis=0, tiled=True)

    def to_tile(arrived):
        if kernels_pack:
            tile = unpack_call(arrived, local_rows, part_rows, tile_cols, row_devs)
            return tile.reshape(tile_rows, tile_cols, channels)
        arrived = [
            part.reshape(row_devs, col_devs, chunk_rows, part_cols, local_rows, local_cols, channels)
            for part in arrived
        ]
        return jnp.concatenate(arrived, axis=2).transpose(4, 0, 2, 5, 3, 1, 6).reshape(
            tile_rows, tile_cols, channels
        )

    def spread(gain):
        return jnp.broadcast_to(gain[:, None], (channels, tokens))

    arrived = []
    for k, tile in enumerate([activations] * chunks + [cotangent] * chunks):
        sends = pack(tile, k % chunks)
        arrived.append(send(sends, *arrived[-1:]))
    act, cot = arrived[:chunks], arrived[chunks:]
    gain_one, gain_two = spread(first_gain), spread(second_gain)
    joint_t = joint_weight.T
    weights = (
        output_weight.T, expand_weight.T, reduce_weight.T, reduce_weight, expand_weight, output_weight
    )
    hidden_dim = expand_weight.shape[1]
    tail_rows, head_rows = 2 * hidden_dim + channels, 3 * channels
    unit = SUB * devices
    fronts = []
    for k in range(chunks):
        fronts.append(attend_call(act[k], gain_one, joint_t))
    tails, out_parts, carried = [], [], ()
    before = cot[-1:]
    for k in range(chunks):
        flat, _, mixed = fronts[k]
        spare = unit - tail_rows % unit if k == chunks - 1 else 0
        tails.append(mlp_call(flat, mixed, cot[k], gain_two, weights, carried, spare))
        carried = tails[-1][3:]
        out_parts.append(give_back(tails[-1][0], *before))
        before = out_parts[-1:]
    steps = stages()
    tail_sum = carried[0]
    heads, in_parts, carried = [], [], ()
    for k in range(chunks):
        flat, triple, _ = fronts[k]
        _, grad_att, grad_mixed = tails[k][:3]
        spare = unit - head_rows % unit if k == chunks - 1 else 0
        grad_mixed = tie(grad_mixed, out_parts[k], *((tail_sum,) if k else ()))
        heads.append(
            back_call(flat, triple, grad_mixed, grad_att, gain_one, joint_weight, cot[k], carried, spare)
        )
        carried = heads[-1][1:]
        in_parts.append(give_back(heads[-1][0], *before))
        before = in_parts[-1:]
        if k < len(steps):
            tail_sum = scatter_sum(tail_sum, *steps[k])
    head_sum = tie(carried[0], tail_sum)
    for stage in steps[:-1]:
        head_sum = scatter_sum(head_sum, *stage)
    rows_left = lax.axis_size("row")
    split = head_sum.shape[0] // rows_left
    both_sums = jnp.concatenate(
        [part.reshape(rows_left, -1, channels) for part in (head_sum, tail_sum)], axis=1
    )
    width_all = both_sums.shape[1]
    both_sums = scatter_sum(both_sums.reshape(-1, channels), *steps[-1])
    for stage in steps[::-1]:
        both_sums = collect(both_sums, *stage)
    both_sums = both_sums.reshape(devices, width_all, channels)
    head_sum = both_sums[:, :split].reshape(-1, channels).astype(F32) * factor
    tail_sum = both_sums[:, split:].reshape(-1, channels).astype(F32) * factor
    block_out = to_tile(out_parts)
    grad_input = to_tile(in_parts)
    return (
        block_out,
        grad_input,
        head_sum[:head_rows].T,
        tail_sum[2 * hidden_dim : tail_rows],
        tail_sum[hidden_dim : 2 * hidden_dim].T,
        tail_sum[:hidden_dim],
        head_sum[head_rows],
        tail_sum[tail_rows],
    )


def solution(mesh):
    placed = (P("row", "col", None), P("row", "col", None), P(), P(), P(), P(), P(), P())
    return jax.shard_map(shards, mesh=mesh, in_specs=placed, out_specs=placed, check_vma=False)
```

profile of v0, /device:TPU:0, one launch (start us, length us, event | category | flops | bytes accessed | tf_op | source)
XLA Modules:
  0.0 379.5 jit_solution(10349466804740683908)
XLA Ops:
  0.6 4.0 %shard_map.143 = bf16[32,4,8,384]{3,2,1,0:T(8,128)(2,1)} custom-call(bf16[4,4,4,32,384]{4,3,2,1,0:T(8,128)(2,1)} %bitcast.99), custom_call_target="tpu_custom_call" | custom-call | flops 1000000 | bytes 1572864 | tf_op jit(solution)/shard_map/pallas_call | solution.py:270
  4.6 7.3 %all-to-all-start = ((bf16[32,4,8,384]{3,2,1,0:T(8,128)(2,1)}), bf16[32,4,8,384]{3,2,1,0:T(8,128)(2,1)S(1)}, u32[]{:S(2)}, u32[]{:S(2)}) async-start(bf16[32,4,8,384]{3,2,1,0:T(8,128)(2,1)} %shard_map.143), calls=%async_computation | async-start | bytes 1572864 | tf_op jit(solution)/shard_map/all_to_all | solution.py:478
  12.0 4.0 %shard_map.146 = bf16[32,4,8,384]{3,2,1,0:T(8,128)(2,1)} custom-call(bf16[4,4,4,32,384]{4,3,2,1,0:T(8,128)(2,1)} %bitcast.100), custom_call_target="tpu_custom_call" | custom-call | flops 1000000 | bytes 1572864 | tf_op jit(solution)/shard_map/pallas_call | solution.py:270
  16.0 16.6 %all-to-all-done.act_ref = bf16[32,4,8,384]{3,2,1,0:T(8,128)(2,1)S(1)} async-done(((bf16[32,4,8,384]{3,2,1,0:T(8,128)(2,1)}), bf16[32,4,8,384]{3,2,1,0:T(8,128)(2,1)S(1)}, u32[]{:S(2)}, u32[]{:S(2)}) %all-to-all-start) | async-done | bytes 786464 | tf_op jit(solution)/shard_map/all_to_all | solution.py:478
  36.2 4.1 %shard_map.145 = bf16[32,4,8,384]{3,2,1,0:T(8,128)(2,1)} custom-call(bf16[4,4,4,32,384]{4,3,2,1,0:T(8,128)(2,1)} %bitcast.101), custom_call_target="tpu_custom_call" | custom-call | flops 1000000 | bytes 1572864 | tf_op jit(solution)/shard_map/pallas_call | solution.py:270
  40.3 16.5 %all-to-all-done.1.act_ref = bf16[32,4,8,384]{3,2,1,0:T(8,128)(2,1)S(1)} async-done(((bf16[32,4,8,384]{3,2,1,0:T(8,128)(2,1)}), bf16[32,4,8,384]{3,2,1,0:T(8,128)(2,1)S(1)}, u32[]{:S(2)}, u32[]{:S(2)}) %all-to-all-start.1) | async-done | bytes 786464 | tf_op jit(solution)/shard_map/all_to_all | solution.py:478
  65.6 4.0 %shard_map.148 = bf16[32,4,8,384]{3,2,1,0:T(8,128)(2,1)} custom-call(bf16[4,4,4,32,384]{4,3,2,1,0:T(8,128)(2,1)} %bitcast.102), custom_call_target="tpu_custom_call" | custom-call | flops 1000000 | bytes 1572864 | tf_op jit(solution)/shard_map/pallas_call | solution.py:270
  70.5 20.4 %shard_map.144 = (bf16[4,384,256]{2,1,0:T(8,128)(2,1)}, bf16[4,1152,256]{2,1,0:T(8,128)(2,1)}, bf16[4,384,256]{2,1,0:T(8,128)(2,1)}) custom-call(bf16[32,4,8,384]{3,2,1,0:T(8,128)(2,1)} %copy-done.8, f32[384,256]{1,0:T(8,128)} %broadcast_in_dim.4.gain_ref, bf16[1152,384]{1,0:T(8,128)(2,1)} %bitcast.121), custom_call_target="tpu_custom_call" | custom-call | flops 12000000000 | bytes 4718592 | tf_op jit(solution)/shard_map/pallas_call | solution.py:324
  90.9 6.1 %all-to-all-start.3 = ((bf16[32,4,8,384]{3,2,1,0:T(8,128)(2,1)}), bf16[32,4,8,384]{3,2,1,0:T(8,128)(2,1)S(1)}, u32[]{:S(2)}, u32[]{:S(2)}) async-start(bf16[32,4,8,384]{3,2,1,0:T(8,128)(2,1)} %shard_map.148), calls=%async_computation.3 | async-start | bytes 1572864 | tf_op jit(solution)/shard_map/all_to_all | solution.py:478
  97.0 20.4 %shard_map.149 = (bf16[4,384,256]{2,1,0:T(8,128)(2,1)}, bf16[4,1152,256]{2,1,0:T(8,128)(2,1)}, bf16[4,384,256]{2,1,0:T(8,128)(2,1)}) custom-call(bf16[32,4,8,384]{3,2,1,0:T(8,128)(2,1)} %copy-done.7, f32[384,256]{1,0:T(8,128)} %broadcast_in_dim.4.gain_ref, bf16[1152,384]{1,0:T(8,128)(2,1)} %bitcast.122), custom_call_target="tpu_custom_call" | custom-call | flops 12000000000 | bytes 4718592 | tf_op jit(solution)/shard_map/pallas_call | solution.py:324
  118.3 28.6 %shard_map.147 = (bf16[32,4,8,384]{3,2,1,0:T(8,128)(2,1)}, f32[4,384,256]{2,1,0:T(8,128)}, bf16[4,384,256]{2,1,0:T(8,128)(2,1)}, f32[3456,384]{1,0:T(8,128)}, f32[384,128]{1,0:T(8,128)}) custom-call(bf16[4,384,256]{2,1,0:T(8,128)(2,1)} %get-tuple-element.38.flat_ref, bf16[4,384,256]{2,1,0:T(8,128)(2,1)} %get-tuple-element.39.mixed_ref, ...), custom_call_target="tpu_custom_call" | custom-call | flops 16000000000 | bytes 5505024 | tf_op jit(solution)/shard_map/pallas_call | solution.py:344
  147.8 30.0 %shard_map.150 = (bf16[32,4,8,384]{3,2,1,0:T(8,128)(2,1)}, f32[4,384,256]{2,1,0:T(8,128)}, bf16[4,384,256]{2,1,0:T(8,128)(2,1)}, bf16[3584,384]{1,0:T(8,128)(2,1)}, f32[384,128]{1,0:T(8,128)}) custom-call(bf16[4,384,256]{2,1,0:T(8,128)(2,1)} %get-tuple-element.45.flat_ref, bf16[4,384,256]{2,1,0:T(8,128)(2,1)} %get-tuple-element.46.mixed_ref, ...), custom_call_target="tpu_custom_call" | custom-call | flops 16000000000 | bytes 5505024 | tf_op jit(solution)/shard_map/pallas_call | solution.py:344
  179.7 5.7 %all-to-all-start.4 = ((bf16[32,4,8,384]{3,2,1,0:T(8,128)(2,1)}), bf16[32,4,8,384]{3,2,1,0:T(8,128)(2,1)S(1)}, u32[]{:S(2)}, u32[]{:S(2)}) async-start(bf16[32,4,8,384]{3,2,1,0:T(8,128)(2,1)} %get-tuple-element.44), calls=%async_computation.4 | async-start | bytes 1572864 | tf_op jit(solution)/shard_map/all_to_all | solution.py:489
  191.7 14.3 %all-to-all-done.4.refs_0_ = bf16[32,4,8,384]{3,2,1,0:T(8,128)(2,1)S(1)} async-done(((bf16[32,4,8,384]{3,2,1,0:T(8,128)(2,1)}), bf16[32,4,8,384]{3,2,1,0:T(8,128)(2,1)S(1)}, u32[]{:S(2)}, u32[]{:S(2)}) %all-to-all-start.4) | async-done | bytes 786464 | tf_op jit(solution)/shard_map/all_to_all | solution.py:489
  206.0 3.8 all-to-all-start.5
  209.8 26.4 %shard_map.152 = (bf16[32,4,8,384]{3,2,1,0:T(8,128)(2,1)}, f32[1152,384]{1,0:T(8,128)}, f32[384,128]{1,0:T(8,128)}) custom-call(bf16[4,384,256]{2,1,0:T(8,128)(2,1)} %get-tuple-element.38.flat_ref, bf16[4,1152,256]{2,1,0:T(8,128)(2,1)} %get-tuple-element.51.triple_ref, bf16[4,384,256]{2,1,0:T(8,128)(2,1)} %get-tuple-element.53.grad_mixed_ref, ...), custom_call_target="tpu_custom_call" | custom-call | flops 24000000000 | bytes 7077888 | tf_op jit(solution)/shard_map/pallas_call | solution.py:373
  237.5 27.0 %shard_map.153 = (bf16[32,4,8,384]{3,2,1,0:T(8,128)(2,1)}, bf16[1280,384]{1,0:T(8,128)(2,1)}, f32[384,128]{1,0:T(8,128)}) custom-call(bf16[4,384,256]{2,1,0:T(8,128)(2,1)} %get-tuple-element.45.flat_ref, bf16[4,1152,256]{2,1,0:T(8,128)(2,1)} %get-tuple-element.57.triple_ref, bf16[4,384,256]{2,1,0:T(8,128)(2,1)} %get-tuple-element.60.grad_mixed_ref, ...), custom_call_target="tpu_custom_call" | custom-call | flops 24000000000 | bytes 7077888 | tf_op jit(solution)/shard_map/pallas_call | solution.py:373
  286.0 6.6 %collective-permute-done.9 = bf16[152,384]{1,0:T(8,128)(2,1)S(1)} collective-permute-done((bf16[152,384]{1,0:T(8,128)(2,1)S(1)}, bf16[152,384]{1,0:T(8,128)(2,1)S(1)}, u32[]{:S(2)}, u32[]{:S(2)}) %collective-permute-start.9) | collective-permute-done | bytes 116768 | tf_op jit(solution)/shard_map/ppermute | solution.py:410
  311.7 7.8 %collective-permute-done.15 = bf16[608,384]{1,0:T(8,128)(2,1)S(1)} collective-permute-done((bf16[608,384]{1,0:T(8,128)(2,1)S(1)}, bf16[608,384]{1,0:T(8,128)(2,1)S(1)}, u32[]{:S(2)}, u32[]{:S(2)}) %collective-permute-start.15) | collective-permute-done | bytes 466976 | tf_op jit(solution)/shard_map/ppermute | solution.py:410
  322.0 12.0 %collective-permute-done.16 = bf16[608,384]{1,0:T(8,128)(2,1)S(1)} collective-permute-done((bf16[608,384]{1,0:T(8,128)(2,1)S(1)}, bf16[608,384]{1,0:T(8,128)(2,1)S(1)}, u32[]{:S(2)}, u32[]{:S(2)}) %collective-permute-start.16) | collective-permute-done | bytes 466976 | tf_op jit(solution)/shard_map/ppermute | solution.py:410
  336.1 4.0 %all-to-all-start.7 = ((bf16[32,4,8,384]{3,2,1,0:T(8,128)(2,1)}), bf16[32,4,8,384]{3,2,1,0:T(8,128)(2,1)S(1)}, u32[]{:S(2)}, u32[]{:S(2)}) async-start(bf16[32,4,8,384]{3,2,1,0:T(8,128)(2,1)} %get-tuple-element.65), calls=%async_computation.7 | async-start | bytes 1572864 | tf_op jit(solution)/shard_map/all_to_all | solution.py:489
  340.2 4.6 %shard_map.151 = bf16[4,4,4,32,384]{4,3,2,1,0:T(8,128)(2,1)} custom-call(bf16[32,4,8,384]{3,2,1,0:T(8,128)(2,1)} %copy-done, bf16[32,4,8,384]{3,2,1,0:T(8,128)(2,1)} %copy-done.1), custom_call_target="tpu_custom_call" | custom-call | flops 1000000 | bytes 3145728 | tf_op jit(solution)/shard_map/pallas_call | solution.py:288
  344.7 16.0 %all-to-all-done.7.refs_1_ = bf16[32,4,8,384]{3,2,1,0:T(8,128)(2,1)S(1)} async-done(((bf16[32,4,8,384]{3,2,1,0:T(8,128)(2,1)}), bf16[32,4,8,384]{3,2,1,0:T(8,128)(2,1)S(1)}, u32[]{:S(2)}, u32[]{:S(2)}) %all-to-all-start.7) | async-done | bytes 786464 | tf_op jit(solution)/shard_map/all_to_all | solution.py:489
  361.6 4.6 %shard_map.154 = bf16[4,4,4,32,384]{4,3,2,1,0:T(8,128)(2,1)} custom-call(bf16[32,4,8,384]{3,2,1,0:T(8,128)(2,1)} %copy-done.2, bf16[32,4,8,384]{3,2,1,0:T(8,128)(2,1)} %copy-done.3), custom_call_target="tpu_custom_call" | custom-call | flops 1000000 | bytes 3145728 | tf_op jit(solution)/shard_map/pallas_call | solution.py:288
  (98 shorter events, 83.5 us)
Async XLA Ops:
  4.6 27.9 %all-to-all-start = ((bf16[32,4,8,384]{3,2,1,0:T(8,128)(2,1)}), bf16[32,4,8,384]{3,2,1,0:T(8,128)(2,1)S(1)}, u32[]{:S(2)}, u32[]{:S(2)}) async-start(bf16[32,4,8,384]{3,2,1,0:T(8,128)(2,1)} %shard_map.143), calls=%async_computation | async-start | bytes 1572864 | tf_op jit(solution)/shard_map/all_to_all | solution.py:478
  32.6 24.2 %all-to-all-start.1 = ((bf16[32,4,8,384]{3,2,1,0:T(8,128)(2,1)}), bf16[32,4,8,384]{3,2,1,0:T(8,128)(2,1)S(1)}, u32[]{:S(2)}, u32[]{:S(2)}) async-start(bf16[32,4,8,384]{3,2,1,0:T(8,128)(2,1)} %shard_map.146), calls=%async_computation.1 | async-start | bytes 1572864 | tf_op jit(solution)/shard_map/all_to_all | solution.py:478
  56.8 34.1 %all-to-all-start.2 = ((bf16[32,4,8,384]{3,2,1,0:T(8,128)(2,1)}), bf16[32,4,8,384]{3,2,1,0:T(8,128)(2,1)}, u32[]{:S(2)}, u32[]{:S(2)}) async-start(bf16[32,4,8,384]{3,2,1,0:T(8,128)(2,1)} %shard_map.145), calls=%async_computation.2 | async-start | bytes 1572864 | tf_op jit(solution)/shard_map/all_to_all | solution.py:478
  90.9 56.0 %all-to-all-start.3 = ((bf16[32,4,8,384]{3,2,1,0:T(8,128)(2,1)}), bf16[32,4,8,384]{3,2,1,0:T(8,128)(2,1)S(1)}, u32[]{:S(2)}, u32[]{:S(2)}) async-start(bf16[32,4,8,384]{3,2,1,0:T(8,128)(2,1)} %shard_map.148), calls=%async_computation.3 | async-start | bytes 1572864 | tf_op jit(solution)/shard_map/all_to_all | solution.py:478
  179.3 6.2 %collective-permute-start = (bf16[1792,384]{1,0:T(8,128)(2,1)S(1)}, bf16[1792,384]{1,0:T(8,128)(2,1)S(1)}, u32[]{:S(2)}, u32[]{:S(2)}) collective-permute-start(bf16[1792,384]{1,0:T(8,128)(2,1)S(1)} %dynamic-slice_bitcast_fusion), channel_id=1, source_target_pairs={{0,1},{1,0},{2,3},{3,2},{4,5},{5,4},{6,7},{7,6},{8,9},{9,8},{10,11... | collective-permute-start | bytes 4128776 | tf_op jit(solution)/shard_map/ppermute | solution.py:410
  179.7 26.3 %all-to-all-start.4 = ((bf16[32,4,8,384]{3,2,1,0:T(8,128)(2,1)}), bf16[32,4,8,384]{3,2,1,0:T(8,128)(2,1)S(1)}, u32[]{:S(2)}, u32[]{:S(2)}) async-start(bf16[32,4,8,384]{3,2,1,0:T(8,128)(2,1)} %get-tuple-element.44), calls=%async_computation.4 | async-start | bytes 1572864 | tf_op jit(solution)/shard_map/all_to_all | solution.py:489
  188.2 48.0 %collective-permute-start.1 = (bf16[448,384]{1,0:T(8,128)(2,1)}, bf16[448,384]{1,0:T(8,128)(2,1)S(1)}, u32[]{:S(2)}, u32[]{:S(2)}) collective-permute-start(bf16[448,384]{1,0:T(8,128)(2,1)} %get-tuple-element.94), channel_id=1, source_target_pairs={{0,2},{1,3},{2,0},{3,1},{4,6},{5,7},{6,4},{7,5},{8,10},{9,11},{10,... | collective-permute-start | bytes 1032200 | tf_op jit(solution)/shard_map/ppermute | solution.py:410
  190.0 46.3 %collective-permute-start.3 = (bf16[448,384]{1,0:T(8,128)(2,1)}, bf16[448,384]{1,0:T(8,128)(2,1)}, u32[]{:S(2)}, u32[]{:S(2)}) collective-permute-start(bf16[448,384]{1,0:T(8,128)(2,1)} %get-tuple-element.95), channel_id=1, source_target_pairs={{0,6},{1,7},{2,4},{3,5},{4,2},{5,3},{6,0},{7,1},{8,14},{9,15},{10,... | collective-permute-start | bytes 1032200 | tf_op jit(solution)/shard_map/ppermute | solution.py:410
  191.4 44.8 %collective-permute-start.2 = (bf16[448,384]{1,0:T(8,128)(2,1)}, bf16[448,384]{1,0:T(8,128)(2,1)}, u32[]{:S(2)}, u32[]{:S(2)}) collective-permute-start(bf16[448,384]{1,0:T(8,128)(2,1)} %get-tuple-element.96), channel_id=1, source_target_pairs={{0,4},{1,5},{2,6},{3,7},{4,0},{5,1},{6,2},{7,3},{8,12},{9,13},{10,... | collective-permute-start | bytes 1032200 | tf_op jit(solution)/shard_map/ppermute | solution.py:410
  206.0 31.5 %all-to-all-start.5 = ((bf16[32,4,8,384]{3,2,1,0:T(8,128)(2,1)}), bf16[32,4,8,384]{3,2,1,0:T(8,128)(2,1)S(1)}, u32[]{:S(2)}, u32[]{:S(2)}) async-start(bf16[32,4,8,384]{3,2,1,0:T(8,128)(2,1)} %get-tuple-element.50), calls=%async_computation.5 | async-start | bytes 1572864 | tf_op jit(solution)/shard_map/all_to_all | solution.py:489
  270.8 7.5 %collective-permute-start.7 = (bf16[160,384]{1,0:T(8,128)(2,1)S(1)}, bf16[160,384]{1,0:T(8,128)(2,1)S(1)}, u32[]{:S(2)}, u32[]{:S(2)}) collective-permute-start(bf16[160,384]{1,0:T(8,128)(2,1)S(1)} %get-tuple-element.98), channel_id=1, source_target_pairs={{0,6},{1,7},{2,4},{3,5},{4,2},{5,3},{6,0},{7,1},{8,14},{9,15},{10,... | collective-permute-start | bytes 368648 | tf_op jit(solution)/shard_map/ppermute | solution.py:410
  272.2 7.4 %collective-permute-start.6 = (bf16[160,384]{1,0:T(8,128)(2,1)S(1)}, bf16[160,384]{1,0:T(8,128)(2,1)S(1)}, u32[]{:S(2)}, u32[]{:S(2)}) collective-permute-start(bf16[160,384]{1,0:T(8,128)(2,1)S(1)} %get-tuple-element.99), channel_id=1, source_target_pairs={{0,4},{1,5},{2,6},{3,7},{4,0},{5,1},{6,2},{7,3},{8,12},{9,13},{10,... | collective-permute-start | bytes 368648 | tf_op jit(solution)/shard_map/ppermute | solution.py:410
  279.8 6.2 %collective-permute-start.8 = (bf16[152,384]{1,0:T(8,128)(2,1)S(1)}, bf16[152,384]{1,0:T(8,128)(2,1)S(1)}, u32[]{:S(2)}, u32[]{:S(2)}) collective-permute-start(bf16[152,384]{1,0:T(8,128)(2,1)S(1)} %get-tuple-element.106), channel_id=1, source_target_pairs={{0,8},{8,0},{16,24},{24,16},{1,9},{9,1},{17,25},{25,17},{2,10},{10... | collective-permute-start | bytes 350216 | tf_op jit(solution)/shard_map/ppermute | solution.py:410
  281.3 11.2 %collective-permute-start.9 = (bf16[152,384]{1,0:T(8,128)(2,1)S(1)}, bf16[152,384]{1,0:T(8,128)(2,1)S(1)}, u32[]{:S(2)}, u32[]{:S(2)}) collective-permute-start(bf16[152,384]{1,0:T(8,128)(2,1)S(1)} %get-tuple-element.107), channel_id=1, source_target_pairs={{0,16},{8,24},{16,0},{24,8},{1,17},{9,25},{17,1},{25,9},{2,18},{10... | collective-permute-start | bytes 350216 | tf_op jit(solution)/shard_map/ppermute | solution.py:410
  283.8 8.8 %collective-permute-start.10 = (bf16[152,384]{1,0:T(8,128)(2,1)S(1)}, bf16[152,384]{1,0:T(8,128)(2,1)S(1)}, u32[]{:S(2)}, u32[]{:S(2)}) collective-permute-start(bf16[152,384]{1,0:T(8,128)(2,1)S(1)} %get-tuple-element.108), channel_id=1, source_target_pairs={{0,24},{8,16},{16,8},{24,0},{1,25},{9,17},{17,9},{25,1},{2,26},{10... | collective-permute-start | bytes 350216 | tf_op jit(solution)/shard_map/ppermute | solution.py:410
  292.6 7.9 %collective-permute-start.13 = (bf16[152,384]{1,0:T(8,128)(2,1)S(1)}, bf16[152,384]{1,0:T(8,128)(2,1)S(1)}, u32[]{:S(2)}, u32[]{:S(2)}) collective-permute-start(bf16[152,384]{1,0:T(8,128)(2,1)S(1)} %fusion.14), channel_id=1, source_target_pairs={{0,24},{8,16},{16,8},{24,0},{1,25},{9,17},{17,9},{25,1},{2,26},{10... | collective-permute-start | bytes 350216 | tf_op jit(solution)/shard_map/ppermute | solution.py:410
  295.1 9.1 %collective-permute-start.12 = (bf16[152,384]{1,0:T(8,128)(2,1)S(1)}, bf16[152,384]{1,0:T(8,128)(2,1)S(1)}, u32[]{:S(2)}, u32[]{:S(2)}) collective-permute-start(bf16[152,384]{1,0:T(8,128)(2,1)S(1)} %fusion.14), channel_id=1, source_target_pairs={{0,16},{8,24},{16,0},{24,8},{1,17},{9,25},{17,1},{25,9},{2,18},{10... | collective-permute-start | bytes 350216 | tf_op jit(solution)/shard_map/ppermute | solution.py:410
  296.0 8.2 %collective-permute-start.11 = (bf16[152,384]{1,0:T(8,128)(2,1)S(1)}, bf16[152,384]{1,0:T(8,128)(2,1)S(1)}, u32[]{:S(2)}, u32[]{:S(2)}) collective-permute-start(bf16[152,384]{1,0:T(8,128)(2,1)S(1)} %fusion.14), channel_id=1, source_target_pairs={{0,8},{8,0},{16,24},{24,16},{1,9},{9,1},{17,25},{25,17},{2,10},{10... | collective-permute-start | bytes 350216 | tf_op jit(solution)/shard_map/ppermute | solution.py:410
  304.4 15.1 %collective-permute-start.15 = (bf16[608,384]{1,0:T(8,128)(2,1)S(1)}, bf16[608,384]{1,0:T(8,128)(2,1)S(1)}, u32[]{:S(2)}, u32[]{:S(2)}) collective-permute-start(bf16[608,384]{1,0:T(8,128)(2,1)S(1)} %get-tuple-element.101), channel_id=1, source_target_pairs={{0,4},{1,5},{2,6},{3,7},{4,0},{5,1},{6,2},{7,3},{8,12},{9,13},{10,... | collective-permute-start | bytes 1400840 | tf_op jit(solution)/shard_map/ppermute | solution.py:410
  304.9 17.1 %collective-permute-start.14 = (bf16[608,384]{1,0:T(8,128)(2,1)S(1)}, bf16[608,384]{1,0:T(8,128)(2,1)S(1)}, u32[]{:S(2)}, u32[]{:S(2)}) collective-permute-start(bf16[608,384]{1,0:T(8,128)(2,1)S(1)} %get-tuple-element.101), channel_id=1, source_target_pairs={{0,2},{1,3},{2,0},{3,1},{4,6},{5,7},{6,4},{7,5},{8,10},{9,11},{10,... | collective-permute-start | bytes 1400840 | tf_op jit(solution)/shard_map/ppermute | solution.py:410
  306.5 27.5 %collective-permute-start.16 = (bf16[608,384]{1,0:T(8,128)(2,1)S(1)}, bf16[608,384]{1,0:T(8,128)(2,1)S(1)}, u32[]{:S(2)}, u32[]{:S(2)}) collective-permute-start(bf16[608,384]{1,0:T(8,128)(2,1)S(1)} %get-tuple-element.101), channel_id=1, source_target_pairs={{0,6},{1,7},{2,4},{3,5},{4,2},{5,3},{6,0},{7,1},{8,14},{9,15},{10,... | collective-permute-start | bytes 1400840 | tf_op jit(solution)/shard_map/ppermute | solution.py:410
  308.0 28.1 %all-to-all-start.6 = ((bf16[32,4,8,384]{3,2,1,0:T(8,128)(2,1)}), bf16[32,4,8,384]{3,2,1,0:T(8,128)(2,1)S(1)}, u32[]{:S(2)}, u32[]{:S(2)}) async-start(bf16[32,4,8,384]{3,2,1,0:T(8,128)(2,1)} %get-tuple-element.56), calls=%async_computation.6 | async-start | bytes 1572864 | tf_op jit(solution)/shard_map/all_to_all | solution.py:489
  336.1 30.1 %collective-permute-start.17 = (bf16[2432,384]{1,0:T(8,128)(2,1)}, bf16[2432,384]{1,0:T(8,128)(2,1)}, u32[]{:S(2)}, u32[]{:S(2)}) collective-permute-start(bf16[2432,384]{1,0:T(8,128)(2,1)} %get-tuple-element.88), channel_id=1, source_target_pairs={{0,1},{1,0},{2,3},{3,2},{4,5},{5,4},{6,7},{7,6},{8,9},{9,8},{10,11... | collective-permute-start | bytes 5603336 | tf_op jit(solution)/shard_map/ppermute | solution.py:410
  336.1 24.6 %all-to-all-start.7 = ((bf16[32,4,8,384]{3,2,1,0:T(8,128)(2,1)}), bf16[32,4,8,384]{3,2,1,0:T(8,128)(2,1)S(1)}, u32[]{:S(2)}, u32[]{:S(2)}) async-start(bf16[32,4,8,384]{3,2,1,0:T(8,128)(2,1)} %get-tuple-element.65), calls=%async_computation.7 | async-start | bytes 1572864 | tf_op jit(solution)/shard_map/all_to_all | solution.py:489
  (15 other events, 183.7 us)
where the time goes:
time: 386 us; the launch traced here: 380 us
  Pallas kernels  178 us (46%)
  waiting for transfers between devices  110 us (28%)
  starting transfers between devices  58.4 us (15%)
  local copies, waits for them, and re-layouts  21.8 us (6%)
  other arithmetic  10.2 us (3%)
    pallas_call x2, Pallas kernels, mlp_call(): pl.pallas_call(mlp_kernel, grid=(groups,), in_specs=[per_group((width, to...  58.5 us
    pallas_call x2, Pallas kernels, back_call(): pl.pallas_call(back_kernel, grid=(groups,), in_specs=[per_group((width, t...  53.5 us
    ppermute x18, waiting for transfers between devices, swap(): lax.ppermute(values, axis, [(i, i ^ offset) for i in range(lax.axis_size(...  46.5 us
    pallas_call x2, Pallas kernels, attend_call(): pl.pallas_call(attend_kernel, grid=(groups,), in_specs=[pieces_spec(act),...  40.9 us
    all_to_all x4, waiting for transfers between devices, send(): lax.all_to_all(tie(sends, *after), both, split_axis=0, concat_axis=0, til...  33 us
    all_to_all x4, waiting for transfers between devices, give_back(): return lax.all_to_all(pieces, both, split_axis=0, concat_axis=0, tiled=True)  30.3 us
    all_to_all x4, starting transfers between devices, send(): lax.all_to_all(tie(sends, *after), both, split_axis=0, concat_axis=0, til...  20.7 us
    ppermute x18, starting transfers between devices, swap(): lax.ppermute(values, axis, [(i, i ^ offset) for i in range(lax.axis_size(...  20.4 us
  transfers between devices with their start and end apart: 26, of which 15 were waited for; matrix products, arithmetic and copies ran while one was open for 3% of the time, Pallas kernels for 31%

commit v1 on v0

--- a/solution.py
+++ b/solution.py
@@ -9,6 +9,7 @@
 HEADS = 12
 GRID = 16
 SUB = 8
+PIECE = 512
 EPSILON = 1e-05
 INV_ROOT_TAU = 0.3989422804014327
 SQRT_HALF = 0.7071067811865476
@@ -103,8 +104,12 @@
         grads_ref[rows:] = jnp.where(first, gains, 0.0).astype(grads_ref.dtype)
 
 
-def attend_kernel(act_ref, gain_ref, joint_ref, flat_ref, triple_ref, mixed_ref):
-    width = gain_ref.shape[0]
+def lane_halves(count):
+    return [slice(start, start + 128) for start in range(0, count, 128)]
+
+
+def attend_kernel(act_ref, gain_ref, joint_ref, flat_ref, triple_ref, mixed_ref, stat_ref, score_ref):
+    width, tokens = gain_ref.shape
     head = width // HEADS
     factor = head ** (-0.5) * LOG2E
     flat = load_rows(act_ref).T
@@ -112,25 +117,35 @@
     normed, _ = normalize(flat)
     scaled = (normed * gain_ref[...]).astype(BF)
     triple_ref[0] = nn(joint_ref[...], scaled).astype(BF)
-    for h in range(HEADS):
-        rows = slice(h * head, (h + 1) * head)
+
+    def score(h):
         queries = triple_ref[0, h * head : (h + 1) * head]
         keys = triple_ref[0, width + h * head : width + (h + 1) * head]
+        score_ref[h % 2] = tn(keys, queries)
+
+    score(0)
+    for h in range(HEADS):
+        if h + 1 < HEADS:
+            score(h + 1)
         values = triple_ref[0, 2 * width + h * head : 2 * width + (h + 1) * head]
-        scores = tn(keys, queries)
-        weights = jnp.exp2((scores - jnp.max(scores, axis=0, keepdims=True)) * factor)
-        weights = weights * (1.0 / jnp.sum(weights, axis=0, keepdims=True))
-        mixed_ref[0, rows] = nn(values, weights.astype(BF)).astype(BF)
+        for lanes in lane_halves(tokens):
+            scores = score_ref[h % 2, :, lanes]
+            top = jnp.max(scores, axis=0, keepdims=True)
+            weights = jnp.exp2((scores - top) * factor)
+            total = jnp.sum(weights, axis=0, keepdims=True)
+            stat_ref[0, h : h + 1, lanes] = top * factor + jnp.log2(total)
+            weights = (weights * (1.0 / total)).astype(BF)
+            mixed_ref[0, h * head : (h + 1) * head, lanes] = nn(values, weights).astype(BF)
 
 
 def mlp_kernel(
     flat_ref, mixed_ref, cot_ref, gain_ref, out_t_ref, up_t_ref, down_t_ref, down_ref, up_ref, out_w_ref,
     *rest,
 ):
-    carried = rest[:-6]
-    result_ref, grad_att_ref, grad_mixed_ref, grads_ref, grad_gain_ref, acc_ref = rest[-6:]
+    carried = rest[:-13]
+    result_ref, grad_att_ref, grad_mixed_ref, grads_ref, grad_gain_ref, acc_ref = rest[-13:-7]
+    scaled_ref, cot_b_ref, cot_tb_ref, pre_ref, grad_hidden_ref, hidden_ref, grad_pre_ref = rest[-7:]
     step = pl.program_id(0)
-    width = gain_ref.shape[0]
     hidden_dim = up_ref.shape[1]
 
     @pl.when(step == 0)
@@ -146,20 +161,42 @@
     normed, inv_std = normalize(attended)
     gain = gain_ref[...]
     scaled = (normed * gain).astype(BF)
-    result = attended
-    grad_scaled = jnp.zeros_like(attended)
-    piece = width
-    for start in range(0, hidden_dim, piece):
-        part = slice(start, start + piece)
-        pre = nn(up_t_ref[part], scaled)
-        phi, gauss = gelu_parts(pre)
-        hidden = (pre * phi).astype(BF)
-        result = result + nn(down_t_ref[:, part], hidden)
-        acc_ref[part] += nn(hidden, cot_b)
-        grad_hidden = nn(down_ref[part], cot_tb).astype(BF).astype(F32)
-        grad_pre = (grad_hidden * (phi + pre * gauss * INV_ROOT_TAU)).astype(BF)
-        grad_scaled = grad_scaled + nn(up_ref[:, part], grad_pre)
-        acc_ref[hidden_dim + start : hidden_dim + start + piece] += nt(grad_pre, scaled)
+    scaled_ref[...] = scaled
+    cot_b_ref[...] = cot_b
+    cot_tb_ref[...] = cot_tb
+
+    def products(n):
+        part = slice(n * PIECE, (n + 1) * PIECE)
+        pre_ref[n % 2] = nn(up_t_ref[part], scaled_ref[...])
+        grad_hidden_ref[n % 2] = nn(down_ref[part], cot_tb_ref[...]).astype(BF)
+
+    def activate(n):
+        for start in range(0, PIECE, 32):
+            some = slice(start, start + 32)
+            here = slice(n * PIECE + start, n * PIECE + start + 32)
+            pre = pre_ref[n % 2, some]
+            phi, gauss = gelu_parts(pre)
+            hidden_ref[here] = (pre * phi).astype(BF)
+            slope = phi + pre * gauss * INV_ROOT_TAU
+            grad_pre_ref[here] = (grad_hidden_ref[n % 2, some].astype(F32) * slope).astype(BF)
+
+    def gather(n):
+        part = slice(n * PIECE, (n + 1) * PIECE)
+        acc_ref[part] += nn(hidden_ref[part], cot_b_ref[...])
+        there = slice(hidden_dim + n * PIECE, hidden_dim + (n + 1) * PIECE)
+        acc_ref[there] += nt(grad_pre_ref[part], scaled_ref[...])
+
+    pieces = hidden_dim // PIECE
+    products(0)
+    for n in range(pieces):
+        if n + 1 < pieces:
+            products(n + 1)
+        activate(n)
+        if n:
+            gather(n - 1)
+    gather(pieces - 1)
+    grad_scaled = nn(up_ref[...], grad_pre_ref[...])
+    result = attended + nn(down_t_ref[...], hidden_ref[...])
     store_rows(result_ref, result.T)
     grad_gain_ref[...] += fold_lanes(grad_scaled * normed)
     grad_att = cot_t + norm_back(grad_scaled * gain, normed, inv_std)
@@ -174,11 +211,12 @@
 
 
 def back_kernel(
-    flat_ref, triple_ref, grad_mixed_ref, grad_att_ref, gain_ref, joint_ref,
+    flat_ref, triple_ref, stat_ref, grad_mixed_ref, grad_att_ref, gain_ref, joint_ref,
     *rest,
 ):
-    carried = rest[:-5]
-    grad_in_ref, grads_ref, grad_gain_ref, acc_ref, grad_triple_ref = rest[-5:]
+    carried = rest[:-9]
+    grad_in_ref, grads_ref, grad_gain_ref, acc_ref, grad_triple_ref = rest[-9:-4]
+    score_ref, slope_ref, grad_score_ref, weight_ref = rest[-4:]
     step = pl.program_id(0)
     width = gain_ref.shape[0]
     head = width // HEADS
@@ -188,22 +226,37 @@
     def _():
         begin(carried, acc_ref, grad_gain_ref)
 
+    tokens = gain_ref.shape[1]
+
+    def rows(part, h):
+        return slice(part * width + h * head, part * width + (h + 1) * head)
+
+    def products(h):
+        score_ref[h % 2] = tn(triple_ref[0, rows(1, h)], triple_ref[0, rows(0, h)])
+        slope_ref[h % 2] = tn(triple_ref[0, rows(2, h)], grad_mixed_ref[0, rows(0, h)])
+
+    def weigh(h):
+        for lanes in lane_halves(tokens):
+            weights = jnp.exp2(score_ref[h % 2, :, lanes] * (scale * LOG2E) - stat_ref[0, h : h + 1, lanes])
+            grad_weights = slope_ref[h % 2, :, lanes]
+            inner = jnp.sum(weights * grad_weights, axis=0, keepdims=True)
+            grad_score_ref[h % 2, :, lanes] = (weights * (grad_weights - inner) * scale).astype(BF)
+            weight_ref[h % 2, :, lanes] = weights.astype(BF)
+
+    def back(h):
+        grad_scores = grad_score_ref[h % 2]
+        grad_triple_ref[rows(0, h)] = nn(triple_ref[0, rows(1, h)], grad_scores).astype(BF)
+        grad_triple_ref[rows(1, h)] = nt(triple_ref[0, rows(0, h)], grad_scores).astype(BF)
+        grad_triple_ref[rows(2, h)] = nt(grad_mixed_ref[0, rows(0, h)], weight_ref[h % 2]).astype(BF)
+
+    products(0)
     for h in range(HEADS):
-        queries = triple_ref[0, h * head : (h + 1) * head]
-        keys = triple_ref[0, width + h * head : width + (h + 1) * head]
-        values = triple_ref[0, 2 * width + h * head : 2 * width + (h + 1) * head]
-        grad_heads = grad_mixed_ref[0, h * head : (h + 1) * head]
-        scores = tn(keys, queries)
-        weights = jnp.exp2((scores - jnp.max(scores, axis=0, keepdims=True)) * (scale * LOG2E))
-        weights = weights * (1.0 / jnp.sum(weights, axis=0, keepdims=True))
-        grad_weights = tn(values, grad_heads)
-        inner = jnp.sum(weights * grad_weights, axis=0, keepdims=True)
-        grad_scores = (weights * (grad_weights - inner) * scale).astype(BF)
-        grad_triple_ref[h * head : (h + 1) * head] = nn(keys, grad_scores).astype(BF)
-        grad_triple_ref[width + h * head : width + (h + 1) * head] = nt(queries, grad_scores).astype(BF)
-        grad_triple_ref[2 * width + h * head : 2 * width + (h + 1) * head] = nt(
-            grad_heads, weights.astype(BF)
-        ).astype(BF)
+        if h + 1 < HEADS:
+            products(h + 1)
+        weigh(h)
+        if h:
+            back(h - 1)
+    back(HEADS - 1)
     normed, inv_std = normalize(flat_ref[0].astype(F32))
     gain = gain_ref[...]
     scaled = (normed * gain).astype(BF)
@@ -325,12 +378,19 @@
         attend_kernel,
         grid=(groups,),
         in_specs=[pieces_spec(act), whole(gain), whole(joint_t)],
-        out_specs=[per_group((width, tokens)), per_group((3 * width, tokens)), per_group((width, tokens))],
+        out_specs=[
+            per_group((width, tokens)),
+            per_group((3 * width, tokens)),
+            per_group((width, tokens)),
+            per_group((16, tokens)),
+        ],
         out_shape=[
             jax.ShapeDtypeStruct((groups, width, tokens), BF),
             jax.ShapeDtypeStruct((groups, 3 * width, tokens), BF),
             jax.ShapeDtypeStruct((groups, width, tokens), BF),
-        ],
+            jax.ShapeDtypeStruct((groups, 16, tokens), F32),
+        ],
+        scratch_shapes=[pltpu.VMEM((2, tokens, tokens), F32)],
         compiler_params=params(),
         cost_estimate=cost(3e9 * groups, 12 * groups * tokens * width, 0),
     )(act, gain, joint_t)
@@ -360,13 +420,22 @@
             jax.ShapeDtypeStruct((rows + spare, width), BF if spare else F32),
             jax.ShapeDtypeStruct((width, 128), F32),
         ],
-        scratch_shapes=[pltpu.VMEM((rows, width), F32)],
+        scratch_shapes=[
+            pltpu.VMEM((rows, width), F32),
+            pltpu.VMEM((width, tokens), BF),
+            pltpu.VMEM((tokens, width), BF),
+            pltpu.VMEM((width, tokens), BF),
+            pltpu.VMEM((2, PIECE, tokens), F32),
+            pltpu.VMEM((2, PIECE, tokens), BF),
+            pltpu.VMEM((hidden_dim, tokens), BF),
+            pltpu.VMEM((hidden_dim, tokens), BF),
+        ],
         compiler_params=params(),
         cost_estimate=cost(4e9 * groups, 14 * groups * tokens * width, 0),
     )(flat, mixed, cot, gain, *weights, *carried)
 
 
-def back_call(flat, triple, grad_mixed, grad_att, gain, joint, like, carried, spare):
+def back_call(flat, triple, stat, grad_mixed, grad_att, gain, joint, like, carried, spare):
     rows = joint.shape[1]
     pieces, groups, sub, width = like.shape
     tokens = pieces * sub
@@ -376,6 +445,7 @@
         in_specs=[
             per_group((width, tokens)),
             per_group((3 * width, tokens)),
+            per_group((16, tokens)),
             per_group((width, tokens)),
             per_group((width, tokens)),
             whole(gain),
@@ -392,10 +462,17 @@
             jax.ShapeDtypeStruct((rows + spare, width), BF if spare else F32),
             jax.ShapeDtypeStruct((width, 128), F32),
         ],
-        scratch_shapes=[pltpu.VMEM((3 * width, width), F32), pltpu.VMEM((3 * width, tokens), BF)],
+        scratch_shapes=[
+            pltpu.VMEM((3 * width, width), F32),
+            pltpu.VMEM((3 * width, tokens), BF),
+            pltpu.VMEM((2, tokens, tokens), F32),
+            pltpu.VMEM((2, tokens, tokens), F32),
+            pltpu.VMEM((2, tokens, tokens), BF),
+            pltpu.VMEM((2, tokens, tokens), BF),
+        ],
         compiler_params=params(),
         cost_estimate=cost(6e9 * groups, 18 * groups * tokens * width, 0),
-    )(flat, triple, grad_mixed, grad_att, gain, joint, *carried)
+    )(flat, triple, stat, grad_mixed, grad_att, gain, joint, *carried)
 
 
 def tie(value, *after):
@@ -417,6 +494,14 @@
     for other in range(1, count):
         part = lax.dynamic_index_in_dim(parts, mine ^ other, 0, keepdims=False)
         total = total + swap(part, axis, other << low).astype(F32)
+    return total.astype(BF)
+
+
+def share_sum(values, axis, low, high):
+    _, count = peers(axis, low, high)
+    total = values.astype(F32)
+    for other in range(1, count):
+        total = total + swap(values, axis, other << low).astype(F32)
     return total.astype(BF)
 
 
@@ -522,7 +607,7 @@
     tails, out_parts, carried = [], [], ()
     before = cot[-1:]
     for k in range(chunks):
-        flat, _, mixed = fronts[k]
+        flat, _, mixed, _ = fronts[k]
         spare = unit - tail_rows % unit if k == chunks - 1 else 0
         tails.append(mlp_call(flat, mixed, cot[k], gain_two, weights, carried, spare))
         carried = tails[-1][3:]
@@ -532,33 +617,31 @@
     tail_sum = carried[0]
     heads, in_parts, carried = [], [], ()
     for k in range(chunks):
-        flat, triple, _ = fronts[k]
+        flat, triple, _, stat = fronts[k]
         _, grad_att, grad_mixed = tails[k][:3]
         spare = unit - head_rows % unit if k == chunks - 1 else 0
         grad_mixed = tie(grad_mixed, out_parts[k], *((tail_sum,) if k else ()))
         heads.append(
-            back_call(flat, triple, grad_mixed, grad_att, gain_one, joint_weight, cot[k], carried, spare)
+            back_call(flat, triple, stat, grad_mixed, grad_att, gain_one, joint_weight, cot[k], carried, spare)
         )
         carried = heads[-1][1:]
         in_parts.append(give_back(heads[-1][0], *before))
         before = in_parts[-1:]
         if k < len(steps):
             tail_sum = scatter_sum(tail_sum, *steps[k])
-    head_sum = tie(carried[0], tail_sum)
-    for stage in steps[:-1]:
-        head_sum = scatter_sum(head_sum, *stage)
-    rows_left = lax.axis_size("row")
-    split = head_sum.shape[0] // rows_left
-    both_sums = jnp.concatenate(
-        [part.reshape(rows_left, -1, channels) for part in (head_sum, tail_sum)], axis=1
-    )
-    width_all = both_sums.shape[1]
-    both_sums = scatter_sum(both_sums.reshape(-1, channels), *steps[-1])
-    for stage in steps[::-1]:
-        both_sums = collect(both_sums, *stage)
-    both_sums = both_sums.reshape(devices, width_all, channels)
-    head_sum = both_sums[:, :split].reshape(-1, channels).astype(F32) * factor
-    tail_sum = both_sums[:, split:].reshape(-1, channels).astype(F32) * factor
+    head_sum = carried[0]
+    near, cols, rows = steps
+    head_sum = scatter_sum(head_sum, *near)
+    tail_sum = scatter_sum(tail_sum, *rows)
+    head_sum = scatter_sum(head_sum, *cols)
+    tail_sum = collect(tail_sum, *rows)
+    head_sum = share_sum(head_sum, *rows)
+    tail_sum = collect(tail_sum, *cols)
+    head_sum = collect(head_sum, *cols)
+    tail_sum = collect(tail_sum, *near)
+    head_sum = collect(head_sum, *near)
+    head_sum = head_sum.astype(F32) * factor
+    tail_sum = tail_sum.astype(F32) * factor
     block_out = to_tile(out_parts)
     grad_input = to_tile(in_parts)
     return (

time: 386 us -> 334 us (0.87); the launches traced: 380 us -> 332 us
  Pallas kernels: 178 us -> 130 us
  waiting for transfers between devices: 110 us -> 99.9 us
  starting transfers between devices: 58.4 us -> 64.8 us
    all_to_all x4, waiting for transfers between devices: 30.3 us -> 7.33 us  [give_back(): return lax.all_to_all(pieces, both, split_axis=0, concat_axis=0, tiled=True)]
    pallas_call x2, Pallas kernels: 53.5 us -> 30.9 us  [back_call(): pl.pallas_call(back_kernel, grid=(groups,), in_specs=[per_group((width, t...]
    pallas_call x2, Pallas kernels: 40.9 us -> 26.8 us  [attend_call(): pl.pallas_call(attend_kernel, grid=(groups,), in_specs=[pieces_spec(act),...]
    ppermute x18 -> x25, waiting for transfers between devices: 46.5 us -> 59.5 us  [swap(): lax.ppermute(values, axis, [(i, i ^ offset) for i in range(lax.axis_size(...]
    pallas_call x2, Pallas kernels: 58.5 us -> 47.1 us  [mlp_call(): pl.pallas_call(mlp_kernel, grid=(groups,), in_specs=[per_group((width, to...]
    ppermute x18 -> x25, starting transfers between devices: 20.4 us -> 27.7 us  [swap(): lax.ppermute(values, axis, [(i, i ^ offset) for i in range(lax.axis_size(...]
    unnamed x32 -> x37, local copies, waits for them, and re-layouts: 11.6 us -> 7.99 us
  transfers between devices with their start and end apart: 26 -> 33, of which waited for: 15 -> 16; matrix products, arithmetic and copies ran while one was open for 3% -> 10% of each run, Pallas kernels for 31% -> 29%
where the time goes in v1:
time: 334 us; the launch traced here: 332 us
  Pallas kernels  130 us (39%)
  waiting for transfers between devices  99.9 us (30%)
  starting transfers between devices  64.8 us (19%)
  local copies, waits for them, and re-layouts  23.6 us (7%)
  other arithmetic  13.2 us (4%)
    ppermute x25, waiting for transfers between devices, swap(): lax.ppermute(values, axis, [(i, i ^ offset) for i in range(lax.axis_size(...  59.5 us
    pallas_call x2, Pallas kernels, mlp_call(): pl.pallas_call(mlp_kernel, grid=(groups,), in_specs=[per_group((width, to...  47.1 us
    all_to_all x4, waiting for transfers between devices, send(): lax.all_to_all(tie(sends, *after), both, split_axis=0, concat_axis=0, til...  33 us
    pallas_call x2, Pallas kernels, back_call(): pl.pallas_call(back_kernel, grid=(groups,), in_specs=[per_group((width, t...  30.9 us
    ppermute x25, starting transfers between devices, swap(): lax.ppermute(values, axis, [(i, i ^ offset) for i in range(lax.axis_size(...  27.7 us
    pallas_call x2, Pallas kernels, attend_call(): pl.pallas_call(attend_kernel, grid=(groups,), in_specs=[pieces_spec(act),...  26.8 us
    all_to_all x4, starting transfers between devices, send(): lax.all_to_all(tie(sends, *after), both, split_axis=0, concat_axis=0, til...  20.6 us
    all_to_all x4, starting transfers between devices, give_back(): return lax.all_to_all(pieces, both, split_axis=0, concat_axis=0, tiled=True)  16.4 us
  transfers between devices with their start and end apart: 33, of which 16 were waited for; matrix products, arithmetic and copies ran while one was open for 10% of the time, Pallas kernels for 29%

profile of v1, /device:TPU:0, one launch (start us, length us, event | category | flops | bytes accessed | tf_op | source)
XLA Modules:
  0.0 332.5 jit_solution(13496430235474638760)
XLA Ops:
  0.6 4.0 %shard_map.143 = bf16[32,4,8,384]{3,2,1,0:T(8,128)(2,1)} custom-call(bf16[4,4,4,32,384]{4,3,2,1,0:T(8,128)(2,1)} %bitcast.101), custom_call_target="tpu_custom_call" | custom-call | flops 1000000 | bytes 1572864 | tf_op jit(solution)/shard_map/pallas_call | solution.py:323
  4.6 7.3 %all-to-all-start = ((bf16[32,4,8,384]{3,2,1,0:T(8,128)(2,1)}), bf16[32,4,8,384]{3,2,1,0:T(8,128)(2,1)S(1)}, u32[]{:S(2)}, u32[]{:S(2)}) async-start(bf16[32,4,8,384]{3,2,1,0:T(8,128)(2,1)} %shard_map.143), calls=%async_computation | async-start | bytes 1572864 | tf_op jit(solution)/shard_map/all_to_all | solution.py:563
  12.0 4.0 %shard_map.146 = bf16[32,4,8,384]{3,2,1,0:T(8,128)(2,1)} custom-call(bf16[4,4,4,32,384]{4,3,2,1,0:T(8,128)(2,1)} %bitcast.102), custom_call_target="tpu_custom_call" | custom-call | flops 1000000 | bytes 1572864 | tf_op jit(solution)/shard_map/pallas_call | solution.py:323
  16.0 16.6 %all-to-all-done.act_ref = bf16[32,4,8,384]{3,2,1,0:T(8,128)(2,1)S(1)} async-done(((bf16[32,4,8,384]{3,2,1,0:T(8,128)(2,1)}), bf16[32,4,8,384]{3,2,1,0:T(8,128)(2,1)S(1)}, u32[]{:S(2)}, u32[]{:S(2)}) %all-to-all-start) | async-done | bytes 786464 | tf_op jit(solution)/shard_map/all_to_all | solution.py:563
  36.2 4.1 %shard_map.145 = bf16[32,4,8,384]{3,2,1,0:T(8,128)(2,1)} custom-call(bf16[4,4,4,32,384]{4,3,2,1,0:T(8,128)(2,1)} %bitcast.103), custom_call_target="tpu_custom_call" | custom-call | flops 1000000 | bytes 1572864 | tf_op jit(solution)/shard_map/pallas_call | solution.py:323
  40.3 16.5 %all-to-all-done.1.act_ref = bf16[32,4,8,384]{3,2,1,0:T(8,128)(2,1)S(1)} async-done(((bf16[32,4,8,384]{3,2,1,0:T(8,128)(2,1)}), bf16[32,4,8,384]{3,2,1,0:T(8,128)(2,1)S(1)}, u32[]{:S(2)}, u32[]{:S(2)}) %all-to-all-start.1) | async-done | bytes 786464 | tf_op jit(solution)/shard_map/all_to_all | solution.py:563
  65.7 4.0 %shard_map.148 = bf16[32,4,8,384]{3,2,1,0:T(8,128)(2,1)} custom-call(bf16[4,4,4,32,384]{4,3,2,1,0:T(8,128)(2,1)} %bitcast.104), custom_call_target="tpu_custom_call" | custom-call | flops 1000000 | bytes 1572864 | tf_op jit(solution)/shard_map/pallas_call | solution.py:323
  70.5 13.4 %shard_map.144 = (bf16[4,384,256]{2,1,0:T(8,128)(2,1)}, bf16[4,1152,256]{2,1,0:T(8,128)(2,1)}, bf16[4,384,256]{2,1,0:T(8,128)(2,1)}, f32[4,16,256]{2,1,0:T(8,128)}) custom-call(bf16[32,4,8,384]{3,2,1,0:T(8,128)(2,1)} %copy-done.11, f32[384,256]{1,0:T(8,128)} %broadcast_in_dim.4.gain_ref, bf16[1152,384]{1,0:T(8,128)(2,1)} %bitcast.129), custom_call_target="tpu_custom_call" | custom-call | flops 12000000000 | bytes 4718592 | tf_op jit(solution)/shard_map/pallas_call | solution.py:377
  83.9 6.0 %all-to-all-start.3 = ((bf16[32,4,8,384]{3,2,1,0:T(8,128)(2,1)}), bf16[32,4,8,384]{3,2,1,0:T(8,128)(2,1)S(1)}, u32[]{:S(2)}, u32[]{:S(2)}) async-start(bf16[32,4,8,384]{3,2,1,0:T(8,128)(2,1)} %shard_map.148), calls=%async_computation.3 | async-start | bytes 1572864 | tf_op jit(solution)/shard_map/all_to_all | solution.py:563
  89.9 13.4 %shard_map.149 = (bf16[4,384,256]{2,1,0:T(8,128)(2,1)}, bf16[4,1152,256]{2,1,0:T(8,128)(2,1)}, bf16[4,384,256]{2,1,0:T(8,128)(2,1)}, f32[4,16,256]{2,1,0:T(8,128)}) custom-call(bf16[32,4,8,384]{3,2,1,0:T(8,128)(2,1)} %copy-done.10, f32[384,256]{1,0:T(8,128)} %broadcast_in_dim.4.gain_ref, bf16[1152,384]{1,0:T(8,128)(2,1)} %bitcast.130), custom_call_target="tpu_custom_call" | custom-call | flops 12000000000 | bytes 4718592 | tf_op jit(solution)/shard_map/pallas_call | solution.py:377
  104.2 23.1 %shard_map.147 = (bf16[32,4,8,384]{3,2,1,0:T(8,128)(2,1)}, f32[4,384,256]{2,1,0:T(8,128)}, bf16[4,384,256]{2,1,0:T(8,128)(2,1)}, f32[3456,384]{1,0:T(8,128)}, f32[384,128]{1,0:T(8,128)}) custom-call(bf16[4,384,256]{2,1,0:T(8,128)(2,1)} %get-tuple-element.39.flat_ref, bf16[4,384,256]{2,1,0:T(8,128)(2,1)} %get-tuple-element.40.mixed_ref, ...), custom_call_target="tpu_custom_call" | custom-call | flops 16000000000 | bytes 5505024 | tf_op jit(solution)/shard_map/pallas_call | solution.py:404
  128.2 24.0 %shard_map.150 = (bf16[32,4,8,384]{3,2,1,0:T(8,128)(2,1)}, f32[4,384,256]{2,1,0:T(8,128)}, bf16[4,384,256]{2,1,0:T(8,128)(2,1)}, bf16[3584,384]{1,0:T(8,128)(2,1)}, f32[384,128]{1,0:T(8,128)}) custom-call(bf16[4,384,256]{2,1,0:T(8,128)(2,1)} %get-tuple-element.46.flat_ref, bf16[4,384,256]{2,1,0:T(8,128)(2,1)} %get-tuple-element.47.mixed_ref, ...), custom_call_target="tpu_custom_call" | custom-call | flops 16000000000 | bytes 5505024 | tf_op jit(solution)/shard_map/pallas_call | solution.py:404
  153.9 5.7 %all-to-all-start.4 = ((bf16[32,4,8,384]{3,2,1,0:T(8,128)(2,1)}), bf16[32,4,8,384]{3,2,1,0:T(8,128)(2,1)S(1)}, u32[]{:S(2)}, u32[]{:S(2)}) async-start(bf16[32,4,8,384]{3,2,1,0:T(8,128)(2,1)} %get-tuple-element.45), calls=%async_computation.4 | async-start | bytes 1572864 | tf_op jit(solution)/shard_map/all_to_all | solution.py:574
  165.7 12.0 %collective-permute-done.12 = bf16[448,384]{1,0:T(8,128)(2,1)S(1)} collective-permute-done((bf16[448,384]{1,0:T(8,128)(2,1)}, bf16[448,384]{1,0:T(8,128)(2,1)S(1)}, u32[]{:S(2)}, u32[]{:S(2)}) %collective-permute-start.12) | collective-permute-done | bytes 344096 | tf_op jit(solution)/shard_map/ppermute | solution.py:487
  177.7 8.8 %collective-permute-done.14 = bf16[448,384]{1,0:T(8,128)(2,1)S(1)} collective-permute-done((bf16[448,384]{1,0:T(8,128)(2,1)}, bf16[448,384]{1,0:T(8,128)(2,1)S(1)}, u32[]{:S(2)}, u32[]{:S(2)}) %collective-permute-start.14) | collective-permute-done | bytes 344096 | tf_op jit(solution)/shard_map/ppermute | solution.py:487
  211.9 15.1 %shard_map.152 = (bf16[32,4,8,384]{3,2,1,0:T(8,128)(2,1)}, f32[1152,384]{1,0:T(8,128)}, f32[384,128]{1,0:T(8,128)}) custom-call(bf16[4,384,256]{2,1,0:T(8,128)(2,1)} %get-tuple-element.39.flat_ref, bf16[4,1152,256]{2,1,0:T(8,128)(2,1)} %get-tuple-element.52.triple_ref, f32[4,16,256]{2,1,0:T(8,128)} %get-tuple-element.53.stat_ref, ...), custom_call_target="tpu_custom_call" | custom-call | flops 24000000000 | bytes 7077888 | tf_op jit(solution)/shard_map/pallas_call | solution.py:442
  227.0 6.2 %collective-permute-done.23 = bf16[448,384]{1,0:T(8,128)(2,1)S(1)} collective-permute-done((bf16[448,384]{1,0:T(8,128)(2,1)S(1)}, bf16[448,384]{1,0:T(8,128)(2,1)S(1)}, u32[]{:S(2)}, u32[]{:S(2)}) %collective-permute-start.23) | collective-permute-done | bytes 344096 | tf_op jit(solution)/shard_map/ppermute | solution.py:487
  234.9 15.8 %shard_map.153 = (bf16[32,4,8,384]{3,2,1,0:T(8,128)(2,1)}, bf16[1280,384]{1,0:T(8,128)(2,1)}, f32[384,128]{1,0:T(8,128)}) custom-call(bf16[4,384,256]{2,1,0:T(8,128)(2,1)} %get-tuple-element.46.flat_ref, bf16[4,1152,256]{2,1,0:T(8,128)(2,1)} %get-tuple-element.59.triple_ref, f32[4,16,256]{2,1,0:T(8,128)} %get-tuple-element.60.stat_ref, ...), custom_call_target="tpu_custom_call" | custom-call | flops 24000000000 | bytes 7077888 | tf_op jit(solution)/shard_map/pallas_call | solution.py:442
  262.6 4.6 %shard_map.151 = bf16[4,4,4,32,384]{4,3,2,1,0:T(8,128)(2,1)} custom-call(bf16[32,4,8,384]{3,2,1,0:T(8,128)(2,1)} %copy-done, bf16[32,4,8,384]{3,2,1,0:T(8,128)(2,1)} %copy-done.2), custom_call_target="tpu_custom_call" | custom-call | flops 1000000 | bytes 3145728 | tf_op jit(solution)/shard_map/pallas_call | solution.py:341
  274.2 8.7 %collective-permute-done.7 = bf16[160,384]{1,0:T(8,128)(2,1)S(1)} collective-permute-done((bf16[160,384]{1,0:T(8,128)(2,1)S(1)}, bf16[160,384]{1,0:T(8,128)(2,1)S(1)}, u32[]{:S(2)}, u32[]{:S(2)}) %collective-permute-start.7) | collective-permute-done | bytes 122912 | tf_op jit(solution)/shard_map/ppermute | solution.py:487
  282.9 10.6 %collective-permute-done.6 = bf16[160,384]{1,0:T(8,128)(2,1)S(1)} collective-permute-done((bf16[160,384]{1,0:T(8,128)(2,1)S(1)}, bf16[160,384]{1,0:T(8,128)(2,1)S(1)}, u32[]{:S(2)}, u32[]{:S(2)}) %collective-permute-start.6) | collective-permute-done | bytes 122912 | tf_op jit(solution)/shard_map/ppermute | solution.py:487
  307.3 4.1 %fusion.21 = (f32[1536,384]{1,0:T(8,128)}, f32[384,1536]{0,1:T(8,128)S(1)}) fusion(f32[3584,384]{1,0:T(8,128)} %convert_multiply_fusion), kind=kLoop, calls=%fused_computation.70 | loop fusion | bytes 9437184 | tf_op jit(solution)/shard_map/slice | solution.py:653
  320.6 7.3 %all-to-all-done.7.refs_1_ = bf16[32,4,8,384]{3,2,1,0:T(8,128)(2,1)} async-done(((bf16[32,4,8,384]{3,2,1,0:T(8,128)(2,1)}), bf16[32,4,8,384]{3,2,1,0:T(8,128)(2,1)}, u32[]{:S(2)}, u32[]{:S(2)}) %all-to-all-start.7) | async-done | bytes 786464 | tf_op jit(solution)/shard_map/all_to_all | solution.py:574
  327.9 4.6 %shard_map.154 = bf16[4,4,4,32,384]{4,3,2,1,0:T(8,128)(2,1)} custom-call(bf16[32,4,8,384]{3,2,1,0:T(8,128)(2,1)} %copy-done.1, bf16[32,4,8,384]{3,2,1,0:T(8,128)(2,1)} %all-to-all-done.7.refs_1_), custom_call_target="tpu_custom_call" | custom-call | flops 1000000 | bytes 3145728 | tf_op jit(solution)/shard_map/pallas_call | solution.py:341
  (127 shorter events, 91.8 us)
Async XLA Ops:
  4.6 27.9 %all-to-all-start = ((bf16[32,4,8,384]{3,2,1,0:T(8,128)(2,1)}), bf16[32,4,8,384]{3,2,1,0:T(8,128)(2,1)S(1)}, u32[]{:S(2)}, u32[]{:S(2)}) async-start(bf16[32,4,8,384]{3,2,1,0:T(8,128)(2,1)} %shard_map.143), calls=%async_computation | async-start | bytes 1572864 | tf_op jit(solution)/shard_map/all_to_all | solution.py:563
  32.6 24.2 %all-to-all-start.1 = ((bf16[32,4,8,384]{3,2,1,0:T(8,128)(2,1)}), bf16[32,4,8,384]{3,2,1,0:T(8,128)(2,1)S(1)}, u32[]{:S(2)}, u32[]{:S(2)}) async-start(bf16[32,4,8,384]{3,2,1,0:T(8,128)(2,1)} %shard_map.146), calls=%async_computation.1 | async-start | bytes 1572864 | tf_op jit(solution)/shard_map/all_to_all | solution.py:563
  56.8 27.2 %all-to-all-start.2 = ((bf16[32,4,8,384]{3,2,1,0:T(8,128)(2,1)}), bf16[32,4,8,384]{3,2,1,0:T(8,128)(2,1)}, u32[]{:S(2)}, u32[]{:S(2)}) async-start(bf16[32,4,8,384]{3,2,1,0:T(8,128)(2,1)} %shard_map.145), calls=%async_computation.2 | async-start | bytes 1572864 | tf_op jit(solution)/shard_map/all_to_all | solution.py:563
  83.9 43.4 %all-to-all-start.3 = ((bf16[32,4,8,384]{3,2,1,0:T(8,128)(2,1)}), bf16[32,4,8,384]{3,2,1,0:T(8,128)(2,1)S(1)}, u32[]{:S(2)}, u32[]{:S(2)}) async-start(bf16[32,4,8,384]{3,2,1,0:T(8,128)(2,1)} %shard_map.148), calls=%async_computation.3 | async-start | bytes 1572864 | tf_op jit(solution)/shard_map/all_to_all | solution.py:563
  153.9 49.1 %all-to-all-start.4 = ((bf16[32,4,8,384]{3,2,1,0:T(8,128)(2,1)}), bf16[32,4,8,384]{3,2,1,0:T(8,128)(2,1)S(1)}, u32[]{:S(2)}, u32[]{:S(2)}) async-start(bf16[32,4,8,384]{3,2,1,0:T(8,128)(2,1)} %get-tuple-element.45), calls=%async_computation.4 | async-start | bytes 1572864 | tf_op jit(solution)/shard_map/all_to_all | solution.py:574
  162.2 15.4 %collective-permute-start.12 = (bf16[448,384]{1,0:T(8,128)(2,1)}, bf16[448,384]{1,0:T(8,128)(2,1)S(1)}, u32[]{:S(2)}, u32[]{:S(2)}) collective-permute-start(bf16[448,384]{1,0:T(8,128)(2,1)} %get-tuple-element.96), channel_id=1, source_target_pairs={{0,2},{1,3},{2,0},{3,1},{4,6},{5,7},{6,4},{7,5},{8,10},{9,11},{10,... | collective-permute-start | bytes 1032200 | tf_op jit(solution)/shard_map/ppermute | solution.py:487
  164.0 22.5 %collective-permute-start.14 = (bf16[448,384]{1,0:T(8,128)(2,1)}, bf16[448,384]{1,0:T(8,128)(2,1)S(1)}, u32[]{:S(2)}, u32[]{:S(2)}) collective-permute-start(bf16[448,384]{1,0:T(8,128)(2,1)} %get-tuple-element.97), channel_id=1, source_target_pairs={{0,6},{1,7},{2,4},{3,5},{4,2},{5,3},{6,0},{7,1},{8,14},{9,15},{10,... | collective-permute-start | bytes 1032200 | tf_op jit(solution)/shard_map/ppermute | solution.py:487
  165.5 21.6 %collective-permute-start.13 = (bf16[448,384]{1,0:T(8,128)(2,1)S(1)}, bf16[448,384]{1,0:T(8,128)(2,1)S(1)}, u32[]{:S(2)}, u32[]{:S(2)}) collective-permute-start(bf16[448,384]{1,0:T(8,128)(2,1)S(1)} %get-tuple-element.98), channel_id=1, source_target_pairs={{0,4},{1,5},{2,6},{3,7},{4,0},{5,1},{6,2},{7,3},{8,12},{9,13},{10,... | collective-permute-start | bytes 1032200 | tf_op jit(solution)/shard_map/ppermute | solution.py:487
  191.2 7.2 %collective-permute-start.16 = (bf16[112,384]{1,0:T(8,128)(2,1)S(1)}, bf16[112,384]{1,0:T(8,128)(2,1)S(1)}, u32[]{:S(2)}, u32[]{:S(2)}) collective-permute-start(bf16[112,384]{1,0:T(8,128)(2,1)S(1)} %get-tuple-element.116), channel_id=1, source_target_pairs={{0,16},{8,24},{16,0},{24,8},{1,17},{9,25},{17,1},{25,9},{2,18},{10... | collective-permute-start | bytes 258056 | tf_op jit(solution)/shard_map/ppermute | solution.py:487
  198.5 7.8 %collective-permute-start.20 = (bf16[112,384]{1,0:T(8,128)(2,1)S(1)}, bf16[112,384]{1,0:T(8,128)(2,1)S(1)}, u32[]{:S(2)}, u32[]{:S(2)}) collective-permute-start(bf16[112,384]{1,0:T(8,128)(2,1)S(1)} %fusion.18), channel_id=1, source_target_pairs={{0,24},{8,16},{16,8},{24,0},{1,25},{9,17},{17,9},{25,1},{2,26},{10... | collective-permute-start | bytes 258056 | tf_op jit(solution)/shard_map/ppermute | solution.py:487
  202.9 32.0 %all-to-all-start.5 = ((bf16[32,4,8,384]{3,2,1,0:T(8,128)(2,1)}), bf16[32,4,8,384]{3,2,1,0:T(8,128)(2,1)S(1)}, u32[]{:S(2)}, u32[]{:S(2)}) async-start(bf16[32,4,8,384]{3,2,1,0:T(8,128)(2,1)} %get-tuple-element.51), calls=%async_computation.5 | async-start | bytes 1572864 | tf_op jit(solution)/shard_map/all_to_all | solution.py:574
  208.3 18.7 %collective-permute-start.22 = (bf16[448,384]{1,0:T(8,128)(2,1)S(1)}, bf16[448,384]{1,0:T(8,128)(2,1)S(1)}, u32[]{:S(2)}, u32[]{:S(2)}) collective-permute-start(bf16[448,384]{1,0:T(8,128)(2,1)S(1)} %get-tuple-element.109), channel_id=1, source_target_pairs={{0,4},{1,5},{2,6},{3,7},{4,0},{5,1},{6,2},{7,3},{8,12},{9,13},{10,... | collective-permute-start | bytes 1032200 | tf_op jit(solution)/shard_map/ppermute | solution.py:487
  209.0 18.0 %collective-permute-start.21 = (bf16[448,384]{1,0:T(8,128)(2,1)S(1)}, bf16[448,384]{1,0:T(8,128)(2,1)S(1)}, u32[]{:S(2)}, u32[]{:S(2)}) collective-permute-start(bf16[448,384]{1,0:T(8,128)(2,1)S(1)} %get-tuple-element.109), channel_id=1, source_target_pairs={{0,2},{1,3},{2,0},{3,1},{4,6},{5,7},{6,4},{7,5},{8,10},{9,11},{10,... | collective-permute-start | bytes 1032200 | tf_op jit(solution)/shard_map/ppermute | solution.py:487
  209.9 23.3 %collective-permute-start.23 = (bf16[448,384]{1,0:T(8,128)(2,1)S(1)}, bf16[448,384]{1,0:T(8,128)(2,1)S(1)}, u32[]{:S(2)}, u32[]{:S(2)}) collective-permute-start(bf16[448,384]{1,0:T(8,128)(2,1)S(1)} %get-tuple-element.109), channel_id=1, source_target_pairs={{0,6},{1,7},{2,4},{3,5},{4,2},{5,3},{6,0},{7,1},{8,14},{9,15},{10,... | collective-permute-start | bytes 1032200 | tf_op jit(solution)/shard_map/ppermute | solution.py:487
  234.9 36.8 %collective-permute-start.24 = (bf16[1792,384]{1,0:T(8,128)(2,1)}, bf16[1792,384]{1,0:T(8,128)(2,1)}, u32[]{:S(2)}, u32[]{:S(2)}) collective-permute-start(bf16[1792,384]{1,0:T(8,128)(2,1)} %get-tuple-element.90), channel_id=1, source_target_pairs={{0,1},{1,0},{2,3},{3,2},{4,5},{5,4},{6,7},{7,6},{8,9},{9,8},{10,11... | collective-permute-start | bytes 4128776 | tf_op jit(solution)/shard_map/ppermute | solution.py:487
  255.0 12.1 %collective-permute-start.2 = (bf16[160,384]{1,0:T(8,128)(2,1)S(1)}, bf16[160,384]{1,0:T(8,128)(2,1)S(1)}, u32[]{:S(2)}, u32[]{:S(2)}) collective-permute-start(bf16[160,384]{1,0:T(8,128)(2,1)S(1)} %get-tuple-element.105), channel_id=1, source_target_pairs={{0,2},{1,3},{2,0},{3,1},{4,6},{5,7},{6,4},{7,5},{8,10},{9,11},{10,... | collective-permute-start | bytes 368648 | tf_op jit(solution)/shard_map/ppermute | solution.py:487
  255.9 11.2 %collective-permute-start.4 = (bf16[160,384]{1,0:T(8,128)(2,1)S(1)}, bf16[160,384]{1,0:T(8,128)(2,1)S(1)}, u32[]{:S(2)}, u32[]{:S(2)}) collective-permute-start(bf16[160,384]{1,0:T(8,128)(2,1)S(1)} %get-tuple-element.106), channel_id=1, source_target_pairs={{0,6},{1,7},{2,4},{3,5},{4,2},{5,3},{6,0},{7,1},{8,14},{9,15},{10,... | collective-permute-start | bytes 368648 | tf_op jit(solution)/shard_map/ppermute | solution.py:487
  257.4 9.8 %collective-permute-start.3 = (bf16[160,384]{1,0:T(8,128)(2,1)S(1)}, bf16[160,384]{1,0:T(8,128)(2,1)S(1)}, u32[]{:S(2)}, u32[]{:S(2)}) collective-permute-start(bf16[160,384]{1,0:T(8,128)(2,1)S(1)} %get-tuple-element.107), channel_id=1, source_target_pairs={{0,4},{1,5},{2,6},{3,7},{4,0},{5,1},{6,2},{7,3},{8,12},{9,13},{10,... | collective-permute-start | bytes 368648 | tf_op jit(solution)/shard_map/ppermute | solution.py:487
  258.6 45.3 %all-to-all-start.6 = ((bf16[32,4,8,384]{3,2,1,0:T(8,128)(2,1)}), bf16[32,4,8,384]{3,2,1,0:T(8,128)(2,1)S(1)}, u32[]{:S(2)}, u32[]{:S(2)}) async-start(bf16[32,4,8,384]{3,2,1,0:T(8,128)(2,1)} %get-tuple-element.58), calls=%async_computation.6 | async-start | bytes 1572864 | tf_op jit(solution)/shard_map/all_to_all | solution.py:574
  267.3 15.6 %collective-permute-start.7 = (bf16[160,384]{1,0:T(8,128)(2,1)S(1)}, bf16[160,384]{1,0:T(8,128)(2,1)S(1)}, u32[]{:S(2)}, u32[]{:S(2)}) collective-permute-start(bf16[160,384]{1,0:T(8,128)(2,1)S(1)} %fusion.15), channel_id=1, source_target_pairs={{0,24},{8,16},{16,8},{24,0},{1,25},{9,17},{17,9},{25,1},{2,26},{10... | collective-permute-start | bytes 368648 | tf_op jit(solution)/shard_map/ppermute | solution.py:487
  270.7 22.8 %collective-permute-start.6 = (bf16[160,384]{1,0:T(8,128)(2,1)S(1)}, bf16[160,384]{1,0:T(8,128)(2,1)S(1)}, u32[]{:S(2)}, u32[]{:S(2)}) collective-permute-start(bf16[160,384]{1,0:T(8,128)(2,1)S(1)} %fusion.15), channel_id=1, source_target_pairs={{0,16},{8,24},{16,0},{24,8},{1,17},{9,25},{17,1},{25,9},{2,18},{10... | collective-permute-start | bytes 368648 | tf_op jit(solution)/shard_map/ppermute | solution.py:487
  270.7 22.8 %collective-permute-start.5 = (bf16[160,384]{1,0:T(8,128)(2,1)S(1)}, bf16[160,384]{1,0:T(8,128)(2,1)S(1)}, u32[]{:S(2)}, u32[]{:S(2)}) collective-permute-start(bf16[160,384]{1,0:T(8,128)(2,1)S(1)} %fusion.15), channel_id=1, source_target_pairs={{0,8},{8,0},{16,24},{24,16},{1,9},{9,1},{17,25},{25,17},{2,10},{10... | collective-permute-start | bytes 368648 | tf_op jit(solution)/shard_map/ppermute | solution.py:487
  303.9 13.0 %collective-permute-start.11 = (bf16[640,384]{0,1:T(8,128)(2,1)}, bf16[640,384]{0,1:T(8,128)(2,1)}, u32[]{:S(2)}, u32[]{:S(2)}) collective-permute-start(bf16[640,384]{0,1:T(8,128)(2,1)} %pad_maximum_fusion.3), channel_id=1, source_target_pairs={{0,1},{1,0},{2,3},{3,2},{4,5},{5,4},{6,7},{7,6},{8,9},{9,8},{10,11... | collective-permute-start | bytes 1474568 | tf_op jit(solution)/shard_map/ppermute | solution.py:487
  304.0 24.0 %all-to-all-start.7 = ((bf16[32,4,8,384]{3,2,1,0:T(8,128)(2,1)}), bf16[32,4,8,384]{3,2,1,0:T(8,128)(2,1)}, u32[]{:S(2)}, u32[]{:S(2)}) async-start(bf16[32,4,8,384]{3,2,1,0:T(8,128)(2,1)} %get-tuple-element.68), calls=%async_computation.7 | async-start | bytes 1572864 | tf_op jit(solution)/shard_map/all_to_all | solution.py:574
  (25 other events, 189.1 us)

commit v2 on v1

--- a/solution.py
+++ b/solution.py
@@ -269,6 +269,34 @@
     @pl.when(step == pl.num_programs(0) - 1)
     def _():
         finish(acc_ref, grads_ref, grad_gain_ref)
+
+
+def prepare_kernel(
+    gain_one_ref, gain_two_ref, joint_ref, out_w_ref, up_ref, down_ref,
+    wide_one_ref, wide_two_ref, joint_t_ref, out_t_ref, up_t_ref, down_t_ref,
+):
+    tokens = wide_one_ref.shape[1]
+    for gain_ref, wide_ref in ((gain_one_ref, wide_one_ref), (gain_two_ref, wide_two_ref)):
+        wide_ref[...] = jnp.broadcast_to(gain_ref[...], (tokens, gain_ref.shape[1])).T
+    for weight_ref, turned_ref in (
+        (joint_ref, joint_t_ref),
+        (out_w_ref, out_t_ref),
+        (up_ref, up_t_ref),
+        (down_ref, down_t_ref),
+    ):
+        turned_ref[...] = weight_ref[...].T
+
+
+def prepare_call(gain_one, gain_two, joint, out_w, up, down, tokens):
+    width = gain_one.shape[0]
+    turned = [jax.ShapeDtypeStruct(w.shape[::-1], w.dtype) for w in (joint, out_w, up, down)]
+    wide = jax.ShapeDtypeStruct((width, tokens), F32)
+    return pl.pallas_call(
+        prepare_kernel,
+        out_shape=[wide, wide] + turned,
+        compiler_params=pltpu.CompilerParams(vmem_limit_bytes=60 << 20),
+        cost_estimate=cost(1e6, 16e6, 0),
+    )(gain_one.reshape(1, width), gain_two.reshape(1, width), joint, out_w, up, down)
 
 
 def pack_kernel(tile_ref, sends_ref, rows_ref):
@@ -585,19 +613,15 @@
             tile_rows, tile_cols, channels
         )
 
-    def spread(gain):
-        return jnp.broadcast_to(gain[:, None], (channels, tokens))
-
     arrived = []
     for k, tile in enumerate([activations] * chunks + [cotangent] * chunks):
         sends = pack(tile, k % chunks)
         arrived.append(send(sends, *arrived[-1:]))
     act, cot = arrived[:chunks], arrived[chunks:]
-    gain_one, gain_two = spread(first_gain), spread(second_gain)
-    joint_t = joint_weight.T
-    weights = (
-        output_weight.T, expand_weight.T, reduce_weight.T, reduce_weight, expand_weight, output_weight
+    gain_one, gain_two, joint_t, out_t, up_t, down_t = prepare_call(
+        first_gain, second_gain, joint_weight, output_weight, expand_weight, reduce_weight, tokens
     )
+    weights = (out_t, up_t, down_t, reduce_weight, expand_weight, output_weight)
     hidden_dim = expand_weight.shape[1]
     tail_rows, head_rows = 2 * hidden_dim + channels, 3 * channels
     unit = SUB * devices
@@ -614,25 +638,23 @@
         out_parts.append(give_back(tails[-1][0], *before))
         before = out_parts[-1:]
     steps = stages()
-    tail_sum = carried[0]
+    tail_sum = scatter_sum(carried[0], *steps[0])
     heads, in_parts, carried = [], [], ()
     for k in range(chunks):
         flat, triple, _, stat = fronts[k]
         _, grad_att, grad_mixed = tails[k][:3]
         spare = unit - head_rows % unit if k == chunks - 1 else 0
-        grad_mixed = tie(grad_mixed, out_parts[k], *((tail_sum,) if k else ()))
+        grad_mixed = tie(grad_mixed, out_parts[k])
         heads.append(
             back_call(flat, triple, stat, grad_mixed, grad_att, gain_one, joint_weight, cot[k], carried, spare)
         )
         carried = heads[-1][1:]
         in_parts.append(give_back(heads[-1][0], *before))
         before = in_parts[-1:]
-        if k < len(steps):
-            tail_sum = scatter_sum(tail_sum, *steps[k])
+        tail_sum = scatter_sum(tail_sum, *steps[k + 1])
     head_sum = carried[0]
     near, cols, rows = steps
     head_sum = scatter_sum(head_sum, *near)
-    tail_sum = scatter_sum(tail_sum, *rows)
     head_sum = scatter_sum(head_sum, *cols)
     tail_sum = collect(tail_sum, *rows)
     head_sum = share_sum(head_sum, *rows)

time: 334 us -> 333 us (level)
  local copies, waits for them, and re-layouts: 23.6 us -> 17.8 us
  Pallas kernels: 130 us -> 134 us
    unnamed x37 -> x27, local copies, waits for them, and re-layouts: 7.99 us -> 2.88 us
    pallas_call x0 -> x1, Pallas kernels: none -> 4.24 us  [prepare_call(): pl.pallas_call(prepare_kernel, out_shape=[wide, wide] + turned, compiler_...]
  transfers between devices with their start and end apart: 33 -> 33, of which waited for: 16 -> 16; matrix products, arithmetic and copies ran while one was open for 10% -> 9% of each run, Pallas kernels for 29% -> 31%
where the time goes in v2:
time: 333 us; the launch traced here: 331 us
  Pallas kernels  134 us (40%)
  waiting for transfers between devices  100 us (30%)
  starting transfers between devices  64.7 us (19%)
  local copies, waits for them, and re-layouts  17.8 us (5%)
  other arithmetic  13.2 us (4%)
    ppermute x25, waiting for transfers between devices, swap(): lax.ppermute(values, axis, [(i, i ^ offset) for i in range(lax.axis_size(...  59.5 us
    pallas_call x2, Pallas kernels, mlp_call(): pl.pallas_call(mlp_kernel, grid=(groups,), in_specs=[per_group((width, to...  47.1 us
    all_to_all x4, waiting for transfers between devices, send(): lax.all_to_all(tie(sends, *after), both, split_axis=0, concat_axis=0, til...  33.1 us
    pallas_call x2, Pallas kernels, back_call(): pl.pallas_call(back_kernel, grid=(groups,), in_specs=[per_group((width, t...  30.9 us
    ppermute x25, starting transfers between devices, swap(): lax.ppermute(values, axis, [(i, i ^ offset) for i in range(lax.axis_size(...  27.7 us
    pallas_call x2, Pallas kernels, attend_call(): pl.pallas_call(attend_kernel, grid=(groups,), in_specs=[pieces_spec(act),...  26.8 us
    all_to_all x4, starting transfers between devices, send(): lax.all_to_all(tie(sends, *after), both, split_axis=0, concat_axis=0, til...  20.6 us
    all_to_all x4, starting transfers between devices, give_back(): return lax.all_to_all(pieces, both, split_axis=0, concat_axis=0, tiled=True)  16.4 us
  transfers between devices with their start and end apart: 33, of which 16 were waited for; matrix products, arithmetic and copies ran while one was open for 9% of the time, Pallas kernels for 31%

profile of v2, /device:TPU:0, one launch (start us, length us, event | category | flops | bytes accessed | tf_op | source)
XLA Modules:
  0.0 331.0 jit_solution(9926152537515612792)
XLA Ops:
  4.6 7.3 %all-to-all-start = ((bf16[32,4,8,384]{3,2,1,0:T(8,128)(2,1)}), bf16[32,4,8,384]{3,2,1,0:T(8,128)(2,1)S(1)}, u32[]{:S(2)}, u32[]{:S(2)}) async-start(bf16[32,4,8,384]{3,2,1,0:T(8,128)(2,1)} %shard_map.143), calls=%async_computation | async-start | bytes 1572864 | tf_op jit(solution)/shard_map/all_to_all | solution.py:591
  12.0 4.0 %shard_map.147 = bf16[32,4,8,384]{3,2,1,0:T(8,128)(2,1)} custom-call(bf16[4,4,4,32,384]{4,3,2,1,0:T(8,128)(2,1)} %bitcast.98), custom_call_target="tpu_custom_call" | custom-call | flops 1000000 | bytes 1572864 | tf_op jit(solution)/shard_map/pallas_call | solution.py:351
  16.0 16.6 %all-to-all-done.act_ref = bf16[32,4,8,384]{3,2,1,0:T(8,128)(2,1)S(1)} async-done(((bf16[32,4,8,384]{3,2,1,0:T(8,128)(2,1)}), bf16[32,4,8,384]{3,2,1,0:T(8,128)(2,1)S(1)}, u32[]{:S(2)}, u32[]{:S(2)}) %all-to-all-start) | async-done | bytes 786464 | tf_op jit(solution)/shard_map/all_to_all | solution.py:591
  36.2 4.0 %shard_map.146 = bf16[32,4,8,384]{3,2,1,0:T(8,128)(2,1)} custom-call(bf16[4,4,4,32,384]{4,3,2,1,0:T(8,128)(2,1)} %bitcast.99), custom_call_target="tpu_custom_call" | custom-call | flops 1000000 | bytes 1572864 | tf_op jit(solution)/shard_map/pallas_call | solution.py:351
  40.2 16.6 %all-to-all-done.1.act_ref = bf16[32,4,8,384]{3,2,1,0:T(8,128)(2,1)S(1)} async-done(((bf16[32,4,8,384]{3,2,1,0:T(8,128)(2,1)}), bf16[32,4,8,384]{3,2,1,0:T(8,128)(2,1)S(1)}, u32[]{:S(2)}, u32[]{:S(2)}) %all-to-all-start.1) | async-done | bytes 786464 | tf_op jit(solution)/shard_map/all_to_all | solution.py:591
  61.6 4.0 %shard_map.149 = bf16[32,4,8,384]{3,2,1,0:T(8,128)(2,1)} custom-call(bf16[4,4,4,32,384]{4,3,2,1,0:T(8,128)(2,1)} %bitcast.100), custom_call_target="tpu_custom_call" | custom-call | flops 1000000 | bytes 1572864 | tf_op jit(solution)/shard_map/pallas_call | solution.py:351
  65.6 4.2 %shard_map.144 = (f32[384,256]{1,0:T(8,128)}, f32[384,256]{1,0:T(8,128)}, bf16[1152,384]{1,0:T(8,128)(2,1)}, bf16[384,384]{1,0:T(8,128)(2,1)}, bf16[1536,384]{1,0:T(8,128)(2,1)}, /*index=5*/bf16[384,1536]{1,0:T(8,128)(2,1)}) custom-call(f32[1,384]{1,0:T(1,128)} %reshape.62.gain_one_ref, f32[1,384]{1,0:T(1,128)} %reshape.63.gain_two_ref, ...), custom_call_target="tpu_custom_call" | custom-call | flops 1000000 | bytes 16000000 | tf_op jit(solution)/shard_map/pallas_call | solution.py:294
  69.8 13.4 %shard_map.145 = (bf16[4,384,256]{2,1,0:T(8,128)(2,1)}, bf16[4,1152,256]{2,1,0:T(8,128)(2,1)}, bf16[4,384,256]{2,1,0:T(8,128)(2,1)}, f32[4,16,256]{2,1,0:T(8,128)}) custom-call(bf16[32,4,8,384]{3,2,1,0:T(8,128)(2,1)} %copy-done.9, f32[384,256]{1,0:T(8,128)} %get-tuple-element.45.gain_ref, bf16[1152,384]{1,0:T(8,128)(2,1)} %get-tuple-element.46.joint_ref), custom_call_target="tpu_custom_call" | custom-call | flops 12000000000 | bytes 4718592 | tf_op jit(solution)/shard_map/pallas_call | solution.py:405
  83.2 6.0 %all-to-all-start.3 = ((bf16[32,4,8,384]{3,2,1,0:T(8,128)(2,1)}), bf16[32,4,8,384]{3,2,1,0:T(8,128)(2,1)S(1)}, u32[]{:S(2)}, u32[]{:S(2)}) async-start(bf16[32,4,8,384]{3,2,1,0:T(8,128)(2,1)} %shard_map.149), calls=%async_computation.3 | async-start | bytes 1572864 | tf_op jit(solution)/shard_map/all_to_all | solution.py:591
  89.3 13.4 %shard_map.150 = (bf16[4,384,256]{2,1,0:T(8,128)(2,1)}, bf16[4,1152,256]{2,1,0:T(8,128)(2,1)}, bf16[4,384,256]{2,1,0:T(8,128)(2,1)}, f32[4,16,256]{2,1,0:T(8,128)}) custom-call(bf16[32,4,8,384]{3,2,1,0:T(8,128)(2,1)} %copy-done.7, f32[384,256]{1,0:T(8,128)} %get-tuple-element.45.gain_ref, bf16[1152,384]{1,0:T(8,128)(2,1)} %get-tuple-element.46.joint_ref), custom_call_target="tpu_custom_call" | custom-call | flops 12000000000 | bytes 4718592 | tf_op jit(solution)/shard_map/pallas_call | solution.py:405
  102.7 23.2 %shard_map.148 = (bf16[32,4,8,384]{3,2,1,0:T(8,128)(2,1)}, f32[4,384,256]{2,1,0:T(8,128)}, bf16[4,384,256]{2,1,0:T(8,128)(2,1)}, f32[3456,384]{1,0:T(8,128)}, f32[384,128]{1,0:T(8,128)}) custom-call(bf16[4,384,256]{2,1,0:T(8,128)(2,1)} %get-tuple-element.47.flat_ref, bf16[4,384,256]{2,1,0:T(8,128)(2,1)} %get-tuple-element.48.mixed_ref, ...), custom_call_target="tpu_custom_call" | custom-call | flops 16000000000 | bytes 5505024 | tf_op jit(solution)/shard_map/pallas_call | solution.py:432
  126.8 24.0 %shard_map.151 = (bf16[32,4,8,384]{3,2,1,0:T(8,128)(2,1)}, f32[4,384,256]{2,1,0:T(8,128)}, bf16[4,384,256]{2,1,0:T(8,128)(2,1)}, bf16[3584,384]{1,0:T(8,128)(2,1)}, f32[384,128]{1,0:T(8,128)}) custom-call(bf16[4,384,256]{2,1,0:T(8,128)(2,1)} %get-tuple-element.58.flat_ref, bf16[4,384,256]{2,1,0:T(8,128)(2,1)} %get-tuple-element.59.mixed_ref, ...), custom_call_target="tpu_custom_call" | custom-call | flops 16000000000 | bytes 5505024 | tf_op jit(solution)/shard_map/pallas_call | solution.py:432
  152.4 5.7 %all-to-all-start.4 = ((bf16[32,4,8,384]{3,2,1,0:T(8,128)(2,1)}), bf16[32,4,8,384]{3,2,1,0:T(8,128)(2,1)S(1)}, u32[]{:S(2)}, u32[]{:S(2)}) async-start(bf16[32,4,8,384]{3,2,1,0:T(8,128)(2,1)} %get-tuple-element.57), calls=%async_computation.4 | async-start | bytes 1572864 | tf_op jit(solution)/shard_map/all_to_all | solution.py:602
  164.2 12.0 %collective-permute-done.12 = bf16[448,384]{1,0:T(8,128)(2,1)S(1)} collective-permute-done((bf16[448,384]{1,0:T(8,128)(2,1)}, bf16[448,384]{1,0:T(8,128)(2,1)S(1)}, u32[]{:S(2)}, u32[]{:S(2)}) %collective-permute-start.12) | collective-permute-done | bytes 344096 | tf_op jit(solution)/shard_map/ppermute | solution.py:515
  176.2 8.8 %collective-permute-done.14 = bf16[448,384]{1,0:T(8,128)(2,1)S(1)} collective-permute-done((bf16[448,384]{1,0:T(8,128)(2,1)}, bf16[448,384]{1,0:T(8,128)(2,1)S(1)}, u32[]{:S(2)}, u32[]{:S(2)}) %collective-permute-start.14) | collective-permute-done | bytes 344096 | tf_op jit(solution)/shard_map/ppermute | solution.py:515
  210.4 15.1 %shard_map.153 = (bf16[32,4,8,384]{3,2,1,0:T(8,128)(2,1)}, f32[1152,384]{1,0:T(8,128)}, f32[384,128]{1,0:T(8,128)}) custom-call(bf16[4,384,256]{2,1,0:T(8,128)(2,1)} %get-tuple-element.47.flat_ref, bf16[4,1152,256]{2,1,0:T(8,128)(2,1)} %get-tuple-element.64.triple_ref, f32[4,16,256]{2,1,0:T(8,128)} %get-tuple-element.65.stat_ref, ...), custom_call_target="tpu_custom_call" | custom-call | flops 24000000000 | bytes 7077888 | tf_op jit(solution)/shard_map/pallas_call | solution.py:470
  225.5 6.2 %collective-permute-done.23 = bf16[448,384]{1,0:T(8,128)(2,1)S(1)} collective-permute-done((bf16[448,384]{1,0:T(8,128)(2,1)S(1)}, bf16[448,384]{1,0:T(8,128)(2,1)S(1)}, u32[]{:S(2)}, u32[]{:S(2)}) %collective-permute-start.23) | collective-permute-done | bytes 344096 | tf_op jit(solution)/shard_map/ppermute | solution.py:515
  233.4 15.8 %shard_map.154 = (bf16[32,4,8,384]{3,2,1,0:T(8,128)(2,1)}, bf16[1280,384]{1,0:T(8,128)(2,1)}, f32[384,128]{1,0:T(8,128)}) custom-call(bf16[4,384,256]{2,1,0:T(8,128)(2,1)} %get-tuple-element.58.flat_ref, bf16[4,1152,256]{2,1,0:T(8,128)(2,1)} %get-tuple-element.71.triple_ref, f32[4,16,256]{2,1,0:T(8,128)} %get-tuple-element.72.stat_ref, ...), custom_call_target="tpu_custom_call" | custom-call | flops 24000000000 | bytes 7077888 | tf_op jit(solution)/shard_map/pallas_call | solution.py:470
  261.1 4.6 %shard_map.152 = bf16[4,4,4,32,384]{4,3,2,1,0:T(8,128)(2,1)} custom-call(bf16[32,4,8,384]{3,2,1,0:T(8,128)(2,1)} %copy-done, bf16[32,4,8,384]{3,2,1,0:T(8,128)(2,1)} %copy-done.2), custom_call_target="tpu_custom_call" | custom-call | flops 1000000 | bytes 3145728 | tf_op jit(solution)/shard_map/pallas_call | solution.py:369
  272.7 8.7 %collective-permute-done.6 = bf16[160,384]{1,0:T(8,128)(2,1)S(1)} collective-permute-done((bf16[160,384]{1,0:T(8,128)(2,1)S(1)}, bf16[160,384]{1,0:T(8,128)(2,1)S(1)}, u32[]{:S(2)}, u32[]{:S(2)}) %collective-permute-start.6) | collective-permute-done | bytes 122912 | tf_op jit(solution)/shard_map/ppermute | solution.py:515
  281.4 10.6 %collective-permute-done.5 = bf16[160,384]{1,0:T(8,128)(2,1)S(1)} collective-permute-done((bf16[160,384]{1,0:T(8,128)(2,1)S(1)}, bf16[160,384]{1,0:T(8,128)(2,1)S(1)}, u32[]{:S(2)}, u32[]{:S(2)}) %collective-permute-start.5) | collective-permute-done | bytes 122912 | tf_op jit(solution)/shard_map/ppermute | solution.py:515
  305.9 4.1 %fusion.21 = (f32[1536,384]{1,0:T(8,128)}, f32[384,1536]{0,1:T(8,128)S(1)}) fusion(f32[3584,384]{1,0:T(8,128)} %convert_multiply_fusion), kind=kLoop, calls=%fused_computation.70 | loop fusion | bytes 9437184 | tf_op jit(solution)/shard_map/slice | solution.py:675
  319.1 7.3 %all-to-all-done.7.refs_1_ = bf16[32,4,8,384]{3,2,1,0:T(8,128)(2,1)} async-done(((bf16[32,4,8,384]{3,2,1,0:T(8,128)(2,1)}), bf16[32,4,8,384]{3,2,1,0:T(8,128)(2,1)}, u32[]{:S(2)}, u32[]{:S(2)}) %all-to-all-start.7) | async-done | bytes 786464 | tf_op jit(solution)/shard_map/all_to_all | solution.py:602
  326.4 4.6 %shard_map.155 = bf16[4,4,4,32,384]{4,3,2,1,0:T(8,128)(2,1)} custom-call(bf16[32,4,8,384]{3,2,1,0:T(8,128)(2,1)} %copy-done.1, bf16[32,4,8,384]{3,2,1,0:T(8,128)(2,1)} %all-to-all-done.7.refs_1_), custom_call_target="tpu_custom_call" | custom-call | flops 1000000 | bytes 3145728 | tf_op jit(solution)/shard_map/pallas_call | solution.py:369
  (118 shorter events, 90.0 us)
Async XLA Ops:
  4.6 27.9 %all-to-all-start = ((bf16[32,4,8,384]{3,2,1,0:T(8,128)(2,1)}), bf16[32,4,8,384]{3,2,1,0:T(8,128)(2,1)S(1)}, u32[]{:S(2)}, u32[]{:S(2)}) async-start(bf16[32,4,8,384]{3,2,1,0:T(8,128)(2,1)} %shard_map.143), calls=%async_computation | async-start | bytes 1572864 | tf_op jit(solution)/shard_map/all_to_all | solution.py:591
  32.6 24.2 %all-to-all-start.1 = ((bf16[32,4,8,384]{3,2,1,0:T(8,128)(2,1)}), bf16[32,4,8,384]{3,2,1,0:T(8,128)(2,1)S(1)}, u32[]{:S(2)}, u32[]{:S(2)}) async-start(bf16[32,4,8,384]{3,2,1,0:T(8,128)(2,1)} %shard_map.147), calls=%async_computation.1 | async-start | bytes 1572864 | tf_op jit(solution)/shard_map/all_to_all | solution.py:591
  56.8 26.4 %all-to-all-start.2 = ((bf16[32,4,8,384]{3,2,1,0:T(8,128)(2,1)}), bf16[32,4,8,384]{3,2,1,0:T(8,128)(2,1)S(1)}, u32[]{:S(2)}, u32[]{:S(2)}) async-start(bf16[32,4,8,384]{3,2,1,0:T(8,128)(2,1)} %shard_map.146), calls=%async_computation.2 | async-start | bytes 1572864 | tf_op jit(solution)/shard_map/all_to_all | solution.py:591
  83.2 42.6 %all-to-all-start.3 = ((bf16[32,4,8,384]{3,2,1,0:T(8,128)(2,1)}), bf16[32,4,8,384]{3,2,1,0:T(8,128)(2,1)S(1)}, u32[]{:S(2)}, u32[]{:S(2)}) async-start(bf16[32,4,8,384]{3,2,1,0:T(8,128)(2,1)} %shard_map.149), calls=%async_computation.3 | async-start | bytes 1572864 | tf_op jit(solution)/shard_map/all_to_all | solution.py:591
  152.4 49.1 %all-to-all-start.4 = ((bf16[32,4,8,384]{3,2,1,0:T(8,128)(2,1)}), bf16[32,4,8,384]{3,2,1,0:T(8,128)(2,1)S(1)}, u32[]{:S(2)}, u32[]{:S(2)}) async-start(bf16[32,4,8,384]{3,2,1,0:T(8,128)(2,1)} %get-tuple-element.57), calls=%async_computation.4 | async-start | bytes 1572864 | tf_op jit(solution)/shard_map/all_to_all | solution.py:602
  160.7 15.5 %collective-permute-start.12 = (bf16[448,384]{1,0:T(8,128)(2,1)}, bf16[448,384]{1,0:T(8,128)(2,1)S(1)}, u32[]{:S(2)}, u32[]{:S(2)}) collective-permute-start(bf16[448,384]{1,0:T(8,128)(2,1)} %get-tuple-element.108), channel_id=1, source_target_pairs={{0,2},{1,3},{2,0},{3,1},{4,6},{5,7},{6,4},{7,5},{8,10},{9,11},{10,... | collective-permute-start | bytes 1032200 | tf_op jit(solution)/shard_map/ppermute | solution.py:515
  162.5 22.5 %collective-permute-start.14 = (bf16[448,384]{1,0:T(8,128)(2,1)}, bf16[448,384]{1,0:T(8,128)(2,1)S(1)}, u32[]{:S(2)}, u32[]{:S(2)}) collective-permute-start(bf16[448,384]{1,0:T(8,128)(2,1)} %get-tuple-element.109), channel_id=1, source_target_pairs={{0,6},{1,7},{2,4},{3,5},{4,2},{5,3},{6,0},{7,1},{8,14},{9,15},{10,... | collective-permute-start | bytes 1032200 | tf_op jit(solution)/shard_map/ppermute | solution.py:515
  164.0 21.6 %collective-permute-start.13 = (bf16[448,384]{1,0:T(8,128)(2,1)S(1)}, bf16[448,384]{1,0:T(8,128)(2,1)S(1)}, u32[]{:S(2)}, u32[]{:S(2)}) collective-permute-start(bf16[448,384]{1,0:T(8,128)(2,1)S(1)} %get-tuple-element.110), channel_id=1, source_target_pairs={{0,4},{1,5},{2,6},{3,7},{4,0},{5,1},{6,2},{7,3},{8,12},{9,13},{10,... | collective-permute-start | bytes 1032200 | tf_op jit(solution)/shard_map/ppermute | solution.py:515
  189.7 7.2 %collective-permute-start.16 = (bf16[112,384]{1,0:T(8,128)(2,1)S(1)}, bf16[112,384]{1,0:T(8,128)(2,1)S(1)}, u32[]{:S(2)}, u32[]{:S(2)}) collective-permute-start(bf16[112,384]{1,0:T(8,128)(2,1)S(1)} %get-tuple-element.128), channel_id=1, source_target_pairs={{0,16},{8,24},{16,0},{24,8},{1,17},{9,25},{17,1},{25,9},{2,18},{10... | collective-permute-start | bytes 258056 | tf_op jit(solution)/shard_map/ppermute | solution.py:515
  197.0 7.8 %collective-permute-start.20 = (bf16[112,384]{1,0:T(8,128)(2,1)S(1)}, bf16[112,384]{1,0:T(8,128)(2,1)S(1)}, u32[]{:S(2)}, u32[]{:S(2)}) collective-permute-start(bf16[112,384]{1,0:T(8,128)(2,1)S(1)} %fusion.18), channel_id=1, source_target_pairs={{0,24},{8,16},{16,8},{24,0},{1,25},{9,17},{17,9},{25,1},{2,26},{10... | collective-permute-start | bytes 258056 | tf_op jit(solution)/shard_map/ppermute | solution.py:515
  201.4 32.0 %all-to-all-start.5 = ((bf16[32,4,8,384]{3,2,1,0:T(8,128)(2,1)}), bf16[32,4,8,384]{3,2,1,0:T(8,128)(2,1)S(1)}, u32[]{:S(2)}, u32[]{:S(2)}) async-start(bf16[32,4,8,384]{3,2,1,0:T(8,128)(2,1)} %get-tuple-element.63), calls=%async_computation.5 | async-start | bytes 1572864 | tf_op jit(solution)/shard_map/all_to_all | solution.py:602
  206.8 18.7 %collective-permute-start.22 = (bf16[448,384]{1,0:T(8,128)(2,1)S(1)}, bf16[448,384]{1,0:T(8,128)(2,1)S(1)}, u32[]{:S(2)}, u32[]{:S(2)}) collective-permute-start(bf16[448,384]{1,0:T(8,128)(2,1)S(1)} %get-tuple-element.121), channel_id=1, source_target_pairs={{0,4},{1,5},{2,6},{3,7},{4,0},{5,1},{6,2},{7,3},{8,12},{9,13},{10,... | collective-permute-start | bytes 1032200 | tf_op jit(solution)/shard_map/ppermute | solution.py:515
  207.5 18.0 %collective-permute-start.21 = (bf16[448,384]{1,0:T(8,128)(2,1)S(1)}, bf16[448,384]{1,0:T(8,128)(2,1)S(1)}, u32[]{:S(2)}, u32[]{:S(2)}) collective-permute-start(bf16[448,384]{1,0:T(8,128)(2,1)S(1)} %get-tuple-element.121), channel_id=1, source_target_pairs={{0,2},{1,3},{2,0},{3,1},{4,6},{5,7},{6,4},{7,5},{8,10},{9,11},{10,... | collective-permute-start | bytes 1032200 | tf_op jit(solution)/shard_map/ppermute | solution.py:515
  208.4 23.3 %collective-permute-start.23 = (bf16[448,384]{1,0:T(8,128)(2,1)S(1)}, bf16[448,384]{1,0:T(8,128)(2,1)S(1)}, u32[]{:S(2)}, u32[]{:S(2)}) collective-permute-start(bf16[448,384]{1,0:T(8,128)(2,1)S(1)} %get-tuple-element.121), channel_id=1, source_target_pairs={{0,6},{1,7},{2,4},{3,5},{4,2},{5,3},{6,0},{7,1},{8,14},{9,15},{10,... | collective-permute-start | bytes 1032200 | tf_op jit(solution)/shard_map/ppermute | solution.py:515
  233.4 36.8 %collective-permute-start.24 = (bf16[1792,384]{1,0:T(8,128)(2,1)}, bf16[1792,384]{1,0:T(8,128)(2,1)}, u32[]{:S(2)}, u32[]{:S(2)}) collective-permute-start(bf16[1792,384]{1,0:T(8,128)(2,1)} %get-tuple-element.102), channel_id=1, source_target_pairs={{0,1},{1,0},{2,3},{3,2},{4,5},{5,4},{6,7},{7,6},{8,9},{9,8},{10,11... | collective-permute-start | bytes 4128776 | tf_op jit(solution)/shard_map/ppermute | solution.py:515
  253.6 12.1 %collective-permute-start.1 = (bf16[160,384]{1,0:T(8,128)(2,1)S(1)}, bf16[160,384]{1,0:T(8,128)(2,1)S(1)}, u32[]{:S(2)}, u32[]{:S(2)}) collective-permute-start(bf16[160,384]{1,0:T(8,128)(2,1)S(1)} %get-tuple-element.117), channel_id=1, source_target_pairs={{0,2},{1,3},{2,0},{3,1},{4,6},{5,7},{6,4},{7,5},{8,10},{9,11},{10,... | collective-permute-start | bytes 368648 | tf_op jit(solution)/shard_map/ppermute | solution.py:515
  254.4 11.2 %collective-permute-start.3 = (bf16[160,384]{1,0:T(8,128)(2,1)S(1)}, bf16[160,384]{1,0:T(8,128)(2,1)S(1)}, u32[]{:S(2)}, u32[]{:S(2)}) collective-permute-start(bf16[160,384]{1,0:T(8,128)(2,1)S(1)} %get-tuple-element.118), channel_id=1, source_target_pairs={{0,6},{1,7},{2,4},{3,5},{4,2},{5,3},{6,0},{7,1},{8,14},{9,15},{10,... | collective-permute-start | bytes 368648 | tf_op jit(solution)/shard_map/ppermute | solution.py:515
  255.9 9.8 %collective-permute-start.2 = (bf16[160,384]{1,0:T(8,128)(2,1)S(1)}, bf16[160,384]{1,0:T(8,128)(2,1)S(1)}, u32[]{:S(2)}, u32[]{:S(2)}) collective-permute-start(bf16[160,384]{1,0:T(8,128)(2,1)S(1)} %get-tuple-element.119), channel_id=1, source_target_pairs={{0,4},{1,5},{2,6},{3,7},{4,0},{5,1},{6,2},{7,3},{8,12},{9,13},{10,... | collective-permute-start | bytes 368648 | tf_op jit(solution)/shard_map/ppermute | solution.py:515
  257.1 45.3 %all-to-all-start.6 = ((bf16[32,4,8,384]{3,2,1,0:T(8,128)(2,1)}), bf16[32,4,8,384]{3,2,1,0:T(8,128)(2,1)S(1)}, u32[]{:S(2)}, u32[]{:S(2)}) async-start(bf16[32,4,8,384]{3,2,1,0:T(8,128)(2,1)} %get-tuple-element.70), calls=%async_computation.6 | async-start | bytes 1572864 | tf_op jit(solution)/shard_map/all_to_all | solution.py:602
  265.8 15.6 %collective-permute-start.6 = (bf16[160,384]{1,0:T(8,128)(2,1)S(1)}, bf16[160,384]{1,0:T(8,128)(2,1)S(1)}, u32[]{:S(2)}, u32[]{:S(2)}) collective-permute-start(bf16[160,384]{1,0:T(8,128)(2,1)S(1)} %fusion.15), channel_id=1, source_target_pairs={{0,24},{8,16},{16,8},{24,0},{1,25},{9,17},{17,9},{25,1},{2,26},{10... | collective-permute-start | bytes 368648 | tf_op jit(solution)/shard_map/ppermute | solution.py:515
  269.2 22.8 %collective-permute-start.5 = (bf16[160,384]{1,0:T(8,128)(2,1)S(1)}, bf16[160,384]{1,0:T(8,128)(2,1)S(1)}, u32[]{:S(2)}, u32[]{:S(2)}) collective-permute-start(bf16[160,384]{1,0:T(8,128)(2,1)S(1)} %fusion.15), channel_id=1, source_target_pairs={{0,16},{8,24},{16,0},{24,8},{1,17},{9,25},{17,1},{25,9},{2,18},{10... | collective-permute-start | bytes 368648 | tf_op jit(solution)/shard_map/ppermute | solution.py:515
  269.2 22.8 %collective-permute-start.4 = (bf16[160,384]{1,0:T(8,128)(2,1)S(1)}, bf16[160,384]{1,0:T(8,128)(2,1)S(1)}, u32[]{:S(2)}, u32[]{:S(2)}) collective-permute-start(bf16[160,384]{1,0:T(8,128)(2,1)S(1)} %fusion.15), channel_id=1, source_target_pairs={{0,8},{8,0},{16,24},{24,16},{1,9},{9,1},{17,25},{25,17},{2,10},{10... | collective-permute-start | bytes 368648 | tf_op jit(solution)/shard_map/ppermute | solution.py:515
  302.4 13.0 %collective-permute-start.10 = (bf16[640,384]{0,1:T(8,128)(2,1)}, bf16[640,384]{0,1:T(8,128)(2,1)}, u32[]{:S(2)}, u32[]{:S(2)}) collective-permute-start(bf16[640,384]{0,1:T(8,128)(2,1)} %pad_maximum_fusion.3), channel_id=1, source_target_pairs={{0,1},{1,0},{2,3},{3,2},{4,5},{5,4},{6,7},{7,6},{8,9},{9,8},{10,11... | collective-permute-start | bytes 1474568 | tf_op jit(solution)/shard_map/ppermute | solution.py:515
  302.5 24.0 %all-to-all-start.7 = ((bf16[32,4,8,384]{3,2,1,0:T(8,128)(2,1)}), bf16[32,4,8,384]{3,2,1,0:T(8,128)(2,1)}, u32[]{:S(2)}, u32[]{:S(2)}) async-start(bf16[32,4,8,384]{3,2,1,0:T(8,128)(2,1)} %get-tuple-element.79), calls=%async_computation.7 | async-start | bytes 1572864 | tf_op jit(solution)/shard_map/all_to_all | solution.py:602
  (22 other events, 174.4 us)

commit v3 on v2

--- a/solution.py
+++ b/solution.py
@@ -108,7 +108,10 @@
     return [slice(start, start + 128) for start in range(0, count, 128)]
 
 
-def attend_kernel(act_ref, gain_ref, joint_ref, flat_ref, triple_ref, mixed_ref, stat_ref, score_ref):
+def attend_kernel(
+    act_ref, gain_ref, joint_ref, out_t_ref,
+    flat_ref, triple_ref, mixed_ref, stat_ref, attended_ref, score_ref,
+):
     width, tokens = gain_ref.shape
     head = width // HEADS
     factor = head ** (-0.5) * LOG2E
@@ -136,10 +139,11 @@
             stat_ref[0, h : h + 1, lanes] = top * factor + jnp.log2(total)
             weights = (weights * (1.0 / total)).astype(BF)
             mixed_ref[0, h * head : (h + 1) * head, lanes] = nn(values, weights).astype(BF)
+    attended_ref[0] = flat_ref[0].astype(F32) + nn(out_t_ref[...], mixed_ref[0])
 
 
 def mlp_kernel(
-    flat_ref, mixed_ref, cot_ref, gain_ref, out_t_ref, up_t_ref, down_t_ref, down_ref, up_ref, out_w_ref,
+    attended_ref, mixed_ref, cot_ref, gain_ref, up_t_ref, down_t_ref, down_ref, up_ref, out_w_ref,
     *rest,
 ):
     carried = rest[:-13]
@@ -157,7 +161,7 @@
     cot_t = cot_rows.T
     cot_tb = cot_t.astype(BF)
     mixed = mixed_ref[0]
-    attended = flat_ref[0].astype(F32) + nn(out_t_ref[...], mixed)
+    attended = attended_ref[0]
     normed, inv_std = normalize(attended)
     gain = gain_ref[...]
     scaled = (normed * gain).astype(BF)
@@ -399,35 +403,37 @@
     return pl.CostEstimate(flops=int(flops), bytes_accessed=int(bytes_moved), transcendentals=int(exps))
 
 
-def attend_call(act, gain, joint_t):
+def attend_call(act, gain, joint_t, out_t):
     pieces, groups, sub, width = act.shape
     tokens = pieces * sub
     return pl.pallas_call(
         attend_kernel,
         grid=(groups,),
-        in_specs=[pieces_spec(act), whole(gain), whole(joint_t)],
+        in_specs=[pieces_spec(act), whole(gain), whole(joint_t), whole(out_t)],
         out_specs=[
             per_group((width, tokens)),
             per_group((3 * width, tokens)),
             per_group((width, tokens)),
             per_group((16, tokens)),
+            per_group((width, tokens)),
         ],
         out_shape=[
             jax.ShapeDtypeStruct((groups, width, tokens), BF),
             jax.ShapeDtypeStruct((groups, 3 * width, tokens), BF),
             jax.ShapeDtypeStruct((groups, width, tokens), BF),
             jax.ShapeDtypeStruct((groups, 16, tokens), F32),
+            jax.ShapeDtypeStruct((groups, width, tokens), F32),
         ],
         scratch_shapes=[pltpu.VMEM((2, tokens, tokens), F32)],
         compiler_params=params(),
         cost_estimate=cost(3e9 * groups, 12 * groups * tokens * width, 0),
-    )(act, gain, joint_t)
-
-
-def mlp_call(flat, mixed, cot, gain, weights, carried, spare):
+    )(act, gain, joint_t, out_t)
+
+
+def mlp_call(attended, mixed, cot, gain, weights, carried, spare):
     pieces, groups, sub, width = cot.shape
     tokens = pieces * sub
-    hidden_dim = weights[1].shape[0]
+    hidden_dim = weights[0].shape[0]
     rows = 2 * hidden_dim + width
     return pl.pallas_call(
         mlp_kernel,
@@ -460,7 +466,7 @@
         ],
         compiler_params=params(),
         cost_estimate=cost(4e9 * groups, 14 * groups * tokens * width, 0),
-    )(flat, mixed, cot, gain, *weights, *carried)
+    )(attended, mixed, cot, gain, *weights, *carried)
 
 
 def back_call(flat, triple, stat, grad_mixed, grad_att, gain, joint, like, carried, spare):
@@ -621,19 +627,19 @@
     gain_one, gain_two, joint_t, out_t, up_t, down_t = prepare_call(
         first_gain, second_gain, joint_weight, output_weight, expand_weight, reduce_weight, tokens
     )
-    weights = (out_t, up_t, down_t, reduce_weight, expand_weight, output_weight)
+    weights = (up_t, down_t, reduce_weight, expand_weight, output_weight)
     hidden_dim = expand_weight.shape[1]
     tail_rows, head_rows = 2 * hidden_dim + channels, 3 * channels
     unit = SUB * devices
     fronts = []
     for k in range(chunks):
-        fronts.append(attend_call(act[k], gain_one, joint_t))
+        fronts.append(attend_call(act[k], gain_one, joint_t, out_t))
     tails, out_parts, carried = [], [], ()
     before = cot[-1:]
     for k in range(chunks):
-        flat, _, mixed, _ = fronts[k]
+        _, _, mixed, _, attended = fronts[k]
         spare = unit - tail_rows % unit if k == chunks - 1 else 0
-        tails.append(mlp_call(flat, mixed, cot[k], gain_two, weights, carried, spare))
+        tails.append(mlp_call(attended, mixed, cot[k], gain_two, weights, carried, spare))
         carried = tails[-1][3:]
         out_parts.append(give_back(tails[-1][0], *before))
         before = out_parts[-1:]
@@ -641,7 +647,7 @@
     tail_sum = scatter_sum(carried[0], *steps[0])
     heads, in_parts, carried = [], [], ()
     for k in range(chunks):
-        flat, triple, _, stat = fronts[k]
+        flat, triple, _, stat, _ = fronts[k]
         _, grad_att, grad_mixed = tails[k][:3]
         spare = unit - head_rows % unit if k == chunks - 1 else 0
         grad_mixed = tie(grad_mixed, out_parts[k])

time: 333 us -> 332 us (level)
  no operation moved by 1% of the time
where the time goes in v3:
time: 332 us; the launch traced here: 331 us
  Pallas kernels  134 us (40%)
  waiting for transfers between devices  99.8 us (30%)
  starting transfers between devices  64.9 us (20%)
  local copies, waits for them, and re-layouts  17.8 us (5%)
  other arithmetic  13.2 us (4%)
    ppermute x25, waiting for transfers between devices, swap(): lax.ppermute(values, axis, [(i, i ^ offset) for i in range(lax.axis_size(...  59.3 us
    pallas_call x2, Pallas kernels, mlp_call(): pl.pallas_call(mlp_kernel, grid=(groups,), in_specs=[per_group((width, to...  44.7 us
    all_to_all x4, waiting for transfers between devices, send(): lax.all_to_all(tie(sends, *after), both, split_axis=0, concat_axis=0, til...  33.1 us
    pallas_call x2, Pallas kernels, back_call(): pl.pallas_call(back_kernel, grid=(groups,), in_specs=[per_group((width, t...  30.9 us
    pallas_call x2, Pallas kernels, attend_call(): pl.pallas_call(attend_kernel, grid=(groups,), in_specs=[pieces_spec(act),...  28.9 us
    ppermute x25, starting transfers between devices, swap(): lax.ppermute(values, axis, [(i, i ^ offset) for i in range(lax.axis_size(...  27.7 us
    all_to_all x4, starting transfers between devices, send(): lax.all_to_all(tie(sends, *after), both, split_axis=0, concat_axis=0, til...  20.6 us
    all_to_all x4, starting transfers between devices, give_back(): return lax.all_to_all(pieces, both, split_axis=0, concat_axis=0, tiled=True)  16.6 us
  transfers between devices with their start and end apart: 33, of which 16 were waited for; matrix products, arithmetic and copies ran while one was open for 9% of the time, Pallas kernels for 31%

profile of v3, /device:TPU:0, one launch (start us, length us, event | category | flops | bytes accessed | tf_op | source)
XLA Modules:
  0.0 330.6 jit_solution(16706351471624740467)
XLA Ops:
  0.6 4.0 %shard_map.143 = bf16[32,4,8,384]{3,2,1,0:T(8,128)(2,1)} custom-call(bf16[4,4,4,32,384]{4,3,2,1,0:T(8,128)(2,1)} %bitcast.97), custom_call_target="tpu_custom_call" | custom-call | flops 1000000 | bytes 1572864 | tf_op jit(solution)/shard_map/pallas_call | solution.py:355
  4.6 7.3 %all-to-all-start = ((bf16[32,4,8,384]{3,2,1,0:T(8,128)(2,1)}), bf16[32,4,8,384]{3,2,1,0:T(8,128)(2,1)S(1)}, u32[]{:S(2)}, u32[]{:S(2)}) async-start(bf16[32,4,8,384]{3,2,1,0:T(8,128)(2,1)} %shard_map.143), calls=%async_computation | async-start | bytes 1572864 | tf_op jit(solution)/shard_map/all_to_all | solution.py:597
  12.0 4.0 %shard_map.147 = bf16[32,4,8,384]{3,2,1,0:T(8,128)(2,1)} custom-call(bf16[4,4,4,32,384]{4,3,2,1,0:T(8,128)(2,1)} %bitcast.98), custom_call_target="tpu_custom_call" | custom-call | flops 1000000 | bytes 1572864 | tf_op jit(solution)/shard_map/pallas_call | solution.py:355
  16.0 16.6 %all-to-all-done.act_ref = bf16[32,4,8,384]{3,2,1,0:T(8,128)(2,1)S(1)} async-done(((bf16[32,4,8,384]{3,2,1,0:T(8,128)(2,1)}), bf16[32,4,8,384]{3,2,1,0:T(8,128)(2,1)S(1)}, u32[]{:S(2)}, u32[]{:S(2)}) %all-to-all-start) | async-done | bytes 786464 | tf_op jit(solution)/shard_map/all_to_all | solution.py:597
  36.2 4.0 %shard_map.146 = bf16[32,4,8,384]{3,2,1,0:T(8,128)(2,1)} custom-call(bf16[4,4,4,32,384]{4,3,2,1,0:T(8,128)(2,1)} %bitcast.99), custom_call_target="tpu_custom_call" | custom-call | flops 1000000 | bytes 1572864 | tf_op jit(solution)/shard_map/pallas_call | solution.py:355
  40.2 16.6 %all-to-all-done.1.act_ref = bf16[32,4,8,384]{3,2,1,0:T(8,128)(2,1)S(1)} async-done(((bf16[32,4,8,384]{3,2,1,0:T(8,128)(2,1)}), bf16[32,4,8,384]{3,2,1,0:T(8,128)(2,1)S(1)}, u32[]{:S(2)}, u32[]{:S(2)}) %all-to-all-start.1) | async-done | bytes 786464 | tf_op jit(solution)/shard_map/all_to_all | solution.py:597
  65.6 4.2 %shard_map.144 = (f32[384,256]{1,0:T(8,128)}, f32[384,256]{1,0:T(8,128)}, bf16[1152,384]{1,0:T(8,128)(2,1)}, bf16[384,384]{1,0:T(8,128)(2,1)}, bf16[1536,384]{1,0:T(8,128)(2,1)}, /*index=5*/bf16[384,1536]{1,0:T(8,128)(2,1)}) custom-call(f32[1,384]{1,0:T(1,128)} %reshape.62.gain_one_ref, f32[1,384]{1,0:T(1,128)} %reshape.63.gain_two_ref, ...), custom_call_target="tpu_custom_call" | custom-call | flops 1000000 | bytes 16000000 | tf_op jit(solution)/shard_map/pallas_call | solution.py:298
  69.8 14.5 %shard_map.145 = (bf16[4,384,256]{2,1,0:T(8,128)(2,1)}, bf16[4,1152,256]{2,1,0:T(8,128)(2,1)}, bf16[4,384,256]{2,1,0:T(8,128)(2,1)}, f32[4,16,256]{2,1,0:T(8,128)}, f32[4,384,256]{2,1,0:T(8,128)}) custom-call(bf16[32,4,8,384]{3,2,1,0:T(8,128)(2,1)} %copy-done.9, f32[384,256]{1,0:T(8,128)} %get-tuple-element.47.gain_ref, ...), custom_call_target="tpu_custom_call" | custom-call | flops 12000000000 | bytes 4718592 | tf_op jit(solution)/shard_map/pallas_call | solution.py:409
  84.3 6.0 %all-to-all-start.3 = ((bf16[32,4,8,384]{3,2,1,0:T(8,128)(2,1)}), bf16[32,4,8,384]{3,2,1,0:T(8,128)(2,1)S(1)}, u32[]{:S(2)}, u32[]{:S(2)}) async-start(bf16[32,4,8,384]{3,2,1,0:T(8,128)(2,1)} %shard_map.149), calls=%async_computation.3 | async-start | bytes 1572864 | tf_op jit(solution)/shard_map/all_to_all | solution.py:597
  90.3 14.5 %shard_map.150 = (bf16[4,384,256]{2,1,0:T(8,128)(2,1)}, bf16[4,1152,256]{2,1,0:T(8,128)(2,1)}, bf16[4,384,256]{2,1,0:T(8,128)(2,1)}, f32[4,16,256]{2,1,0:T(8,128)}, f32[4,384,256]{2,1,0:T(8,128)}) custom-call(bf16[32,4,8,384]{3,2,1,0:T(8,128)(2,1)} %copy-done.7, f32[384,256]{1,0:T(8,128)} %get-tuple-element.47.gain_ref, ...), custom_call_target="tpu_custom_call" | custom-call | flops 12000000000 | bytes 4718592 | tf_op jit(solution)/shard_map/pallas_call | solution.py:409
  104.8 21.9 %shard_map.148 = (bf16[32,4,8,384]{3,2,1,0:T(8,128)(2,1)}, f32[4,384,256]{2,1,0:T(8,128)}, bf16[4,384,256]{2,1,0:T(8,128)(2,1)}, f32[3456,384]{1,0:T(8,128)}, f32[384,128]{1,0:T(8,128)}) custom-call(f32[4,384,256]{2,1,0:T(8,128)} %get-tuple-element.50.attended_ref, bf16[4,384,256]{2,1,0:T(8,128)(2,1)} %get-tuple-element.51.mixed_ref, ...), custom_call_target="tpu_custom_call" | custom-call | flops 16000000000 | bytes 5505024 | tf_op jit(solution)/shard_map/pallas_call | solution.py:438
  127.7 22.7 %shard_map.151 = (bf16[32,4,8,384]{3,2,1,0:T(8,128)(2,1)}, f32[4,384,256]{2,1,0:T(8,128)}, bf16[4,384,256]{2,1,0:T(8,128)(2,1)}, bf16[3584,384]{1,0:T(8,128)(2,1)}, f32[384,128]{1,0:T(8,128)}) custom-call(f32[4,384,256]{2,1,0:T(8,128)} %get-tuple-element.60.attended_ref, bf16[4,384,256]{2,1,0:T(8,128)(2,1)} %get-tuple-element.61.mixed_ref, ...), custom_call_target="tpu_custom_call" | custom-call | flops 16000000000 | bytes 5505024 | tf_op jit(solution)/shard_map/pallas_call | solution.py:438
  152.0 5.9 %all-to-all-start.4 = ((bf16[32,4,8,384]{3,2,1,0:T(8,128)(2,1)}), bf16[32,4,8,384]{3,2,1,0:T(8,128)(2,1)S(1)}, u32[]{:S(2)}, u32[]{:S(2)}) async-start(bf16[32,4,8,384]{3,2,1,0:T(8,128)(2,1)} %get-tuple-element.59), calls=%async_computation.4 | async-start | bytes 1572864 | tf_op jit(solution)/shard_map/all_to_all | solution.py:608
  164.1 11.8 %collective-permute-done.12 = bf16[448,384]{1,0:T(8,128)(2,1)S(1)} collective-permute-done((bf16[448,384]{1,0:T(8,128)(2,1)}, bf16[448,384]{1,0:T(8,128)(2,1)S(1)}, u32[]{:S(2)}, u32[]{:S(2)}) %collective-permute-start.12) | collective-permute-done | bytes 344096 | tf_op jit(solution)/shard_map/ppermute | solution.py:521
  175.9 8.7 %collective-permute-done.14 = bf16[448,384]{1,0:T(8,128)(2,1)S(1)} collective-permute-done((bf16[448,384]{1,0:T(8,128)(2,1)}, bf16[448,384]{1,0:T(8,128)(2,1)S(1)}, u32[]{:S(2)}, u32[]{:S(2)}) %collective-permute-start.14) | collective-permute-done | bytes 344096 | tf_op jit(solution)/shard_map/ppermute | solution.py:521
  210.1 15.1 %shard_map.153 = (bf16[32,4,8,384]{3,2,1,0:T(8,128)(2,1)}, f32[1152,384]{1,0:T(8,128)}, f32[384,128]{1,0:T(8,128)}) custom-call(bf16[4,384,256]{2,1,0:T(8,128)(2,1)} %get-tuple-element.66.flat_ref, bf16[4,1152,256]{2,1,0:T(8,128)(2,1)} %get-tuple-element.67.triple_ref, f32[4,16,256]{2,1,0:T(8,128)} %get-tuple-element.68.stat_ref, ...), custom_call_target="tpu_custom_call" | custom-call | flops 24000000000 | bytes 7077888 | tf_op jit(solution)/shard_map/pallas_call | solution.py:476
  225.2 6.2 %collective-permute-done.23 = bf16[448,384]{1,0:T(8,128)(2,1)S(1)} collective-permute-done((bf16[448,384]{1,0:T(8,128)(2,1)S(1)}, bf16[448,384]{1,0:T(8,128)(2,1)S(1)}, u32[]{:S(2)}, u32[]{:S(2)}) %collective-permute-start.23) | collective-permute-done | bytes 344096 | tf_op jit(solution)/shard_map/ppermute | solution.py:521
  233.1 15.8 %shard_map.154 = (bf16[32,4,8,384]{3,2,1,0:T(8,128)(2,1)}, bf16[1280,384]{1,0:T(8,128)(2,1)}, f32[384,128]{1,0:T(8,128)}) custom-call(bf16[4,384,256]{2,1,0:T(8,128)(2,1)} %get-tuple-element.74.flat_ref, bf16[4,1152,256]{2,1,0:T(8,128)(2,1)} %get-tuple-element.75.triple_ref, f32[4,16,256]{2,1,0:T(8,128)} %get-tuple-element.76.stat_ref, ...), custom_call_target="tpu_custom_call" | custom-call | flops 24000000000 | bytes 7077888 | tf_op jit(solution)/shard_map/pallas_call | solution.py:476
  260.7 4.6 %shard_map.152 = bf16[4,4,4,32,384]{4,3,2,1,0:T(8,128)(2,1)} custom-call(bf16[32,4,8,384]{3,2,1,0:T(8,128)(2,1)} %copy-done, bf16[32,4,8,384]{3,2,1,0:T(8,128)(2,1)} %copy-done.2), custom_call_target="tpu_custom_call" | custom-call | flops 1000000 | bytes 3145728 | tf_op jit(solution)/shard_map/pallas_call | solution.py:373
  272.3 8.7 %collective-permute-done.6 = bf16[160,384]{1,0:T(8,128)(2,1)S(1)} collective-permute-done((bf16[160,384]{1,0:T(8,128)(2,1)S(1)}, bf16[160,384]{1,0:T(8,128)(2,1)S(1)}, u32[]{:S(2)}, u32[]{:S(2)}) %collective-permute-start.6) | collective-permute-done | bytes 122912 | tf_op jit(solution)/shard_map/ppermute | solution.py:521
  281.0 10.6 %collective-permute-done.5 = bf16[160,384]{1,0:T(8,128)(2,1)S(1)} collective-permute-done((bf16[160,384]{1,0:T(8,128)(2,1)S(1)}, bf16[160,384]{1,0:T(8,128)(2,1)S(1)}, u32[]{:S(2)}, u32[]{:S(2)}) %collective-permute-start.5) | collective-permute-done | bytes 122912 | tf_op jit(solution)/shard_map/ppermute | solution.py:521
  305.5 4.1 %fusion.21 = (f32[1536,384]{1,0:T(8,128)}, f32[384,1536]{0,1:T(8,128)S(1)}) fusion(f32[3584,384]{1,0:T(8,128)} %convert_multiply_fusion), kind=kLoop, calls=%fused_computation.70 | loop fusion | bytes 9437184 | tf_op jit(solution)/shard_map/slice | solution.py:681
  318.8 7.3 %all-to-all-done.7.refs_1_ = bf16[32,4,8,384]{3,2,1,0:T(8,128)(2,1)} async-done(((bf16[32,4,8,384]{3,2,1,0:T(8,128)(2,1)}), bf16[32,4,8,384]{3,2,1,0:T(8,128)(2,1)}, u32[]{:S(2)}, u32[]{:S(2)}) %all-to-all-start.7) | async-done | bytes 786464 | tf_op jit(solution)/shard_map/all_to_all | solution.py:608
  326.1 4.6 %shard_map.155 = bf16[4,4,4,32,384]{4,3,2,1,0:T(8,128)(2,1)} custom-call(bf16[32,4,8,384]{3,2,1,0:T(8,128)(2,1)} %copy-done.1, bf16[32,4,8,384]{3,2,1,0:T(8,128)(2,1)} %all-to-all-done.7.refs_1_), custom_call_target="tpu_custom_call" | custom-call | flops 1000000 | bytes 3145728 | tf_op jit(solution)/shard_map/pallas_call | solution.py:373
  (118 shorter events, 90.0 us)
Async XLA Ops:
  4.6 27.9 %all-to-all-start = ((bf16[32,4,8,384]{3,2,1,0:T(8,128)(2,1)}), bf16[32,4,8,384]{3,2,1,0:T(8,128)(2,1)S(1)}, u32[]{:S(2)}, u32[]{:S(2)}) async-start(bf16[32,4,8,384]{3,2,1,0:T(8,128)(2,1)} %shard_map.143), calls=%async_computation | async-start | bytes 1572864 | tf_op jit(solution)/shard_map/all_to_all | solution.py:597
  32.6 24.2 %all-to-all-start.1 = ((bf16[32,4,8,384]{3,2,1,0:T(8,128)(2,1)}), bf16[32,4,8,384]{3,2,1,0:T(8,128)(2,1)S(1)}, u32[]{:S(2)}, u32[]{:S(2)}) async-start(bf16[32,4,8,384]{3,2,1,0:T(8,128)(2,1)} %shard_map.147), calls=%async_computation.1 | async-start | bytes 1572864 | tf_op jit(solution)/shard_map/all_to_all | solution.py:597
  56.8 27.5 %all-to-all-start.2 = ((bf16[32,4,8,384]{3,2,1,0:T(8,128)(2,1)}), bf16[32,4,8,384]{3,2,1,0:T(8,128)(2,1)S(1)}, u32[]{:S(2)}, u32[]{:S(2)}) async-start(bf16[32,4,8,384]{3,2,1,0:T(8,128)(2,1)} %shard_map.146), calls=%async_computation.2 | async-start | bytes 1572864 | tf_op jit(solution)/shard_map/all_to_all | solution.py:597
  84.3 42.5 %all-to-all-start.3 = ((bf16[32,4,8,384]{3,2,1,0:T(8,128)(2,1)}), bf16[32,4,8,384]{3,2,1,0:T(8,128)(2,1)S(1)}, u32[]{:S(2)}, u32[]{:S(2)}) async-start(bf16[32,4,8,384]{3,2,1,0:T(8,128)(2,1)} %shard_map.149), calls=%async_computation.3 | async-start | bytes 1572864 | tf_op jit(solution)/shard_map/all_to_all | solution.py:597
  152.0 49.1 %all-to-all-start.4 = ((bf16[32,4,8,384]{3,2,1,0:T(8,128)(2,1)}), bf16[32,4,8,384]{3,2,1,0:T(8,128)(2,1)S(1)}, u32[]{:S(2)}, u32[]{:S(2)}) async-start(bf16[32,4,8,384]{3,2,1,0:T(8,128)(2,1)} %get-tuple-element.59), calls=%async_computation.4 | async-start | bytes 1572864 | tf_op jit(solution)/shard_map/all_to_all | solution.py:608
  160.6 15.3 %collective-permute-start.12 = (bf16[448,384]{1,0:T(8,128)(2,1)}, bf16[448,384]{1,0:T(8,128)(2,1)S(1)}, u32[]{:S(2)}, u32[]{:S(2)}) collective-permute-start(bf16[448,384]{1,0:T(8,128)(2,1)} %get-tuple-element.112), channel_id=1, source_target_pairs={{0,2},{1,3},{2,0},{3,1},{4,6},{5,7},{6,4},{7,5},{8,10},{9,11},{10,... | collective-permute-start | bytes 1032200 | tf_op jit(solution)/shard_map/ppermute | solution.py:521
  162.2 22.5 %collective-permute-start.14 = (bf16[448,384]{1,0:T(8,128)(2,1)}, bf16[448,384]{1,0:T(8,128)(2,1)S(1)}, u32[]{:S(2)}, u32[]{:S(2)}) collective-permute-start(bf16[448,384]{1,0:T(8,128)(2,1)} %get-tuple-element.113), channel_id=1, source_target_pairs={{0,6},{1,7},{2,4},{3,5},{4,2},{5,3},{6,0},{7,1},{8,14},{9,15},{10,... | collective-permute-start | bytes 1032200 | tf_op jit(solution)/shard_map/ppermute | solution.py:521
  163.6 21.6 %collective-permute-start.13 = (bf16[448,384]{1,0:T(8,128)(2,1)S(1)}, bf16[448,384]{1,0:T(8,128)(2,1)S(1)}, u32[]{:S(2)}, u32[]{:S(2)}) collective-permute-start(bf16[448,384]{1,0:T(8,128)(2,1)S(1)} %get-tuple-element.114), channel_id=1, source_target_pairs={{0,4},{1,5},{2,6},{3,7},{4,0},{5,1},{6,2},{7,3},{8,12},{9,13},{10,... | collective-permute-start | bytes 1032200 | tf_op jit(solution)/shard_map/ppermute | solution.py:521
  189.3 7.2 %collective-permute-start.16 = (bf16[112,384]{1,0:T(8,128)(2,1)S(1)}, bf16[112,384]{1,0:T(8,128)(2,1)S(1)}, u32[]{:S(2)}, u32[]{:S(2)}) collective-permute-start(bf16[112,384]{1,0:T(8,128)(2,1)S(1)} %get-tuple-element.132), channel_id=1, source_target_pairs={{0,16},{8,24},{16,0},{24,8},{1,17},{9,25},{17,1},{25,9},{2,18},{10... | collective-permute-start | bytes 258056 | tf_op jit(solution)/shard_map/ppermute | solution.py:521
  196.6 7.8 %collective-permute-start.20 = (bf16[112,384]{1,0:T(8,128)(2,1)S(1)}, bf16[112,384]{1,0:T(8,128)(2,1)S(1)}, u32[]{:S(2)}, u32[]{:S(2)}) collective-permute-start(bf16[112,384]{1,0:T(8,128)(2,1)S(1)} %fusion.18), channel_id=1, source_target_pairs={{0,24},{8,16},{16,8},{24,0},{1,25},{9,17},{17,9},{25,1},{2,26},{10... | collective-permute-start | bytes 258056 | tf_op jit(solution)/shard_map/ppermute | solution.py:521
  201.1 32.0 %all-to-all-start.5 = ((bf16[32,4,8,384]{3,2,1,0:T(8,128)(2,1)}), bf16[32,4,8,384]{3,2,1,0:T(8,128)(2,1)S(1)}, u32[]{:S(2)}, u32[]{:S(2)}) async-start(bf16[32,4,8,384]{3,2,1,0:T(8,128)(2,1)} %get-tuple-element.65), calls=%async_computation.5 | async-start | bytes 1572864 | tf_op jit(solution)/shard_map/all_to_all | solution.py:608
  206.5 18.7 %collective-permute-start.22 = (bf16[448,384]{1,0:T(8,128)(2,1)S(1)}, bf16[448,384]{1,0:T(8,128)(2,1)S(1)}, u32[]{:S(2)}, u32[]{:S(2)}) collective-permute-start(bf16[448,384]{1,0:T(8,128)(2,1)S(1)} %get-tuple-element.125), channel_id=1, source_target_pairs={{0,4},{1,5},{2,6},{3,7},{4,0},{5,1},{6,2},{7,3},{8,12},{9,13},{10,... | collective-permute-start | bytes 1032200 | tf_op jit(solution)/shard_map/ppermute | solution.py:521
  207.2 18.0 %collective-permute-start.21 = (bf16[448,384]{1,0:T(8,128)(2,1)S(1)}, bf16[448,384]{1,0:T(8,128)(2,1)S(1)}, u32[]{:S(2)}, u32[]{:S(2)}) collective-permute-start(bf16[448,384]{1,0:T(8,128)(2,1)S(1)} %get-tuple-element.125), channel_id=1, source_target_pairs={{0,2},{1,3},{2,0},{3,1},{4,6},{5,7},{6,4},{7,5},{8,10},{9,11},{10,... | collective-permute-start | bytes 1032200 | tf_op jit(solution)/shard_map/ppermute | solution.py:521
  208.1 23.3 %collective-permute-start.23 = (bf16[448,384]{1,0:T(8,128)(2,1)S(1)}, bf16[448,384]{1,0:T(8,128)(2,1)S(1)}, u32[]{:S(2)}, u32[]{:S(2)}) collective-permute-start(bf16[448,384]{1,0:T(8,128)(2,1)S(1)} %get-tuple-element.125), channel_id=1, source_target_pairs={{0,6},{1,7},{2,4},{3,5},{4,2},{5,3},{6,0},{7,1},{8,14},{9,15},{10,... | collective-permute-start | bytes 1032200 | tf_op jit(solution)/shard_map/ppermute | solution.py:521
  233.1 36.8 %collective-permute-start.24 = (bf16[1792,384]{1,0:T(8,128)(2,1)}, bf16[1792,384]{1,0:T(8,128)(2,1)}, u32[]{:S(2)}, u32[]{:S(2)}) collective-permute-start(bf16[1792,384]{1,0:T(8,128)(2,1)} %get-tuple-element.106), channel_id=1, source_target_pairs={{0,1},{1,0},{2,3},{3,2},{4,5},{5,4},{6,7},{7,6},{8,9},{9,8},{10,11... | collective-permute-start | bytes 4128776 | tf_op jit(solution)/shard_map/ppermute | solution.py:521
  253.2 12.1 %collective-permute-start.1 = (bf16[160,384]{1,0:T(8,128)(2,1)S(1)}, bf16[160,384]{1,0:T(8,128)(2,1)S(1)}, u32[]{:S(2)}, u32[]{:S(2)}) collective-permute-start(bf16[160,384]{1,0:T(8,128)(2,1)S(1)} %get-tuple-element.121), channel_id=1, source_target_pairs={{0,2},{1,3},{2,0},{3,1},{4,6},{5,7},{6,4},{7,5},{8,10},{9,11},{10,... | collective-permute-start | bytes 368648 | tf_op jit(solution)/shard_map/ppermute | solution.py:521
  254.1 11.2 %collective-permute-start.3 = (bf16[160,384]{1,0:T(8,128)(2,1)S(1)}, bf16[160,384]{1,0:T(8,128)(2,1)S(1)}, u32[]{:S(2)}, u32[]{:S(2)}) collective-permute-start(bf16[160,384]{1,0:T(8,128)(2,1)S(1)} %get-tuple-element.122), channel_id=1, source_target_pairs={{0,6},{1,7},{2,4},{3,5},{4,2},{5,3},{6,0},{7,1},{8,14},{9,15},{10,... | collective-permute-start | bytes 368648 | tf_op jit(solution)/shard_map/ppermute | solution.py:521
  255.6 9.8 %collective-permute-start.2 = (bf16[160,384]{1,0:T(8,128)(2,1)S(1)}, bf16[160,384]{1,0:T(8,128)(2,1)S(1)}, u32[]{:S(2)}, u32[]{:S(2)}) collective-permute-start(bf16[160,384]{1,0:T(8,128)(2,1)S(1)} %get-tuple-element.123), channel_id=1, source_target_pairs={{0,4},{1,5},{2,6},{3,7},{4,0},{5,1},{6,2},{7,3},{8,12},{9,13},{10,... | collective-permute-start | bytes 368648 | tf_op jit(solution)/shard_map/ppermute | solution.py:521
  256.8 45.3 %all-to-all-start.6 = ((bf16[32,4,8,384]{3,2,1,0:T(8,128)(2,1)}), bf16[32,4,8,384]{3,2,1,0:T(8,128)(2,1)S(1)}, u32[]{:S(2)}, u32[]{:S(2)}) async-start(bf16[32,4,8,384]{3,2,1,0:T(8,128)(2,1)} %get-tuple-element.73), calls=%async_computation.6 | async-start | bytes 1572864 | tf_op jit(solution)/shard_map/all_to_all | solution.py:608
  265.4 15.6 %collective-permute-start.6 = (bf16[160,384]{1,0:T(8,128)(2,1)S(1)}, bf16[160,384]{1,0:T(8,128)(2,1)S(1)}, u32[]{:S(2)}, u32[]{:S(2)}) collective-permute-start(bf16[160,384]{1,0:T(8,128)(2,1)S(1)} %fusion.15), channel_id=1, source_target_pairs={{0,24},{8,16},{16,8},{24,0},{1,25},{9,17},{17,9},{25,1},{2,26},{10... | collective-permute-start | bytes 368648 | tf_op jit(solution)/shard_map/ppermute | solution.py:521
  268.9 22.8 %collective-permute-start.5 = (bf16[160,384]{1,0:T(8,128)(2,1)S(1)}, bf16[160,384]{1,0:T(8,128)(2,1)S(1)}, u32[]{:S(2)}, u32[]{:S(2)}) collective-permute-start(bf16[160,384]{1,0:T(8,128)(2,1)S(1)} %fusion.15), channel_id=1, source_target_pairs={{0,16},{8,24},{16,0},{24,8},{1,17},{9,25},{17,1},{25,9},{2,18},{10... | collective-permute-start | bytes 368648 | tf_op jit(solution)/shard_map/ppermute | solution.py:521
  268.9 22.8 %collective-permute-start.4 = (bf16[160,384]{1,0:T(8,128)(2,1)S(1)}, bf16[160,384]{1,0:T(8,128)(2,1)S(1)}, u32[]{:S(2)}, u32[]{:S(2)}) collective-permute-start(bf16[160,384]{1,0:T(8,128)(2,1)S(1)} %fusion.15), channel_id=1, source_target_pairs={{0,8},{8,0},{16,24},{24,16},{1,9},{9,1},{17,25},{25,17},{2,10},{10... | collective-permute-start | bytes 368648 | tf_op jit(solution)/shard_map/ppermute | solution.py:521
  302.1 13.0 %collective-permute-start.10 = (bf16[640,384]{0,1:T(8,128)(2,1)}, bf16[640,384]{0,1:T(8,128)(2,1)}, u32[]{:S(2)}, u32[]{:S(2)}) collective-permute-start(bf16[640,384]{0,1:T(8,128)(2,1)} %pad_maximum_fusion.3), channel_id=1, source_target_pairs={{0,1},{1,0},{2,3},{3,2},{4,5},{5,4},{6,7},{7,6},{8,9},{9,8},{10,11... | collective-permute-start | bytes 1474568 | tf_op jit(solution)/shard_map/ppermute | solution.py:521
  302.1 24.0 %all-to-all-start.7 = ((bf16[32,4,8,384]{3,2,1,0:T(8,128)(2,1)}), bf16[32,4,8,384]{3,2,1,0:T(8,128)(2,1)}, u32[]{:S(2)}, u32[]{:S(2)}) async-start(bf16[32,4,8,384]{3,2,1,0:T(8,128)(2,1)} %get-tuple-element.83), calls=%async_computation.7 | async-start | bytes 1572864 | tf_op jit(solution)/shard_map/all_to_all | solution.py:608
  (22 other events, 175.7 us)

commit v4 on v3

--- a/solution.py
+++ b/solution.py
@@ -85,18 +85,35 @@
     return total
 
 
+def by_rows(rows, body):
+    def step(n, _):
+        body(pl.ds(pl.multiple_of(n * 128, 128), 128))
+        return 0
+
+    lax.fori_loop(0, rows // 128, step, 0)
+
+
 def begin(carried, acc_ref, grad_gain_ref):
+    def fill(part):
+        if carried:
+            acc_ref[part] = carried[0][part]
+        else:
+            acc_ref[part] = jnp.zeros((128, acc_ref.shape[1]), F32)
+
+    by_rows(acc_ref.shape[0], fill)
     if carried:
-        acc_ref[...] = carried[0][...]
         grad_gain_ref[...] = carried[1][...]
     else:
-        acc_ref[...] = jnp.zeros_like(acc_ref)
         grad_gain_ref[...] = jnp.zeros_like(grad_gain_ref)
 
 
 def finish(acc_ref, grads_ref, grad_gain_ref):
     rows = acc_ref.shape[0]
-    grads_ref[:rows] = acc_ref[...].astype(grads_ref.dtype)
+
+    def cast(part):
+        grads_ref[part] = acc_ref[part].astype(grads_ref.dtype)
+
+    by_rows(rows, cast)
     if grads_ref.shape[0] > rows:
         gains = jnp.sum(grad_gain_ref[...].T, axis=0, keepdims=True)
         spare = grads_ref.shape[0] - rows

time: 332 us -> 333 us (level)
  no operation moved by 1% of the time
where the time goes in v4:
time: 333 us; the launch traced here: 331 us
  Pallas kernels  134 us (40%)
  waiting for transfers between devices  99.7 us (30%)
  starting transfers between devices  64.9 us (19%)
  local copies, waits for them, and re-layouts  17.8 us (5%)
  other arithmetic  13.2 us (4%)
    ppermute x25, waiting for transfers between devices, swap(): lax.ppermute(values, axis, [(i, i ^ offset) for i in range(lax.axis_size(...  59.3 us
    pallas_call x2, Pallas kernels, mlp_call(): pl.pallas_call(mlp_kernel, grid=(groups,), in_specs=[per_group((width, to...  45.1 us
    all_to_all x4, waiting for transfers between devices, send(): lax.all_to_all(tie(sends, *after), both, split_axis=0, concat_axis=0, til...  33.1 us
    pallas_call x2, Pallas kernels, back_call(): pl.pallas_call(back_kernel, grid=(groups,), in_specs=[per_group((width, t...  31 us
    pallas_call x2, Pallas kernels, attend_call(): pl.pallas_call(attend_kernel, grid=(groups,), in_specs=[pieces_spec(act),...  28.9 us
    ppermute x25, starting transfers between devices, swap(): lax.ppermute(values, axis, [(i, i ^ offset) for i in range(lax.axis_size(...  27.7 us
    all_to_all x4, starting transfers between devices, send(): lax.all_to_all(tie(sends, *after), both, split_axis=0, concat_axis=0, til...  20.6 us
    all_to_all x4, starting transfers between devices, give_back(): return lax.all_to_all(pieces, both, split_axis=0, concat_axis=0, tiled=True)  16.6 us
  transfers between devices with their start and end apart: 33, of which 16 were waited for; matrix products, arithmetic and copies ran while one was open for 9% of the time, Pallas kernels for 31%

profile of v4, /device:TPU:0, one launch (start us, length us, event | category | flops | bytes accessed | tf_op | source)
XLA Modules:
  0.0 331.2 jit_solution(14897568940175025089)
XLA Ops:
  0.6 4.0 %shard_map.143 = bf16[32,4,8,384]{3,2,1,0:T(8,128)(2,1)} custom-call(bf16[4,4,4,32,384]{4,3,2,1,0:T(8,128)(2,1)} %bitcast.97), custom_call_target="tpu_custom_call" | custom-call | flops 1000000 | bytes 1572864 | tf_op jit(solution)/shard_map/pallas_call | solution.py:372
  4.6 7.3 %all-to-all-start = ((bf16[32,4,8,384]{3,2,1,0:T(8,128)(2,1)}), bf16[32,4,8,384]{3,2,1,0:T(8,128)(2,1)S(1)}, u32[]{:S(2)}, u32[]{:S(2)}) async-start(bf16[32,4,8,384]{3,2,1,0:T(8,128)(2,1)} %shard_map.143), calls=%async_computation | async-start | bytes 1572864 | tf_op jit(solution)/shard_map/all_to_all | solution.py:614
  12.0 4.0 %shard_map.147 = bf16[32,4,8,384]{3,2,1,0:T(8,128)(2,1)} custom-call(bf16[4,4,4,32,384]{4,3,2,1,0:T(8,128)(2,1)} %bitcast.98), custom_call_target="tpu_custom_call" | custom-call | flops 1000000 | bytes 1572864 | tf_op jit(solution)/shard_map/pallas_call | solution.py:372
  16.0 16.6 %all-to-all-done.act_ref = bf16[32,4,8,384]{3,2,1,0:T(8,128)(2,1)S(1)} async-done(((bf16[32,4,8,384]{3,2,1,0:T(8,128)(2,1)}), bf16[32,4,8,384]{3,2,1,0:T(8,128)(2,1)S(1)}, u32[]{:S(2)}, u32[]{:S(2)}) %all-to-all-start) | async-done | bytes 786464 | tf_op jit(solution)/shard_map/all_to_all | solution.py:614
  36.2 4.0 %shard_map.146 = bf16[32,4,8,384]{3,2,1,0:T(8,128)(2,1)} custom-call(bf16[4,4,4,32,384]{4,3,2,1,0:T(8,128)(2,1)} %bitcast.99), custom_call_target="tpu_custom_call" | custom-call | flops 1000000 | bytes 1572864 | tf_op jit(solution)/shard_map/pallas_call | solution.py:372
  40.2 16.6 %all-to-all-done.1.act_ref = bf16[32,4,8,384]{3,2,1,0:T(8,128)(2,1)S(1)} async-done(((bf16[32,4,8,384]{3,2,1,0:T(8,128)(2,1)}), bf16[32,4,8,384]{3,2,1,0:T(8,128)(2,1)S(1)}, u32[]{:S(2)}, u32[]{:S(2)}) %all-to-all-start.1) | async-done | bytes 786464 | tf_op jit(solution)/shard_map/all_to_all | solution.py:614
  65.6 4.2 %shard_map.144 = (f32[384,256]{1,0:T(8,128)}, f32[384,256]{1,0:T(8,128)}, bf16[1152,384]{1,0:T(8,128)(2,1)}, bf16[384,384]{1,0:T(8,128)(2,1)}, bf16[1536,384]{1,0:T(8,128)(2,1)}, /*index=5*/bf16[384,1536]{1,0:T(8,128)(2,1)}) custom-call(f32[1,384]{1,0:T(1,128)} %reshape.62.gain_one_ref, f32[1,384]{1,0:T(1,128)} %reshape.63.gain_two_ref, ...), custom_call_target="tpu_custom_call" | custom-call | flops 1000000 | bytes 16000000 | tf_op jit(solution)/shard_map/pallas_call | solution.py:315
  69.8 14.5 %shard_map.145 = (bf16[4,384,256]{2,1,0:T(8,128)(2,1)}, bf16[4,1152,256]{2,1,0:T(8,128)(2,1)}, bf16[4,384,256]{2,1,0:T(8,128)(2,1)}, f32[4,16,256]{2,1,0:T(8,128)}, f32[4,384,256]{2,1,0:T(8,128)}) custom-call(bf16[32,4,8,384]{3,2,1,0:T(8,128)(2,1)} %copy-done.9, f32[384,256]{1,0:T(8,128)} %get-tuple-element.47.gain_ref, ...), custom_call_target="tpu_custom_call" | custom-call | flops 12000000000 | bytes 4718592 | tf_op jit(solution)/shard_map/pallas_call | solution.py:426
  84.3 6.0 %all-to-all-start.3 = ((bf16[32,4,8,384]{3,2,1,0:T(8,128)(2,1)}), bf16[32,4,8,384]{3,2,1,0:T(8,128)(2,1)S(1)}, u32[]{:S(2)}, u32[]{:S(2)}) async-start(bf16[32,4,8,384]{3,2,1,0:T(8,128)(2,1)} %shard_map.149), calls=%async_computation.3 | async-start | bytes 1572864 | tf_op jit(solution)/shard_map/all_to_all | solution.py:614
  90.3 14.5 %shard_map.150 = (bf16[4,384,256]{2,1,0:T(8,128)(2,1)}, bf16[4,1152,256]{2,1,0:T(8,128)(2,1)}, bf16[4,384,256]{2,1,0:T(8,128)(2,1)}, f32[4,16,256]{2,1,0:T(8,128)}, f32[4,384,256]{2,1,0:T(8,128)}) custom-call(bf16[32,4,8,384]{3,2,1,0:T(8,128)(2,1)} %copy-done.7, f32[384,256]{1,0:T(8,128)} %get-tuple-element.47.gain_ref, ...), custom_call_target="tpu_custom_call" | custom-call | flops 12000000000 | bytes 4718592 | tf_op jit(solution)/shard_map/pallas_call | solution.py:426
  104.8 22.1 %shard_map.148 = (bf16[32,4,8,384]{3,2,1,0:T(8,128)(2,1)}, f32[4,384,256]{2,1,0:T(8,128)}, bf16[4,384,256]{2,1,0:T(8,128)(2,1)}, f32[3456,384]{1,0:T(8,128)}, f32[384,128]{1,0:T(8,128)}) custom-call(f32[4,384,256]{2,1,0:T(8,128)} %get-tuple-element.50.attended_ref, bf16[4,384,256]{2,1,0:T(8,128)(2,1)} %get-tuple-element.51.mixed_ref, ...), custom_call_target="tpu_custom_call" | custom-call | flops 16000000000 | bytes 5505024 | tf_op jit(solution)/shard_map/pallas_call | solution.py:455
  127.8 23.0 %shard_map.151 = (bf16[32,4,8,384]{3,2,1,0:T(8,128)(2,1)}, f32[4,384,256]{2,1,0:T(8,128)}, bf16[4,384,256]{2,1,0:T(8,128)(2,1)}, bf16[3584,384]{1,0:T(8,128)(2,1)}, f32[384,128]{1,0:T(8,128)}) custom-call(f32[4,384,256]{2,1,0:T(8,128)} %get-tuple-element.60.attended_ref, bf16[4,384,256]{2,1,0:T(8,128)(2,1)} %get-tuple-element.61.mixed_ref, ...), custom_call_target="tpu_custom_call" | custom-call | flops 16000000000 | bytes 5505024 | tf_op jit(solution)/shard_map/pallas_call | solution.py:455
  152.4 5.9 %all-to-all-start.4 = ((bf16[32,4,8,384]{3,2,1,0:T(8,128)(2,1)}), bf16[32,4,8,384]{3,2,1,0:T(8,128)(2,1)S(1)}, u32[]{:S(2)}, u32[]{:S(2)}) async-start(bf16[32,4,8,384]{3,2,1,0:T(8,128)(2,1)} %get-tuple-element.59), calls=%async_computation.4 | async-start | bytes 1572864 | tf_op jit(solution)/shard_map/all_to_all | solution.py:625
  164.5 11.8 %collective-permute-done.12 = bf16[448,384]{1,0:T(8,128)(2,1)S(1)} collective-permute-done((bf16[448,384]{1,0:T(8,128)(2,1)}, bf16[448,384]{1,0:T(8,128)(2,1)S(1)}, u32[]{:S(2)}, u32[]{:S(2)}) %collective-permute-start.12) | collective-permute-done | bytes 344096 | tf_op jit(solution)/shard_map/ppermute | solution.py:538
  176.3 8.7 %collective-permute-done.14 = bf16[448,384]{1,0:T(8,128)(2,1)S(1)} collective-permute-done((bf16[448,384]{1,0:T(8,128)(2,1)}, bf16[448,384]{1,0:T(8,128)(2,1)S(1)}, u32[]{:S(2)}, u32[]{:S(2)}) %collective-permute-start.14) | collective-permute-done | bytes 344096 | tf_op jit(solution)/shard_map/ppermute | solution.py:538
  210.5 15.2 %shard_map.153 = (bf16[32,4,8,384]{3,2,1,0:T(8,128)(2,1)}, f32[1152,384]{1,0:T(8,128)}, f32[384,128]{1,0:T(8,128)}) custom-call(bf16[4,384,256]{2,1,0:T(8,128)(2,1)} %get-tuple-element.66.flat_ref, bf16[4,1152,256]{2,1,0:T(8,128)(2,1)} %get-tuple-element.67.triple_ref, f32[4,16,256]{2,1,0:T(8,128)} %get-tuple-element.68.stat_ref, ...), custom_call_target="tpu_custom_call" | custom-call | flops 24000000000 | bytes 7077888 | tf_op jit(solution)/shard_map/pallas_call | solution.py:493
  225.6 6.1 %collective-permute-done.23 = bf16[448,384]{1,0:T(8,128)(2,1)S(1)} collective-permute-done((bf16[448,384]{1,0:T(8,128)(2,1)S(1)}, bf16[448,384]{1,0:T(8,128)(2,1)S(1)}, u32[]{:S(2)}, u32[]{:S(2)}) %collective-permute-start.23) | collective-permute-done | bytes 344096 | tf_op jit(solution)/shard_map/ppermute | solution.py:538
  233.5 15.9 %shard_map.154 = (bf16[32,4,8,384]{3,2,1,0:T(8,128)(2,1)}, bf16[1280,384]{1,0:T(8,128)(2,1)}, f32[384,128]{1,0:T(8,128)}) custom-call(bf16[4,384,256]{2,1,0:T(8,128)(2,1)} %get-tuple-element.74.flat_ref, bf16[4,1152,256]{2,1,0:T(8,128)(2,1)} %get-tuple-element.75.triple_ref, f32[4,16,256]{2,1,0:T(8,128)} %get-tuple-element.76.stat_ref, ...), custom_call_target="tpu_custom_call" | custom-call | flops 24000000000 | bytes 7077888 | tf_op jit(solution)/shard_map/pallas_call | solution.py:493
  261.3 4.6 %shard_map.152 = bf16[4,4,4,32,384]{4,3,2,1,0:T(8,128)(2,1)} custom-call(bf16[32,4,8,384]{3,2,1,0:T(8,128)(2,1)} %copy-done, bf16[32,4,8,384]{3,2,1,0:T(8,128)(2,1)} %copy-done.2), custom_call_target="tpu_custom_call" | custom-call | flops 1000000 | bytes 3145728 | tf_op jit(solution)/shard_map/pallas_call | solution.py:390
  272.9 8.7 %collective-permute-done.6 = bf16[160,384]{1,0:T(8,128)(2,1)S(1)} collective-permute-done((bf16[160,384]{1,0:T(8,128)(2,1)S(1)}, bf16[160,384]{1,0:T(8,128)(2,1)S(1)}, u32[]{:S(2)}, u32[]{:S(2)}) %collective-permute-start.6) | collective-permute-done | bytes 122912 | tf_op jit(solution)/shard_map/ppermute | solution.py:538
  281.6 10.6 %collective-permute-done.5 = bf16[160,384]{1,0:T(8,128)(2,1)S(1)} collective-permute-done((bf16[160,384]{1,0:T(8,128)(2,1)S(1)}, bf16[160,384]{1,0:T(8,128)(2,1)S(1)}, u32[]{:S(2)}, u32[]{:S(2)}) %collective-permute-start.5) | collective-permute-done | bytes 122912 | tf_op jit(solution)/shard_map/ppermute | solution.py:538
  306.1 4.1 %fusion.21 = (f32[1536,384]{1,0:T(8,128)}, f32[384,1536]{0,1:T(8,128)S(1)}) fusion(f32[3584,384]{1,0:T(8,128)} %convert_multiply_fusion), kind=kLoop, calls=%fused_computation.70 | loop fusion | bytes 9437184 | tf_op jit(solution)/shard_map/slice | solution.py:698
  319.3 7.3 %all-to-all-done.7.refs_1_ = bf16[32,4,8,384]{3,2,1,0:T(8,128)(2,1)} async-done(((bf16[32,4,8,384]{3,2,1,0:T(8,128)(2,1)}), bf16[32,4,8,384]{3,2,1,0:T(8,128)(2,1)}, u32[]{:S(2)}, u32[]{:S(2)}) %all-to-all-start.7) | async-done | bytes 786464 | tf_op jit(solution)/shard_map/all_to_all | solution.py:625
  326.6 4.6 %shard_map.155 = bf16[4,4,4,32,384]{4,3,2,1,0:T(8,128)(2,1)} custom-call(bf16[32,4,8,384]{3,2,1,0:T(8,128)(2,1)} %copy-done.1, bf16[32,4,8,384]{3,2,1,0:T(8,128)(2,1)} %all-to-all-done.7.refs_1_), custom_call_target="tpu_custom_call" | custom-call | flops 1000000 | bytes 3145728 | tf_op jit(solution)/shard_map/pallas_call | solution.py:390
  (118 shorter events, 90.0 us)
Async XLA Ops:
  4.6 27.9 %all-to-all-start = ((bf16[32,4,8,384]{3,2,1,0:T(8,128)(2,1)}), bf16[32,4,8,384]{3,2,1,0:T(8,128)(2,1)S(1)}, u32[]{:S(2)}, u32[]{:S(2)}) async-start(bf16[32,4,8,384]{3,2,1,0:T(8,128)(2,1)} %shard_map.143), calls=%async_computation | async-start | bytes 1572864 | tf_op jit(solution)/shard_map/all_to_all | solution.py:614
  32.6 24.2 %all-to-all-start.1 = ((bf16[32,4,8,384]{3,2,1,0:T(8,128)(2,1)}), bf16[32,4,8,384]{3,2,1,0:T(8,128)(2,1)S(1)}, u32[]{:S(2)}, u32[]{:S(2)}) async-start(bf16[32,4,8,384]{3,2,1,0:T(8,128)(2,1)} %shard_map.147), calls=%async_computation.1 | async-start | bytes 1572864 | tf_op jit(solution)/shard_map/all_to_all | solution.py:614
  56.8 27.5 %all-to-all-start.2 = ((bf16[32,4,8,384]{3,2,1,0:T(8,128)(2,1)}), bf16[32,4,8,384]{3,2,1,0:T(8,128)(2,1)S(1)}, u32[]{:S(2)}, u32[]{:S(2)}) async-start(bf16[32,4,8,384]{3,2,1,0:T(8,128)(2,1)} %shard_map.146), calls=%async_computation.2 | async-start | bytes 1572864 | tf_op jit(solution)/shard_map/all_to_all | solution.py:614
  84.3 42.6 %all-to-all-start.3 = ((bf16[32,4,8,384]{3,2,1,0:T(8,128)(2,1)}), bf16[32,4,8,384]{3,2,1,0:T(8,128)(2,1)S(1)}, u32[]{:S(2)}, u32[]{:S(2)}) async-start(bf16[32,4,8,384]{3,2,1,0:T(8,128)(2,1)} %shard_map.149), calls=%async_computation.3 | async-start | bytes 1572864 | tf_op jit(solution)/shard_map/all_to_all | solution.py:614
  152.4 49.1 %all-to-all-start.4 = ((bf16[32,4,8,384]{3,2,1,0:T(8,128)(2,1)}), bf16[32,4,8,384]{3,2,1,0:T(8,128)(2,1)S(1)}, u32[]{:S(2)}, u32[]{:S(2)}) async-start(bf16[32,4,8,384]{3,2,1,0:T(8,128)(2,1)} %get-tuple-element.59), calls=%async_computation.4 | async-start | bytes 1572864 | tf_op jit(solution)/shard_map/all_to_all | solution.py:625
  161.0 15.3 %collective-permute-start.12 = (bf16[448,384]{1,0:T(8,128)(2,1)}, bf16[448,384]{1,0:T(8,128)(2,1)S(1)}, u32[]{:S(2)}, u32[]{:S(2)}) collective-permute-start(bf16[448,384]{1,0:T(8,128)(2,1)} %get-tuple-element.112), channel_id=1, source_target_pairs={{0,2},{1,3},{2,0},{3,1},{4,6},{5,7},{6,4},{7,5},{8,10},{9,11},{10,... | collective-permute-start | bytes 1032200 | tf_op jit(solution)/shard_map/ppermute | solution.py:538
  162.6 22.5 %collective-permute-start.14 = (bf16[448,384]{1,0:T(8,128)(2,1)}, bf16[448,384]{1,0:T(8,128)(2,1)S(1)}, u32[]{:S(2)}, u32[]{:S(2)}) collective-permute-start(bf16[448,384]{1,0:T(8,128)(2,1)} %get-tuple-element.113), channel_id=1, source_target_pairs={{0,6},{1,7},{2,4},{3,5},{4,2},{5,3},{6,0},{7,1},{8,14},{9,15},{10,... | collective-permute-start | bytes 1032200 | tf_op jit(solution)/shard_map/ppermute | solution.py:538
  164.1 21.6 %collective-permute-start.13 = (bf16[448,384]{1,0:T(8,128)(2,1)S(1)}, bf16[448,384]{1,0:T(8,128)(2,1)S(1)}, u32[]{:S(2)}, u32[]{:S(2)}) collective-permute-start(bf16[448,384]{1,0:T(8,128)(2,1)S(1)} %get-tuple-element.114), channel_id=1, source_target_pairs={{0,4},{1,5},{2,6},{3,7},{4,0},{5,1},{6,2},{7,3},{8,12},{9,13},{10,... | collective-permute-start | bytes 1032200 | tf_op jit(solution)/shard_map/ppermute | solution.py:538
  189.8 7.2 %collective-permute-start.16 = (bf16[112,384]{1,0:T(8,128)(2,1)S(1)}, bf16[112,384]{1,0:T(8,128)(2,1)S(1)}, u32[]{:S(2)}, u32[]{:S(2)}) collective-permute-start(bf16[112,384]{1,0:T(8,128)(2,1)S(1)} %get-tuple-element.132), channel_id=1, source_target_pairs={{0,16},{8,24},{16,0},{24,8},{1,17},{9,25},{17,1},{25,9},{2,18},{10... | collective-permute-start | bytes 258056 | tf_op jit(solution)/shard_map/ppermute | solution.py:538
  197.1 7.8 %collective-permute-start.20 = (bf16[112,384]{1,0:T(8,128)(2,1)S(1)}, bf16[112,384]{1,0:T(8,128)(2,1)S(1)}, u32[]{:S(2)}, u32[]{:S(2)}) collective-permute-start(bf16[112,384]{1,0:T(8,128)(2,1)S(1)} %fusion.18), channel_id=1, source_target_pairs={{0,24},{8,16},{16,8},{24,0},{1,25},{9,17},{17,9},{25,1},{2,26},{10... | collective-permute-start | bytes 258056 | tf_op jit(solution)/shard_map/ppermute | solution.py:538
  201.5 32.0 %all-to-all-start.5 = ((bf16[32,4,8,384]{3,2,1,0:T(8,128)(2,1)}), bf16[32,4,8,384]{3,2,1,0:T(8,128)(2,1)S(1)}, u32[]{:S(2)}, u32[]{:S(2)}) async-start(bf16[32,4,8,384]{3,2,1,0:T(8,128)(2,1)} %get-tuple-element.65), calls=%async_computation.5 | async-start | bytes 1572864 | tf_op jit(solution)/shard_map/all_to_all | solution.py:625
  206.9 18.7 %collective-permute-start.22 = (bf16[448,384]{1,0:T(8,128)(2,1)S(1)}, bf16[448,384]{1,0:T(8,128)(2,1)S(1)}, u32[]{:S(2)}, u32[]{:S(2)}) collective-permute-start(bf16[448,384]{1,0:T(8,128)(2,1)S(1)} %get-tuple-element.125), channel_id=1, source_target_pairs={{0,4},{1,5},{2,6},{3,7},{4,0},{5,1},{6,2},{7,3},{8,12},{9,13},{10,... | collective-permute-start | bytes 1032200 | tf_op jit(solution)/shard_map/ppermute | solution.py:538
  207.6 18.0 %collective-permute-start.21 = (bf16[448,384]{1,0:T(8,128)(2,1)S(1)}, bf16[448,384]{1,0:T(8,128)(2,1)S(1)}, u32[]{:S(2)}, u32[]{:S(2)}) collective-permute-start(bf16[448,384]{1,0:T(8,128)(2,1)S(1)} %get-tuple-element.125), channel_id=1, source_target_pairs={{0,2},{1,3},{2,0},{3,1},{4,6},{5,7},{6,4},{7,5},{8,10},{9,11},{10,... | collective-permute-start | bytes 1032200 | tf_op jit(solution)/shard_map/ppermute | solution.py:538
  208.5 23.3 %collective-permute-start.23 = (bf16[448,384]{1,0:T(8,128)(2,1)S(1)}, bf16[448,384]{1,0:T(8,128)(2,1)S(1)}, u32[]{:S(2)}, u32[]{:S(2)}) collective-permute-start(bf16[448,384]{1,0:T(8,128)(2,1)S(1)} %get-tuple-element.125), channel_id=1, source_target_pairs={{0,6},{1,7},{2,4},{3,5},{4,2},{5,3},{6,0},{7,1},{8,14},{9,15},{10,... | collective-permute-start | bytes 1032200 | tf_op jit(solution)/shard_map/ppermute | solution.py:538
  233.5 37.0 %collective-permute-start.24 = (bf16[1792,384]{1,0:T(8,128)(2,1)}, bf16[1792,384]{1,0:T(8,128)(2,1)}, u32[]{:S(2)}, u32[]{:S(2)}) collective-permute-start(bf16[1792,384]{1,0:T(8,128)(2,1)} %get-tuple-element.106), channel_id=1, source_target_pairs={{0,1},{1,0},{2,3},{3,2},{4,5},{5,4},{6,7},{7,6},{8,9},{9,8},{10,11... | collective-permute-start | bytes 4128776 | tf_op jit(solution)/shard_map/ppermute | solution.py:538
  253.8 12.1 %collective-permute-start.1 = (bf16[160,384]{1,0:T(8,128)(2,1)S(1)}, bf16[160,384]{1,0:T(8,128)(2,1)S(1)}, u32[]{:S(2)}, u32[]{:S(2)}) collective-permute-start(bf16[160,384]{1,0:T(8,128)(2,1)S(1)} %get-tuple-element.121), channel_id=1, source_target_pairs={{0,2},{1,3},{2,0},{3,1},{4,6},{5,7},{6,4},{7,5},{8,10},{9,11},{10,... | collective-permute-start | bytes 368648 | tf_op jit(solution)/shard_map/ppermute | solution.py:538
  254.7 11.2 %collective-permute-start.3 = (bf16[160,384]{1,0:T(8,128)(2,1)S(1)}, bf16[160,384]{1,0:T(8,128)(2,1)S(1)}, u32[]{:S(2)}, u32[]{:S(2)}) collective-permute-start(bf16[160,384]{1,0:T(8,128)(2,1)S(1)} %get-tuple-element.122), channel_id=1, source_target_pairs={{0,6},{1,7},{2,4},{3,5},{4,2},{5,3},{6,0},{7,1},{8,14},{9,15},{10,... | collective-permute-start | bytes 368648 | tf_op jit(solution)/shard_map/ppermute | solution.py:538
  256.1 9.8 %collective-permute-start.2 = (bf16[160,384]{1,0:T(8,128)(2,1)S(1)}, bf16[160,384]{1,0:T(8,128)(2,1)S(1)}, u32[]{:S(2)}, u32[]{:S(2)}) collective-permute-start(bf16[160,384]{1,0:T(8,128)(2,1)S(1)} %get-tuple-element.123), channel_id=1, source_target_pairs={{0,4},{1,5},{2,6},{3,7},{4,0},{5,1},{6,2},{7,3},{8,12},{9,13},{10,... | collective-permute-start | bytes 368648 | tf_op jit(solution)/shard_map/ppermute | solution.py:538
  257.3 45.3 %all-to-all-start.6 = ((bf16[32,4,8,384]{3,2,1,0:T(8,128)(2,1)}), bf16[32,4,8,384]{3,2,1,0:T(8,128)(2,1)S(1)}, u32[]{:S(2)}, u32[]{:S(2)}) async-start(bf16[32,4,8,384]{3,2,1,0:T(8,128)(2,1)} %get-tuple-element.73), calls=%async_computation.6 | async-start | bytes 1572864 | tf_op jit(solution)/shard_map/all_to_all | solution.py:625
  266.0 15.6 %collective-permute-start.6 = (bf16[160,384]{1,0:T(8,128)(2,1)S(1)}, bf16[160,384]{1,0:T(8,128)(2,1)S(1)}, u32[]{:S(2)}, u32[]{:S(2)}) collective-permute-start(bf16[160,384]{1,0:T(8,128)(2,1)S(1)} %fusion.15), channel_id=1, source_target_pairs={{0,24},{8,16},{16,8},{24,0},{1,25},{9,17},{17,9},{25,1},{2,26},{10... | collective-permute-start | bytes 368648 | tf_op jit(solution)/shard_map/ppermute | solution.py:538
  269.4 22.8 %collective-permute-start.5 = (bf16[160,384]{1,0:T(8,128)(2,1)S(1)}, bf16[160,384]{1,0:T(8,128)(2,1)S(1)}, u32[]{:S(2)}, u32[]{:S(2)}) collective-permute-start(bf16[160,384]{1,0:T(8,128)(2,1)S(1)} %fusion.15), channel_id=1, source_target_pairs={{0,16},{8,24},{16,0},{24,8},{1,17},{9,25},{17,1},{25,9},{2,18},{10... | collective-permute-start | bytes 368648 | tf_op jit(solution)/shard_map/ppermute | solution.py:538
  269.4 22.8 %collective-permute-start.4 = (bf16[160,384]{1,0:T(8,128)(2,1)S(1)}, bf16[160,384]{1,0:T(8,128)(2,1)S(1)}, u32[]{:S(2)}, u32[]{:S(2)}) collective-permute-start(bf16[160,384]{1,0:T(8,128)(2,1)S(1)} %fusion.15), channel_id=1, source_target_pairs={{0,8},{8,0},{16,24},{24,16},{1,9},{9,1},{17,25},{25,17},{2,10},{10... | collective-permute-start | bytes 368648 | tf_op jit(solution)/shard_map/ppermute | solution.py:538
  302.6 13.0 %collective-permute-start.10 = (bf16[640,384]{0,1:T(8,128)(2,1)}, bf16[640,384]{0,1:T(8,128)(2,1)}, u32[]{:S(2)}, u32[]{:S(2)}) collective-permute-start(bf16[640,384]{0,1:T(8,128)(2,1)} %pad_maximum_fusion.3), channel_id=1, source_target_pairs={{0,1},{1,0},{2,3},{3,2},{4,5},{5,4},{6,7},{7,6},{8,9},{9,8},{10,11... | collective-permute-start | bytes 1474568 | tf_op jit(solution)/shard_map/ppermute | solution.py:538
  302.7 24.0 %all-to-all-start.7 = ((bf16[32,4,8,384]{3,2,1,0:T(8,128)(2,1)}), bf16[32,4,8,384]{3,2,1,0:T(8,128)(2,1)}, u32[]{:S(2)}, u32[]{:S(2)}) async-start(bf16[32,4,8,384]{3,2,1,0:T(8,128)(2,1)} %get-tuple-element.83), calls=%async_computation.7 | async-start | bytes 1572864 | tf_op jit(solution)/shard_map/all_to_all | solution.py:625
  (22 other events, 175.8 us)

commit v5 on v4

--- a/solution.py
+++ b/solution.py
@@ -685,19 +685,17 @@
     head_sum = collect(head_sum, *cols)
     tail_sum = collect(tail_sum, *near)
     head_sum = collect(head_sum, *near)
-    head_sum = head_sum.astype(F32) * factor
-    tail_sum = tail_sum.astype(F32) * factor
     block_out = to_tile(out_parts)
     grad_input = to_tile(in_parts)
     return (
         block_out,
         grad_input,
-        head_sum[:head_rows].T,
-        tail_sum[2 * hidden_dim : tail_rows],
-        tail_sum[hidden_dim : 2 * hidden_dim].T,
-        tail_sum[:hidden_dim],
-        head_sum[head_rows],
-        tail_sum[tail_rows],
+        head_sum[:head_rows].T.astype(F32) * factor,
+        tail_sum[2 * hidden_dim : tail_rows].astype(F32) * factor,
+        tail_sum[hidden_dim : 2 * hidden_dim].T.astype(F32) * factor,
+        tail_sum[:hidden_dim].astype(F32) * factor,
+        head_sum[head_rows].astype(F32) * factor,
+        tail_sum[tail_rows].astype(F32) * factor,
     )
 
 

time: 333 us -> 322 us (0.967)
  local copies, waits for them, and re-layouts: 17.8 us -> 10.9 us
  waiting for transfers between devices: 99.7 us -> 94.1 us
    ppermute x25, waiting for transfers between devices: 59.3 us -> 50.3 us  [swap(): lax.ppermute(values, axis, [(i, i ^ offset) for i in range(lax.axis_size(...]
    slice x4 -> x0, local copies, waits for them, and re-layouts: 8.03 us -> none  [the longest x1 4.09 us: shards(): tail_sum[:hidden_dim]]
    squeeze x2 -> x1, other arithmetic: 3.93 us -> 0.41 us  [collect(): lax.dynamic_index_in_dim(got, slot ^ mine, 0, keepdims=False)]
  transfers between devices with their start and end apart: 33 -> 33, of which waited for: 16 -> 17; matrix products, arithmetic and copies ran while one was open for 9% -> 7% of each run, Pallas kernels for 31% -> 32%
where the time goes in v5:
time: 322 us; the launch traced here: 321 us
  Pallas kernels  135 us (42%)
  waiting for transfers between devices  94.1 us (29%)
  starting transfers between devices  65.4 us (20%)
  other arithmetic  15 us (5%)
  local copies, waits for them, and re-layouts  10.9 us (3%)
    ppermute x25, waiting for transfers between devices, swap(): lax.ppermute(values, axis, [(i, i ^ offset) for i in range(lax.axis_size(...  50.3 us
    pallas_call x2, Pallas kernels, mlp_call(): pl.pallas_call(mlp_kernel, grid=(groups,), in_specs=[per_group((width, to...  45.1 us
    all_to_all x4, waiting for transfers between devices, send(): lax.all_to_all(tie(sends, *after), both, split_axis=0, concat_axis=0, til...  33.1 us
    pallas_call x2, Pallas kernels, back_call(): pl.pallas_call(back_kernel, grid=(groups,), in_specs=[per_group((width, t...  31 us
    pallas_call x2, Pallas kernels, attend_call(): pl.pallas_call(attend_kernel, grid=(groups,), in_specs=[pieces_spec(act),...  28.9 us
    ppermute x25, starting transfers between devices, swap(): lax.ppermute(values, axis, [(i, i ^ offset) for i in range(lax.axis_size(...  28.1 us
    all_to_all x4, starting transfers between devices, send(): lax.all_to_all(tie(sends, *after), both, split_axis=0, concat_axis=0, til...  20.6 us
    all_to_all x4, starting transfers between devices, give_back(): return lax.all_to_all(pieces, both, split_axis=0, concat_axis=0, tiled=True)  16.7 us
  transfers between devices with their start and end apart: 33, of which 17 were waited for; matrix products, arithmetic and copies ran while one was open for 7% of the time, Pallas kernels for 32%

profile of v5, /device:TPU:0, one launch (start us, length us, event | category | flops | bytes accessed | tf_op | source)
XLA Modules:
  0.0 320.9 jit_solution(9468659502314876115)
XLA Ops:
  0.6 4.0 %shard_map.143 = bf16[32,4,8,384]{3,2,1,0:T(8,128)(2,1)} custom-call(bf16[4,4,4,32,384]{4,3,2,1,0:T(8,128)(2,1)} %bitcast.104), custom_call_target="tpu_custom_call" | custom-call | flops 1000000 | bytes 1572864 | tf_op jit(solution)/shard_map/pallas_call | solution.py:372
  4.6 7.3 %all-to-all-start = ((bf16[32,4,8,384]{3,2,1,0:T(8,128)(2,1)}), bf16[32,4,8,384]{3,2,1,0:T(8,128)(2,1)S(1)}, u32[]{:S(2)}, u32[]{:S(2)}) async-start(bf16[32,4,8,384]{3,2,1,0:T(8,128)(2,1)} %shard_map.143), calls=%async_computation | async-start | bytes 1572864 | tf_op jit(solution)/shard_map/all_to_all | solution.py:614
  12.0 4.0 %shard_map.147 = bf16[32,4,8,384]{3,2,1,0:T(8,128)(2,1)} custom-call(bf16[4,4,4,32,384]{4,3,2,1,0:T(8,128)(2,1)} %bitcast.105), custom_call_target="tpu_custom_call" | custom-call | flops 1000000 | bytes 1572864 | tf_op jit(solution)/shard_map/pallas_call | solution.py:372
  16.0 16.6 %all-to-all-done.act_ref = bf16[32,4,8,384]{3,2,1,0:T(8,128)(2,1)S(1)} async-done(((bf16[32,4,8,384]{3,2,1,0:T(8,128)(2,1)}), bf16[32,4,8,384]{3,2,1,0:T(8,128)(2,1)S(1)}, u32[]{:S(2)}, u32[]{:S(2)}) %all-to-all-start) | async-done | bytes 786464 | tf_op jit(solution)/shard_map/all_to_all | solution.py:614
  36.2 4.0 %shard_map.146 = bf16[32,4,8,384]{3,2,1,0:T(8,128)(2,1)} custom-call(bf16[4,4,4,32,384]{4,3,2,1,0:T(8,128)(2,1)} %bitcast.106), custom_call_target="tpu_custom_call" | custom-call | flops 1000000 | bytes 1572864 | tf_op jit(solution)/shard_map/pallas_call | solution.py:372
  40.2 16.6 %all-to-all-done.1.act_ref = bf16[32,4,8,384]{3,2,1,0:T(8,128)(2,1)S(1)} async-done(((bf16[32,4,8,384]{3,2,1,0:T(8,128)(2,1)}), bf16[32,4,8,384]{3,2,1,0:T(8,128)(2,1)S(1)}, u32[]{:S(2)}, u32[]{:S(2)}) %all-to-all-start.1) | async-done | bytes 786464 | tf_op jit(solution)/shard_map/all_to_all | solution.py:614
  61.6 4.0 %shard_map.149 = bf16[32,4,8,384]{3,2,1,0:T(8,128)(2,1)} custom-call(bf16[4,4,4,32,384]{4,3,2,1,0:T(8,128)(2,1)} %bitcast.107), custom_call_target="tpu_custom_call" | custom-call | flops 1000000 | bytes 1572864 | tf_op jit(solution)/shard_map/pallas_call | solution.py:372
  65.6 4.2 %shard_map.144 = (f32[384,256]{1,0:T(8,128)}, f32[384,256]{1,0:T(8,128)}, bf16[1152,384]{1,0:T(8,128)(2,1)}, bf16[384,384]{1,0:T(8,128)(2,1)}, bf16[1536,384]{1,0:T(8,128)(2,1)}, /*index=5*/bf16[384,1536]{1,0:T(8,128)(2,1)}) custom-call(f32[1,384]{1,0:T(1,128)} %reshape.80.gain_one_ref, f32[1,384]{1,0:T(1,128)} %reshape.81.gain_two_ref, ...), custom_call_target="tpu_custom_call" | custom-call | flops 1000000 | bytes 16000000 | tf_op jit(solution)/shard_map/pallas_call | solution.py:315
  69.8 14.5 %shard_map.145 = (bf16[4,384,256]{2,1,0:T(8,128)(2,1)}, bf16[4,1152,256]{2,1,0:T(8,128)(2,1)}, bf16[4,384,256]{2,1,0:T(8,128)(2,1)}, f32[4,16,256]{2,1,0:T(8,128)}, f32[4,384,256]{2,1,0:T(8,128)}) custom-call(bf16[32,4,8,384]{3,2,1,0:T(8,128)(2,1)} %copy-done.7, f32[384,256]{1,0:T(8,128)} %get-tuple-element.47.gain_ref, ...), custom_call_target="tpu_custom_call" | custom-call | flops 12000000000 | bytes 4718592 | tf_op jit(solution)/shard_map/pallas_call | solution.py:426
  84.3 6.0 %all-to-all-start.3 = ((bf16[32,4,8,384]{3,2,1,0:T(8,128)(2,1)}), bf16[32,4,8,384]{3,2,1,0:T(8,128)(2,1)S(1)}, u32[]{:S(2)}, u32[]{:S(2)}) async-start(bf16[32,4,8,384]{3,2,1,0:T(8,128)(2,1)} %shard_map.149), calls=%async_computation.3 | async-start | bytes 1572864 | tf_op jit(solution)/shard_map/all_to_all | solution.py:614
  90.3 14.5 %shard_map.150 = (bf16[4,384,256]{2,1,0:T(8,128)(2,1)}, bf16[4,1152,256]{2,1,0:T(8,128)(2,1)}, bf16[4,384,256]{2,1,0:T(8,128)(2,1)}, f32[4,16,256]{2,1,0:T(8,128)}, f32[4,384,256]{2,1,0:T(8,128)}) custom-call(bf16[32,4,8,384]{3,2,1,0:T(8,128)(2,1)} %copy-done.5, f32[384,256]{1,0:T(8,128)} %get-tuple-element.47.gain_ref, ...), custom_call_target="tpu_custom_call" | custom-call | flops 12000000000 | bytes 4718592 | tf_op jit(solution)/shard_map/pallas_call | solution.py:426
  104.8 22.1 %shard_map.148 = (bf16[32,4,8,384]{3,2,1,0:T(8,128)(2,1)}, f32[4,384,256]{2,1,0:T(8,128)}, bf16[4,384,256]{2,1,0:T(8,128)(2,1)}, f32[3456,384]{1,0:T(8,128)}, f32[384,128]{1,0:T(8,128)}) custom-call(f32[4,384,256]{2,1,0:T(8,128)} %get-tuple-element.50.attended_ref, bf16[4,384,256]{2,1,0:T(8,128)(2,1)} %get-tuple-element.51.mixed_ref, ...), custom_call_target="tpu_custom_call" | custom-call | flops 16000000000 | bytes 5505024 | tf_op jit(solution)/shard_map/pallas_call | solution.py:455
  127.8 23.0 %shard_map.151 = (bf16[32,4,8,384]{3,2,1,0:T(8,128)(2,1)}, f32[4,384,256]{2,1,0:T(8,128)}, bf16[4,384,256]{2,1,0:T(8,128)(2,1)}, bf16[3584,384]{1,0:T(8,128)(2,1)}, f32[384,128]{1,0:T(8,128)}) custom-call(f32[4,384,256]{2,1,0:T(8,128)} %get-tuple-element.60.attended_ref, bf16[4,384,256]{2,1,0:T(8,128)(2,1)} %get-tuple-element.61.mixed_ref, ...), custom_call_target="tpu_custom_call" | custom-call | flops 16000000000 | bytes 5505024 | tf_op jit(solution)/shard_map/pallas_call | solution.py:455
  152.4 5.9 %all-to-all-start.4 = ((bf16[32,4,8,384]{3,2,1,0:T(8,128)(2,1)}), bf16[32,4,8,384]{3,2,1,0:T(8,128)(2,1)S(1)}, u32[]{:S(2)}, u32[]{:S(2)}) async-start(bf16[32,4,8,384]{3,2,1,0:T(8,128)(2,1)} %get-tuple-element.59), calls=%async_computation.4 | async-start | bytes 1572864 | tf_op jit(solution)/shard_map/all_to_all | solution.py:625
  164.5 11.8 %collective-permute-done.12 = bf16[448,384]{1,0:T(8,128)(2,1)S(1)} collective-permute-done((bf16[448,384]{1,0:T(8,128)(2,1)}, bf16[448,384]{1,0:T(8,128)(2,1)S(1)}, u32[]{:S(2)}, u32[]{:S(2)}) %collective-permute-start.12) | collective-permute-done | bytes 344096 | tf_op jit(solution)/shard_map/ppermute | solution.py:538
  176.3 8.7 %collective-permute-done.14 = bf16[448,384]{1,0:T(8,128)(2,1)S(1)} collective-permute-done((bf16[448,384]{1,0:T(8,128)(2,1)}, bf16[448,384]{1,0:T(8,128)(2,1)S(1)}, u32[]{:S(2)}, u32[]{:S(2)}) %collective-permute-start.14) | collective-permute-done | bytes 344096 | tf_op jit(solution)/shard_map/ppermute | solution.py:538
  210.5 15.1 %shard_map.153 = (bf16[32,4,8,384]{3,2,1,0:T(8,128)(2,1)}, f32[1152,384]{1,0:T(8,128)}, f32[384,128]{1,0:T(8,128)}) custom-call(bf16[4,384,256]{2,1,0:T(8,128)(2,1)} %get-tuple-element.66.flat_ref, bf16[4,1152,256]{2,1,0:T(8,128)(2,1)} %get-tuple-element.67.triple_ref, f32[4,16,256]{2,1,0:T(8,128)} %get-tuple-element.68.stat_ref, ...), custom_call_target="tpu_custom_call" | custom-call | flops 24000000000 | bytes 7077888 | tf_op jit(solution)/shard_map/pallas_call | solution.py:493
  225.6 6.1 %collective-permute-done.23 = bf16[448,384]{1,0:T(8,128)(2,1)S(1)} collective-permute-done((bf16[448,384]{1,0:T(8,128)(2,1)S(1)}, bf16[448,384]{1,0:T(8,128)(2,1)S(1)}, u32[]{:S(2)}, u32[]{:S(2)}) %collective-permute-start.23) | collective-permute-done | bytes 344096 | tf_op jit(solution)/shard_map/ppermute | solution.py:538
  233.5 15.9 %shard_map.154 = (bf16[32,4,8,384]{3,2,1,0:T(8,128)(2,1)}, bf16[1280,384]{1,0:T(8,128)(2,1)}, f32[384,128]{1,0:T(8,128)}) custom-call(bf16[4,384,256]{2,1,0:T(8,128)(2,1)} %get-tuple-element.74.flat_ref, bf16[4,1152,256]{2,1,0:T(8,128)(2,1)} %get-tuple-element.75.triple_ref, f32[4,16,256]{2,1,0:T(8,128)} %get-tuple-element.76.stat_ref, ...), custom_call_target="tpu_custom_call" | custom-call | flops 24000000000 | bytes 7077888 | tf_op jit(solution)/shard_map/pallas_call | solution.py:493
  255.0 4.6 %shard_map.152 = bf16[4,4,4,32,384]{4,3,2,1,0:T(8,128)(2,1)} custom-call(bf16[32,4,8,384]{3,2,1,0:T(8,128)(2,1)} %copy-done.1, bf16[32,4,8,384]{3,2,1,0:T(8,128)(2,1)} %copy-done.3), custom_call_target="tpu_custom_call" | custom-call | flops 1000000 | bytes 3145728 | tf_op jit(solution)/shard_map/pallas_call | solution.py:390
  273.4 4.0 %collective-permute-start.6 = (bf16[160,384]{1,0:T(8,128)(2,1)S(1)}, bf16[160,384]{1,0:T(8,128)(2,1)S(1)}, u32[]{:S(2)}, u32[]{:S(2)}) collective-permute-start(bf16[160,384]{1,0:T(8,128)(2,1)S(1)} %fusion.12), channel_id=1, source_target_pairs={{0,24},{8,16},{16,8},{24,0},{1,25},{9,17},{17,9},{25,1},{2,26},{10... | collective-permute-start | bytes 368648 | tf_op jit(solution)/shard_map/ppermute | solution.py:538
  281.6 5.7 %collective-permute-done.5 = bf16[160,384]{1,0:T(8,128)(2,1)S(1)} collective-permute-done((bf16[160,384]{1,0:T(8,128)(2,1)S(1)}, bf16[160,384]{1,0:T(8,128)(2,1)S(1)}, u32[]{:S(2)}, u32[]{:S(2)}) %collective-permute-start.5) | collective-permute-done | bytes 122912 | tf_op jit(solution)/shard_map/ppermute | solution.py:538
  305.7 10.6 %all-to-all-done.7.refs_1_ = bf16[32,4,8,384]{3,2,1,0:T(8,128)(2,1)} async-done(((bf16[32,4,8,384]{3,2,1,0:T(8,128)(2,1)}), bf16[32,4,8,384]{3,2,1,0:T(8,128)(2,1)}, u32[]{:S(2)}, u32[]{:S(2)}) %all-to-all-start.7) | async-done | bytes 786464 | tf_op jit(solution)/shard_map/all_to_all | solution.py:625
  316.4 4.6 %shard_map.155 = bf16[4,4,4,32,384]{4,3,2,1,0:T(8,128)(2,1)} custom-call(bf16[32,4,8,384]{3,2,1,0:T(8,128)(2,1)} %copy-done.2, bf16[32,4,8,384]{3,2,1,0:T(8,128)(2,1)} %all-to-all-done.7.refs_1_), custom_call_target="tpu_custom_call" | custom-call | flops 1000000 | bytes 3145728 | tf_op jit(solution)/shard_map/pallas_call | solution.py:390
  (109 shorter events, 86.0 us)
Async XLA Ops:
  4.6 27.9 %all-to-all-start = ((bf16[32,4,8,384]{3,2,1,0:T(8,128)(2,1)}), bf16[32,4,8,384]{3,2,1,0:T(8,128)(2,1)S(1)}, u32[]{:S(2)}, u32[]{:S(2)}) async-start(bf16[32,4,8,384]{3,2,1,0:T(8,128)(2,1)} %shard_map.143), calls=%async_computation | async-start | bytes 1572864 | tf_op jit(solution)/shard_map/all_to_all | solution.py:614
  32.6 24.2 %all-to-all-start.1 = ((bf16[32,4,8,384]{3,2,1,0:T(8,128)(2,1)}), bf16[32,4,8,384]{3,2,1,0:T(8,128)(2,1)S(1)}, u32[]{:S(2)}, u32[]{:S(2)}) async-start(bf16[32,4,8,384]{3,2,1,0:T(8,128)(2,1)} %shard_map.147), calls=%async_computation.1 | async-start | bytes 1572864 | tf_op jit(solution)/shard_map/all_to_all | solution.py:614
  56.8 27.5 %all-to-all-start.2 = ((bf16[32,4,8,384]{3,2,1,0:T(8,128)(2,1)}), bf16[32,4,8,384]{3,2,1,0:T(8,128)(2,1)S(1)}, u32[]{:S(2)}, u32[]{:S(2)}) async-start(bf16[32,4,8,384]{3,2,1,0:T(8,128)(2,1)} %shard_map.146), calls=%async_computation.2 | async-start | bytes 1572864 | tf_op jit(solution)/shard_map/all_to_all | solution.py:614
  84.3 42.6 %all-to-all-start.3 = ((bf16[32,4,8,384]{3,2,1,0:T(8,128)(2,1)}), bf16[32,4,8,384]{3,2,1,0:T(8,128)(2,1)S(1)}, u32[]{:S(2)}, u32[]{:S(2)}) async-start(bf16[32,4,8,384]{3,2,1,0:T(8,128)(2,1)} %shard_map.149), calls=%async_computation.3 | async-start | bytes 1572864 | tf_op jit(solution)/shard_map/all_to_all | solution.py:614
  152.4 49.1 %all-to-all-start.4 = ((bf16[32,4,8,384]{3,2,1,0:T(8,128)(2,1)}), bf16[32,4,8,384]{3,2,1,0:T(8,128)(2,1)S(1)}, u32[]{:S(2)}, u32[]{:S(2)}) async-start(bf16[32,4,8,384]{3,2,1,0:T(8,128)(2,1)} %get-tuple-element.59), calls=%async_computation.4 | async-start | bytes 1572864 | tf_op jit(solution)/shard_map/all_to_all | solution.py:625
  161.0 15.3 %collective-permute-start.12 = (bf16[448,384]{1,0:T(8,128)(2,1)}, bf16[448,384]{1,0:T(8,128)(2,1)S(1)}, u32[]{:S(2)}, u32[]{:S(2)}) collective-permute-start(bf16[448,384]{1,0:T(8,128)(2,1)} %get-tuple-element.102), channel_id=1, source_target_pairs={{0,2},{1,3},{2,0},{3,1},{4,6},{5,7},{6,4},{7,5},{8,10},{9,11},{10,... | collective-permute-start | bytes 1032200 | tf_op jit(solution)/shard_map/ppermute | solution.py:538
  162.6 22.5 %collective-permute-start.14 = (bf16[448,384]{1,0:T(8,128)(2,1)}, bf16[448,384]{1,0:T(8,128)(2,1)S(1)}, u32[]{:S(2)}, u32[]{:S(2)}) collective-permute-start(bf16[448,384]{1,0:T(8,128)(2,1)} %get-tuple-element.103), channel_id=1, source_target_pairs={{0,6},{1,7},{2,4},{3,5},{4,2},{5,3},{6,0},{7,1},{8,14},{9,15},{10,... | collective-permute-start | bytes 1032200 | tf_op jit(solution)/shard_map/ppermute | solution.py:538
  164.0 21.6 %collective-permute-start.13 = (bf16[448,384]{1,0:T(8,128)(2,1)S(1)}, bf16[448,384]{1,0:T(8,128)(2,1)S(1)}, u32[]{:S(2)}, u32[]{:S(2)}) collective-permute-start(bf16[448,384]{1,0:T(8,128)(2,1)S(1)} %get-tuple-element.104), channel_id=1, source_target_pairs={{0,4},{1,5},{2,6},{3,7},{4,0},{5,1},{6,2},{7,3},{8,12},{9,13},{10,... | collective-permute-start | bytes 1032200 | tf_op jit(solution)/shard_map/ppermute | solution.py:538
  201.5 32.0 %all-to-all-start.5 = ((bf16[32,4,8,384]{3,2,1,0:T(8,128)(2,1)}), bf16[32,4,8,384]{3,2,1,0:T(8,128)(2,1)S(1)}, u32[]{:S(2)}, u32[]{:S(2)}) async-start(bf16[32,4,8,384]{3,2,1,0:T(8,128)(2,1)} %get-tuple-element.65), calls=%async_computation.5 | async-start | bytes 1572864 | tf_op jit(solution)/shard_map/all_to_all | solution.py:625
  206.9 18.7 %collective-permute-start.22 = (bf16[448,384]{1,0:T(8,128)(2,1)S(1)}, bf16[448,384]{1,0:T(8,128)(2,1)S(1)}, u32[]{:S(2)}, u32[]{:S(2)}) collective-permute-start(bf16[448,384]{1,0:T(8,128)(2,1)S(1)} %get-tuple-element.117), channel_id=1, source_target_pairs={{0,4},{1,5},{2,6},{3,7},{4,0},{5,1},{6,2},{7,3},{8,12},{9,13},{10,... | collective-permute-start | bytes 1032200 | tf_op jit(solution)/shard_map/ppermute | solution.py:538
  207.6 18.0 %collective-permute-start.21 = (bf16[448,384]{1,0:T(8,128)(2,1)S(1)}, bf16[448,384]{1,0:T(8,128)(2,1)S(1)}, u32[]{:S(2)}, u32[]{:S(2)}) collective-permute-start(bf16[448,384]{1,0:T(8,128)(2,1)S(1)} %get-tuple-element.117), channel_id=1, source_target_pairs={{0,2},{1,3},{2,0},{3,1},{4,6},{5,7},{6,4},{7,5},{8,10},{9,11},{10,... | collective-permute-start | bytes 1032200 | tf_op jit(solution)/shard_map/ppermute | solution.py:538
  208.5 23.3 %collective-permute-start.23 = (bf16[448,384]{1,0:T(8,128)(2,1)S(1)}, bf16[448,384]{1,0:T(8,128)(2,1)S(1)}, u32[]{:S(2)}, u32[]{:S(2)}) collective-permute-start(bf16[448,384]{1,0:T(8,128)(2,1)S(1)} %get-tuple-element.117), channel_id=1, source_target_pairs={{0,6},{1,7},{2,4},{3,5},{4,2},{5,3},{6,0},{7,1},{8,14},{9,15},{10,... | collective-permute-start | bytes 1032200 | tf_op jit(solution)/shard_map/ppermute | solution.py:538
  233.5 31.1 %collective-permute-start.24 = (bf16[1792,384]{1,0:T(8,128)(2,1)S(1)}, bf16[1792,384]{1,0:T(8,128)(2,1)}, u32[]{:S(2)}, u32[]{:S(2)}) collective-permute-start(bf16[1792,384]{1,0:T(8,128)(2,1)S(1)} %get-tuple-element.96), channel_id=1, source_target_pairs={{0,1},{1,0},{2,3},{3,2},{4,5},{5,4},{6,7},{7,6},{8,9},{9,8},{10,11... | collective-permute-start | bytes 4128776 | tf_op jit(solution)/shard_map/ppermute | solution.py:538
  250.5 9.2 %collective-permute-start = (bf16[640,384]{1,0:T(8,128)(2,1)S(1)}, bf16[640,384]{1,0:T(8,128)(2,1)}, u32[]{:S(2)}, u32[]{:S(2)}) collective-permute-start(bf16[640,384]{1,0:T(8,128)(2,1)S(1)} %dynamic-slice_bitcast_fusion.1), channel_id=1, source_target_pairs={{0,1},{1,0},{2,3},{3,2},{4,5},{5,4},{6,7},{7,6},{8,9},{9,8},{10,11... | collective-permute-start | bytes 1474568 | tf_op jit(solution)/shard_map/ppermute | solution.py:538
  251.0 41.3 %all-to-all-start.6 = ((bf16[32,4,8,384]{3,2,1,0:T(8,128)(2,1)}), bf16[32,4,8,384]{3,2,1,0:T(8,128)(2,1)S(1)}, u32[]{:S(2)}, u32[]{:S(2)}) async-start(bf16[32,4,8,384]{3,2,1,0:T(8,128)(2,1)} %get-tuple-element.73), calls=%async_computation.6 | async-start | bytes 1572864 | tf_op jit(solution)/shard_map/all_to_all | solution.py:625
  262.6 9.7 %collective-permute-start.3 = (bf16[160,384]{1,0:T(8,128)(2,1)S(1)}, bf16[160,384]{1,0:T(8,128)(2,1)S(1)}, u32[]{:S(2)}, u32[]{:S(2)}) collective-permute-start(bf16[160,384]{1,0:T(8,128)(2,1)S(1)} %get-tuple-element.114), channel_id=1, source_target_pairs={{0,6},{1,7},{2,4},{3,5},{4,2},{5,3},{6,0},{7,1},{8,14},{9,15},{10,... | collective-permute-start | bytes 368648 | tf_op jit(solution)/shard_map/ppermute | solution.py:538
  264.1 9.2 %collective-permute-start.2 = (bf16[160,384]{1,0:T(8,128)(2,1)S(1)}, bf16[160,384]{1,0:T(8,128)(2,1)S(1)}, u32[]{:S(2)}, u32[]{:S(2)}) collective-permute-start(bf16[160,384]{1,0:T(8,128)(2,1)S(1)} %get-tuple-element.115), channel_id=1, source_target_pairs={{0,4},{1,5},{2,6},{3,7},{4,0},{5,1},{6,2},{7,3},{8,12},{9,13},{10,... | collective-permute-start | bytes 368648 | tf_op jit(solution)/shard_map/ppermute | solution.py:538
  273.4 8.2 %collective-permute-start.6 = (bf16[160,384]{1,0:T(8,128)(2,1)S(1)}, bf16[160,384]{1,0:T(8,128)(2,1)S(1)}, u32[]{:S(2)}, u32[]{:S(2)}) collective-permute-start(bf16[160,384]{1,0:T(8,128)(2,1)S(1)} %fusion.12), channel_id=1, source_target_pairs={{0,24},{8,16},{16,8},{24,0},{1,25},{9,17},{17,9},{25,1},{2,26},{10... | collective-permute-start | bytes 368648 | tf_op jit(solution)/shard_map/ppermute | solution.py:538
  277.4 9.9 %collective-permute-start.5 = (bf16[160,384]{1,0:T(8,128)(2,1)S(1)}, bf16[160,384]{1,0:T(8,128)(2,1)S(1)}, u32[]{:S(2)}, u32[]{:S(2)}) collective-permute-start(bf16[160,384]{1,0:T(8,128)(2,1)S(1)} %fusion.12), channel_id=1, source_target_pairs={{0,16},{8,24},{16,0},{24,8},{1,17},{9,25},{17,1},{25,9},{2,18},{10... | collective-permute-start | bytes 368648 | tf_op jit(solution)/shard_map/ppermute | solution.py:538
  277.4 9.9 %collective-permute-start.4 = (bf16[160,384]{1,0:T(8,128)(2,1)S(1)}, bf16[160,384]{1,0:T(8,128)(2,1)S(1)}, u32[]{:S(2)}, u32[]{:S(2)}) collective-permute-start(bf16[160,384]{1,0:T(8,128)(2,1)S(1)} %fusion.12), channel_id=1, source_target_pairs={{0,8},{8,0},{16,24},{24,16},{1,9},{9,1},{17,25},{25,17},{2,10},{10... | collective-permute-start | bytes 368648 | tf_op jit(solution)/shard_map/ppermute | solution.py:538
  288.0 11.5 %collective-permute-start.9 = (bf16[160,384]{1,0:T(8,128)(2,1)}, bf16[160,384]{1,0:T(8,128)(2,1)}, u32[]{:S(2)}, u32[]{:S(2)}) collective-permute-start(bf16[160,384]{1,0:T(8,128)(2,1)} %add_convert_fusion), channel_id=1, source_target_pairs={{0,6},{1,7},{2,4},{3,5},{4,2},{5,3},{6,0},{7,1},{8,14},{9,15},{10,... | collective-permute-start | bytes 368648 | tf_op jit(solution)/shard_map/ppermute | solution.py:538
  289.0 10.4 %collective-permute-start.8 = (bf16[160,384]{1,0:T(8,128)(2,1)}, bf16[160,384]{1,0:T(8,128)(2,1)}, u32[]{:S(2)}, u32[]{:S(2)}) collective-permute-start(bf16[160,384]{1,0:T(8,128)(2,1)} %add_convert_fusion), channel_id=1, source_target_pairs={{0,4},{1,5},{2,6},{3,7},{4,0},{5,1},{6,2},{7,3},{8,12},{9,13},{10,... | collective-permute-start | bytes 368648 | tf_op jit(solution)/shard_map/ppermute | solution.py:538
  290.1 9.3 %collective-permute-start.7 = (bf16[160,384]{1,0:T(8,128)(2,1)}, bf16[160,384]{1,0:T(8,128)(2,1)}, u32[]{:S(2)}, u32[]{:S(2)}) collective-permute-start(bf16[160,384]{1,0:T(8,128)(2,1)} %add_convert_fusion), channel_id=1, source_target_pairs={{0,2},{1,3},{2,0},{3,1},{4,6},{5,7},{6,4},{7,5},{8,10},{9,11},{10,... | collective-permute-start | bytes 368648 | tf_op jit(solution)/shard_map/ppermute | solution.py:538
  292.3 24.0 %all-to-all-start.7 = ((bf16[32,4,8,384]{3,2,1,0:T(8,128)(2,1)}), bf16[32,4,8,384]{3,2,1,0:T(8,128)(2,1)}, u32[]{:S(2)}, u32[]{:S(2)}) async-start(bf16[32,4,8,384]{3,2,1,0:T(8,128)(2,1)} %get-tuple-element.83), calls=%async_computation.7 | async-start | bytes 1572864 | tf_op jit(solution)/shard_map/all_to_all | solution.py:625
  (20 other events, 180.8 us)
